TPU v7x, 32 devices: a whole 2x2x4 slice. The times are simulated.
32 devices in a mesh: sens: 4 (over y, x), slab: 8 (over z, core).
Axes of the slice: x: 2, y: 2, z: 4, core: 2. Of those that a mesh axis runs over, the one named last changes fastest.
Arguments:
- pressure: bfloat16 [32768, 128], P('slab'), may hold values from 0 to 1
- kernels: bfloat16 [4, 64, 256], replicated, may hold values from -0.0625 to 0.0625
- filter_gains: float32 [512], replicated, may hold values from 0.25 to 2
- measured: float32 [1024, 2, 512], P('sens'), may hold values from -6 to 6
- blocks: int32 [1024, 8, 64], P('sens', 'slab'), may hold values from 0 to 4095
- frames: int32 [1024, 8, 64], P('sens', 'slab'), may hold values from 0 to 2
- classes: int32 [1024, 8, 64], P('sens', 'slab'), may hold values from 0 to 3
- counts: int32 [1024, 8], P('sens', 'slab'), may hold values from 1 to 64, as said below
Outputs:
- residual: float32 [1024, 2, 512], P(('sens', 'slab'))
- gradient: float32 [32768, 128], P('slab', 'sens')
Inputs may be any that keep to these rules, and one draw needn't show every extreme that they name: counts[s, j] slots of sensor s in slab j are live; some sensor has all 64 slots live in some slab. `blocks`: slots at or past counts[s, j] are ignored.
All inputs are finite; a program needn't handle non-finite values.
Results may differ from a plain program's by a relative error of at most 0.00077.
Values may be sent and summed in bfloat16 or wider, within the bound.
No kernel may reach another device: no remote copies, remote signals or barrier semaphores. Data moves between devices by JAX's collectives and lax.ppermute only.
A program may use at most 256 MiB of HBM per device.

v0:
```python
import math

import jax
import jax.numpy as jnp
from jax import lax
from jax.sharding import PartitionSpec as P


def dft_pair(time_len):
    sample_ids = jnp.arange(time_len, dtype=jnp.int32)
    phase_ids = sample_ids[:, None] * sample_ids[None, :] % time_len
    angles = phase_ids.astype(jnp.float32) * (2.0 * math.pi / time_len)
    return (jnp.cos(angles), jnp.sin(angles))


def time_filter(traces, filter_gains, forward_basis, inverse_basis):
    time_len = filter_gains.shape[0]
    rows_flat = traces.reshape(-1, time_len)
    spectrum = jnp.dot(
        rows_flat,
        forward_basis,
        precision=lax.Precision.HIGHEST,
        preferred_element_type=jnp.float32,
    )
    spectrum = spectrum * jnp.concatenate([filter_gains, filter_gains])
    result = jnp.dot(
        spectrum, inverse_basis, precision=lax.Precision.HIGHEST, preferred_element_type=jnp.float32
    )
    return (result / time_len).reshape(traces.shape)


def per_device(pressure, kernels, filter_gains, measured, blocks, frames, classes, counts):
    kind_count, voxel_count, tap_count = kernels.shape
    block_count = pressure.shape[0]
    wave_count = pressure.shape[1] // voxel_count
    frame_len = tap_count // 2
    time_len = filter_gains.shape[0]
    frame_count = time_len // frame_len
    place_count = frame_count - 1
    combo_count = kind_count * place_count
    sensor_count, slot_count = (blocks.shape[0], blocks.shape[2])
    share_rows = sensor_count // lax.axis_size("slab")
    cosine_table, sine_table = dft_pair(time_len)
    forward_basis = jnp.concatenate([cosine_table, sine_table], axis=1)
    inverse_basis = jnp.concatenate([cosine_table, sine_table], axis=0)
    placed_list = []
    for offset in range(place_count):
        placed_list.append(
            jnp.pad(
                kernels,
                ((0, 0), (0, 0), (offset * frame_len, time_len - tap_count - offset * frame_len)),
            )
        )
    placed_kern = jnp.stack(placed_list, axis=1).reshape(combo_count, voxel_count, time_len)
    placed_wide = placed_kern.astype(jnp.float32)
    block_ids = blocks[:, 0, :]
    combo_ids = classes[:, 0, :] * place_count + frames[:, 0, :]
    live_slot = jnp.arange(slot_count, dtype=jnp.int32)[None, :] < counts[:, 0][:, None]
    combo_hot = (
        (combo_ids[:, :, None] == jnp.arange(combo_count, dtype=jnp.int32)) & live_slot[:, :, None]
    ).astype(jnp.bfloat16)
    block_range = jnp.arange(block_count, dtype=jnp.int32)
    picked_ids = block_ids.reshape(-1)
    row_hot = combo_hot
    picked = pressure[picked_ids].reshape(
        share_rows * lax.axis_size("slab"), slot_count, wave_count * voxel_count
    )
    grouped = jnp.einsum("skc,skx->scx", row_hot, picked, preferred_element_type=jnp.float32)
    grouped = grouped.reshape(
        share_rows * lax.axis_size("slab"), combo_count, wave_count, voxel_count
    )
    traces = lax.psum_scatter(
        jnp.einsum(
            "scwv,cvt->swt",
            grouped,
            placed_wide,
            precision=lax.Precision.HIGHEST,
            preferred_element_type=jnp.float32,
        ),
        "slab",
        scatter_dimension=0,
        tiled=True,
    )
    measured_share = lax.dynamic_slice_in_dim(
        measured, lax.axis_index("slab") * share_rows, share_rows, 0
    )
    residual = time_filter(traces, filter_gains, forward_basis, inverse_basis) - measured_share
    back_share = time_filter(residual, filter_gains, forward_basis, inverse_basis).astype(
        jnp.bfloat16
    )
    piece_rows = lax.all_gather(back_share, "slab", axis=0, tiled=True)
    row_count = piece_rows.shape[0]
    row_hot = combo_hot
    responses = jnp.einsum(
        "swt,cvt->scwv", piece_rows, placed_kern, preferred_element_type=jnp.float32
    )
    responses = responses.reshape(row_count * combo_count, wave_count * voxel_count)
    block_hot = (block_ids[:, :, None] == block_range).astype(jnp.bfloat16)
    tallies = jnp.einsum("skb,skc->bsc", block_hot, row_hot, preferred_element_type=jnp.float32)
    tallies = tallies.reshape(block_count, row_count * combo_count)
    partial_grad = jnp.dot(
        tallies, responses, precision=lax.Precision.HIGHEST, preferred_element_type=jnp.float32
    )
    gradient = lax.psum_scatter(partial_grad, "sens", scatter_dimension=1, tiled=True)
    return (residual, gradient)


def solution(mesh):
    return jax.shard_map(
        per_device,
        mesh=mesh,
        in_specs=(
            P("slab", None),
            P(),
            P(),
            P("sens", None, None),
            P("sens", "slab", None),
            P("sens", "slab", None),
            P("sens", "slab", None),
            P("sens", "slab"),
        ),
        out_specs=(P(("sens", "slab"), None, None), P("slab", "sens")),
        check_vma=False,
    )
```

profile of v0, /device:TPU:0, one launch (start us, length us, event | category | flops | bytes accessed | tf_op | source)
XLA Modules:
  0.0 294.2 jit_solution(7339451144219462057)
XLA Ops:
  7.2 0.0 copy-start
  7.2 0.0 reduce-scatter.3.cloned.1.call-start
  7.2 0.9 iota_compare_fusion.5
  8.1 0.9 add_bitcast_fusion
  9.0 0.1 copy.15
  9.1 0.9 copy.16
  10.0 0.1 reshape_squeeze.3
  10.2 0.1 compare_select_fusion
  10.2 1.1 pad_bitcast_fusion.2
  11.4 0.1 pad_maximum_fusion.16
  11.5 0.9 copy.18
  12.4 0.0 copy-done
  12.4 57.4 %gather_fusion = bf16[16384,128]{1,0:T(8,128)(2,1)} fusion(bf16[4096,128]{1,0:T(8,128)(2,1)S(1)} %copy-done, s32[16384]{0:T(1024)S(1)} %broadcast_clamp_fusion), kind=kCustom, calls=%fused_computation | custom fusion | bytes 8454144 | tf_op jit(solution)/shard_map/gather | solution.py:65
  69.8 3.4 %fusion.5 = f32[256,12,128]{2,1,0:T(8,128)S(1)} fusion(bf16[256,64,128]{2,1,0:T(8,128)(2,1)} %bitcast.41, s32[256,64]{1,0:T(8,128)S(1)} %copy.15, pred[256,64]{1,0:T(8,128)(4,1)S(1)} %iota_compare_fusion.5), kind=kOutput, calls=%fused_computation.9 | convolution fusion | flops 50724864 | bytes 5849088 | tf_op jit(solution)/shard_map/skc,skx->scx/dot_general | solution.py:68
  73.2 0.0 copy-start.2
  73.2 1.6 copy.17
  74.8 0.0 copy-done.2
  74.8 0.0 copy-start.5
  74.8 3.9 %convolution_bitcast_fusion.1 = f32[256,2,512]{2,0,1:T(8,128)} fusion(f32[256,12,2,64]{0,3,2,1:T(8,128)} %bitcast.44, bf16[12,64,512,1]{2,1,3,0:T(8,128)(2,1)S(1)} %bitcast.42), kind=kOutput, calls=%fused_computation.18 | convolution fusion | flops 2415919104 | bytes 3407872 | tf_op jit(solution)/shard_map/scwv,cvt->swt/dot_general | solution.py:73
  78.7 0.0 reduce-scatter.3.cloned.1.call-update
  78.7 0.0 reduce-scatter.5.cloned.1.call-start
  78.8 0.0 copy-done.5
  78.8 0.1 copy.21
  78.9 46.5 %fusion.2 = f32[4096,256,12]{0,2,1:T(8,128)} fusion(s32[256,64]{1,0:T(8,128)S(1)} %copy.21, s32[256,64]{1,0:T(8,128)S(1)} %copy.15, pred[256,64]{1,0:T(8,128)(4,1)S(1)} %iota_compare_fusion.5), kind=kOutput, calls=%fused_computation.4 | convolution fusion | flops 1678114816 | bytes 50479104 | tf_op jit(solution)/shard_map/skb,skc->bsc/dot_general | solution.py:99
  125.4 0.0 copy-start.6
  125.4 54.3 %reshape.100 = f32[4096,3072]{0,1:T(8,128)} reshape(f32[4096,256,12]{0,2,1:T(8,128)} %fusion.2) | data formatting | bytes 100663296 | tf_op jit(solution)/shard_map/reshape | solution.py:100
  179.6 0.0 copy-done.6
  179.6 4.1 %fusion.27 = (f32[512,512]{1,0:T(8,128)S(1)}, f32[512,512]{1,0:T(8,128)S(1)}) fusion(), kind=kLoop, calls=%fused_computation.36 | loop fusion | flops 3670016 | bytes 2097152 | tf_op jit(solution)/shard_map/sin | solution.py:13
  183.7 0.0 reduce-scatter.3.cloned.1.call-done
  183.8 1.0 copy.20
  184.8 0.1 reshape.98
  184.9 1.4 fusion.11
  186.2 1.4 fusion.13
  187.6 0.1 reshape.99
  187.7 1.0 dynamic-slice_subtract_fusion
  188.7 0.0 copy-start.4
  188.7 0.1 reshape.101
  188.8 1.4 fusion.12
  190.2 0.0 copy-start.3
  190.2 1.4 fusion.15
  191.6 0.0 copy-done.4
  191.6 16.6 %all_gather.3 = bf16[256,2,512]{2,0,1:T(8,128)(2,1)S(1)} all-gather(bf16[32,2,512]{2,0,1:T(8,128)(2,1)S(1)} %copy.22), channel_id=1, replica_groups=mesh['sens'=4,'slab'=8] {'slab'}, dimensions={0}, use_global_device_ids=true | all-gather | bytes 589824 | tf_op jit(solution)/shard_map/all_gather | solution.py:91
  208.2 0.0 copy-done.3
  208.2 0.6 convolution_bitcast_fusion
  208.8 3.7 %copy.23 = f32[256,12,2,64]{3,2,1,0:T(2,128)} copy(f32[256,12,2,64]{0,3,2,1:T(8,128)S(1)} %convolution_bitcast_fusion) | data formatting | bytes 3145728 | tf_op jit(solution)/shard_map/swt,cvt->scwv/transpose | solution.py:94
  212.6 3.4 %reshape.102 = f32[3072,128]{1,0:T(8,128)S(1)} reshape(f32[256,12,2,64]{3,2,1,0:T(2,128)} %copy.23) | data formatting | bytes 3145728 | tf_op jit(solution)/shard_map/reshape | solution.py:97
  215.9 0.0 copy-start.1
  215.9 34.9 %fusion.33 = f32[4096,128]{0,1:T(8,128)} fusion(f32[4096,3072]{0,1:T(8,128)} %reshape.100, f32[3072,128]{1,0:T(8,128)S(1)} %reshape.102), kind=kOutput, calls=%fused_computation.51 | convolution fusion | flops 19327352832 | bytes 54001664 | tf_op jit(solution)/shard_map/dot_general | solution.py:101
  250.9 0.0 reduce-scatter.5.cloned.1.call-update
  250.9 36.4 %reduce-scatter.5.cloned.1.call-done = f32[4096,32]{0,1:T(8,128)} async-done(((f32[4096,128]{0,1:T(8,128)}), f32[4096,32]{0,1:T(8,128)}) %reduce-scatter.5.cloned.1.call-update) | async-done | bytes 524304 | tf_op jit(solution)/shard_map/reduce_scatter | solution.py:104
  287.3 0.0 copy-done.1
  (4 shorter events, 0.1 us)
Async XLA Ops:
  7.2 5.2 %copy-start = (bf16[4096,128]{1,0:T(8,128)(2,1)S(1)}, bf16[4096,128]{1,0:T(8,128)(2,1)}, u32[]{:S(2)}) copy-start(bf16[4096,128]{1,0:T(8,128)(2,1)} %param.8) | copy-start | bytes 3145732
  7.2 176.6 %reduce-scatter.3.cloned.1.call-start = ((), (), s32[]{:S(2)}) async-start(), calls=%async_computation.2 | async-start | bytes 1179648 | tf_op jit(solution)/shard_map/reduce_scatter | solution.py:72
  73.2 1.6 copy-start.2
  74.8 3.9 %copy-start.5 = (s32[256,1,64]{0,2,1:T(8,128)S(1)}, s32[256,1,64]{0,2,1:T(8,128)}, u32[]{:S(2)}) copy-start(s32[256,1,64]{0,2,1:T(8,128)} %param.12) | copy-start | bytes 196612
  78.7 208.6 %reduce-scatter.5.cloned.1.call-start = ((), (), s32[]{:S(2)}) async-start(), calls=%async_computation.3 | async-start | bytes 2621440 | tf_op jit(solution)/shard_map/reduce_scatter | solution.py:104
  125.4 54.3 %copy-start.6 = (f32[512]{0:T(512)S(1)}, f32[512]{0:T(512)}, u32[]{:S(2)}) copy-start(f32[512]{0:T(512)} %param.10) | copy-start | bytes 6148
  188.7 2.9 copy-start.4
  190.2 18.0 %copy-start.3 = (bf16[4,3,64,512]{3,2,1,0:T(8,128)(2,1)S(1)}, bf16[4,3,64,512]{3,2,1,0:T(8,128)(2,1)}, u32[]{:S(2)}) copy-start(bf16[4,3,64,512]{3,2,1,0:T(8,128)(2,1)} %copy.18) | copy-start | bytes 2359300
  215.9 71.4 %copy-start.1 = (bf16[4096,128]{1,0:T(8,128)(2,1)S(1)}, bf16[4096,128]{1,0:T(8,128)(2,1)}, u32[]{:S(2)}) copy-start(bf16[4096,128]{1,0:T(8,128)(2,1)} %param.8) | copy-start | bytes 3145732
Sparse Core Ops, SparseCore 0:
  78.8 34.8 reduce-scatter.2
  251.0 36.2 reduce-scatter.4
where the time goes:
time: 295 us; the launch traced here: 294 us
  local copies, waits for them, and re-layouts  125 us (42%)
  matrix products  94.8 us (32%)
  waiting for transfers between devices  36.5 us (12%)
  blocking collectives  16.6 us (6%)
  between operations  14.2 us (5%)
  other arithmetic  6.99 us (2%)
    gather x1, local copies, waits for them, and re-layouts, per_device(): pressure[picked_ids]  57.4 us
    reshape x1, local copies, waits for them, and re-layouts, per_device(): tallies = tallies.reshape(block_count, row_count * combo_count)  54.3 us
    dot_general x1, matrix products, per_device(): jnp.einsum('skb,skc->bsc', block_hot, row_hot, preferred_element_type=jnp...  46.5 us
    reduce_scatter x1, waiting for transfers between devices, per_device(): lax.psum_scatter(partial_grad, 'sens', scatter_dimension=1, tiled=True)  36.4 us
    dot_general x1, matrix products, per_device(): jnp.dot(tallies, responses, precision=lax.Precision.HIGHEST, preferred_el...  34.9 us
    all_gather x1, blocking collectives, per_device(): piece_rows = lax.all_gather(back_share, 'slab', axis=0, tiled=True)  16.6 us
  transfers between devices with their start and end apart: 2, of which 1 were waited for; matrix products, arithmetic and copies ran while one was open for 36% of the time, Pallas kernels for 0%

commit v1 on v0

v1 whole, which is shorter than its diff:
```python
import functools
import math

import jax
import jax.numpy as jnp
from jax import lax
from jax.experimental import pallas as pl
from jax.experimental.pallas import tpu as pltpu
from jax.sharding import PartitionSpec as P

LANES = 256
UNIT = 4


def filter_matrix(filter_gains):
    time_len = filter_gains.shape[0]
    sample_ids = jnp.arange(time_len, dtype=jnp.int32)
    phase_ids = sample_ids[:, None] * sample_ids[None, :] % time_len
    angles = phase_ids.astype(jnp.float32) * (2.0 * math.pi / time_len)
    basis = jnp.concatenate([jnp.cos(angles), jnp.sin(angles)], axis=1)
    gains = jnp.concatenate([filter_gains, filter_gains])
    product = lax.dot_general(
        basis * gains,
        basis,
        (((1,), (1,)), ((), ())),
        precision=lax.Precision.HIGHEST,
        preferred_element_type=jnp.float32,
    )
    return product / time_len


def split_parts(array, count):
    parts = []
    for _ in range(count):
        part = array.astype(jnp.bfloat16)
        parts.append(part)
        array = array - part.astype(jnp.float32)
    return parts


def forward_kernel(
    kinds, places, code_ref, pressure_ref, kernel_ref, tally_ref, traces_ref, grouped_ref
):
    combos = kinds * places
    rows = UNIT * combos
    blocks = pressure_ref.shape[0]
    tops = blocks // LANES
    units = code_ref.shape[0]
    sensors = units * UNIT
    slots = code_ref.shape[1]
    voxels = pressure_ref.shape[1] // 2
    frame = kernel_ref.shape[1] // 2

    def unit_step(unit, _):
        code = code_ref[pl.ds(unit, 1), :]
        row_code = lax.shift_right_arithmetic(code, 8)
        low_code = code & (LANES - 1)
        row_hot = (lax.broadcasted_iota(jnp.int32, (tops * rows, slots), 0) == row_code).astype(
            jnp.bfloat16
        )
        low_hot = (lax.broadcasted_iota(jnp.int32, (LANES, slots), 0) == low_code).astype(
            jnp.bfloat16
        )
        tally = lax.dot_general(
            row_hot, low_hot, (((1,), (1,)), ((), ())), preferred_element_type=jnp.float32
        ).astype(jnp.bfloat16)
        base = pl.multiple_of(unit * rows, rows)
        for top in range(tops):
            tally_ref[pl.ds(base, rows), top * LANES : (top + 1) * LANES] = tally[
                top * rows : (top + 1) * rows
            ]
        return 0

    lax.fori_loop(0, units, unit_step, 0)
    grouped_ref[...] = jnp.dot(
        tally_ref[...], pressure_ref[...], preferred_element_type=jnp.float32
    )
    sums = [None] * (places + 1)
    for place in range(places):
        picked = [
            grouped_ref[pl.ds(place * kinds + kind, sensors, stride=combos), :]
            for kind in range(kinds)
        ]
        wide = jnp.concatenate(
            [
                jnp.concatenate([g[:, w * voxels : (w + 1) * voxels] for g in picked], axis=1)
                for w in range(2)
            ],
            axis=0,
        )
        taps = jnp.dot(
            jnp.concatenate(split_parts(wide, 3), axis=0),
            kernel_ref[...],
            preferred_element_type=jnp.float32,
        )
        count = 2 * sensors
        taps = taps[:count] + (taps[count : 2 * count] + taps[2 * count :])
        for half in range(2):
            piece = taps[:, half * frame : (half + 1) * frame]
            spot = place + half
            sums[spot] = piece if sums[spot] is None else sums[spot] + piece
    total = jnp.concatenate(sums, axis=1)
    time_len = total.shape[1]
    for w in range(2):
        traces_ref[:, w * time_len : (w + 1) * time_len] = total[w * sensors : (w + 1) * sensors]


def forward(code, pressure, kern_rows, kinds, places, time_len, steps):
    units = code.shape[0]
    sensors = units * UNIT
    combos = kinds * places
    per_step = units // steps
    block_count = pressure.shape[0]
    return pl.pallas_call(
        functools.partial(forward_kernel, kinds, places),
        grid=(steps,),
        in_specs=[
            pl.BlockSpec((per_step, code.shape[1]), lambda i: (i, 0)),
            pl.BlockSpec(pressure.shape, lambda i: (0, 0)),
            pl.BlockSpec(kern_rows.shape, lambda i: (0, 0)),
        ],
        out_specs=[
            pl.BlockSpec((per_step * UNIT * combos, block_count), lambda i: (i, 0)),
            pl.BlockSpec((per_step * UNIT, 2 * time_len), lambda i: (i, 0)),
        ],
        out_shape=[
            jax.ShapeDtypeStruct((sensors * combos, block_count), jnp.bfloat16),
            jax.ShapeDtypeStruct((sensors, 2 * time_len), jnp.float32),
        ],
        scratch_shapes=[pltpu.VMEM((per_step * UNIT * combos, pressure.shape[1]), jnp.float32)],
        compiler_params=pltpu.CompilerParams(
            dimension_semantics=("arbitrary",), vmem_limit_bytes=56 << 20
        ),
        name="forward",
    )(code, pressure, kern_rows)


def backward_kernel(kinds, places, back_ref, kernel_ref, tally_ref, grad_ref, wide_ref, resp_ref):
    combos = kinds * places
    sensors = back_ref.shape[0]
    time_len = back_ref.shape[1] // 2
    taps = kernel_ref.shape[1]
    frame = taps // 2
    width = wide_ref.shape[1]
    voxels = width // 2

    @pl.when(pl.program_id(0) == 0)
    def _():
        for place in range(places):
            waves = []
            for w in range(2):
                start = w * time_len + place * frame
                waves.append(
                    lax.dot_general(
                        back_ref[:, start : start + taps],
                        kernel_ref[...],
                        (((1,), (1,)), ((), ())),
                        preferred_element_type=jnp.float32,
                    )
                )
            for kind in range(kinds):
                cut = slice(kind * voxels, (kind + 1) * voxels)
                wide_ref[pl.ds(place * kinds + kind, sensors, stride=combos), :] = jnp.concatenate(
                    [waves[0][:, cut], waves[1][:, cut]], axis=1
                )
        flipped = wide_ref[...].T
        high, low = split_parts(flipped, 2)
        resp_ref[:width] = high
        resp_ref[width:] = low

    both = jnp.dot(resp_ref[...], tally_ref[...], preferred_element_type=jnp.float32)
    grad_ref[...] = both[:width] + both[width:]


def backward(back, kern_rows, tally, kinds, places, width, steps):
    rows, block_count = tally.shape
    cut = block_count // steps
    return pl.pallas_call(
        functools.partial(backward_kernel, kinds, places),
        grid=(steps,),
        in_specs=[
            pl.BlockSpec(back.shape, lambda i: (0, 0)),
            pl.BlockSpec(kern_rows.shape, lambda i: (0, 0)),
            pl.BlockSpec((rows, cut), lambda i: (0, i)),
        ],
        out_specs=pl.BlockSpec((width, cut), lambda i: (0, i)),
        out_shape=jax.ShapeDtypeStruct((width, block_count), jnp.float32),
        scratch_shapes=[
            pltpu.VMEM((rows, width), jnp.float32),
            pltpu.VMEM((2 * width, rows), jnp.bfloat16),
        ],
        compiler_params=pltpu.CompilerParams(
            dimension_semantics=("arbitrary",), vmem_limit_bytes=56 << 20
        ),
        name="backward",
    )(back, kern_rows, tally)


def scatter_slab(partial):
    slabs = lax.axis_size("slab")
    chips = slabs // 2
    place = lax.axis_index("slab")
    core = place % 2
    chip = place // 2
    rows = partial.reshape(chips, 2, partial.shape[0] // slabs, partial.shape[1])
    mine = lax.dynamic_index_in_dim(rows, core, 1, keepdims=False)
    other = lax.dynamic_index_in_dim(rows, 1 - core, 1, keepdims=False)
    paired = mine + lax.ppermute(other, "slab", [(j, j ^ 1) for j in range(slabs)])
    total = lax.dynamic_index_in_dim(paired, chip, 0, keepdims=False)
    for step in range(1, chips):
        block = lax.dynamic_index_in_dim(paired, (chip + step) % chips, 0, keepdims=False)
        total = total + lax.ppermute(
            block, "slab", [(j, (j + 2 * step) % slabs) for j in range(slabs)]
        )
    return total


def gather_slab(share):
    return lax.all_gather(share, "slab", axis=0, tiled=True)


def scatter_sens(partial):
    groups = lax.axis_size("sens")
    own = lax.axis_index("sens")
    blocks = partial.reshape(groups, partial.shape[0] // groups, partial.shape[1])
    total = lax.dynamic_index_in_dim(blocks, own, 0, keepdims=False)
    for step in range(1, groups):
        block = lax.dynamic_index_in_dim(blocks, own ^ step, 0, keepdims=False)
        total = total + lax.ppermute(block, "sens", [(q, q ^ step) for q in range(groups)])
    return total


def per_device(pressure, kernels, filter_gains, measured, blocks, frames, classes, counts):
    kinds, voxels, taps = kernels.shape
    block_count, width = pressure.shape
    frame = taps // 2
    time_len = filter_gains.shape[0]
    places = time_len // frame - 1
    combos = kinds * places
    sensors, slots = blocks.shape[0], blocks.shape[2]
    share = sensors // lax.axis_size("slab")

    block_ids = blocks[:, 0, :]
    combo_ids = frames[:, 0, :] * kinds + classes[:, 0, :]
    live = jnp.arange(slots, dtype=jnp.int32)[None, :] < counts
    lane = jnp.arange(sensors, dtype=jnp.int32)[:, None] % UNIT
    row_code = (block_ids // LANES) * (UNIT * combos) + lane * combos + combo_ids
    code = jnp.where(live, row_code * LANES + block_ids % LANES, -LANES)
    code = code.reshape(sensors // UNIT, UNIT * slots)
    kern_rows = kernels.reshape(kinds * voxels, taps)

    tally, partial = forward(code, pressure, kern_rows, kinds, places, time_len, 4)
    traces = scatter_slab(partial).reshape(share * 2, time_len)
    matrix = filter_matrix(filter_gains)
    measured_share = lax.dynamic_slice_in_dim(measured, lax.axis_index("slab") * share, share, 0)
    dot = functools.partial(
        jnp.dot, precision=lax.Precision.HIGHEST, preferred_element_type=jnp.float32
    )
    residual = dot(traces, matrix) - measured_share.reshape(share * 2, time_len)
    back = dot(residual, matrix).astype(jnp.bfloat16)
    back_all = gather_slab(back.reshape(share, 2 * time_len))
    grad = backward(back_all, kern_rows, tally, kinds, places, width, 4)
    gradient = scatter_sens(grad).T
    return (residual.reshape(share, 2, time_len), gradient)


def solution(mesh):
    return jax.shard_map(
        per_device,
        mesh=mesh,
        in_specs=(
            P("slab", None),
            P(),
            P(),
            P("sens", None, None),
            P("sens", "slab", None),
            P("sens", "slab", None),
            P("sens", "slab", None),
            P("sens", "slab"),
        ),
        out_specs=(P(("sens", "slab"), None, None), P("slab", "sens")),
        check_vma=False,
    )
```

time: 295 us -> 124 us (0.42)
  local copies, waits for them, and re-layouts: 125 us -> 5.99 us
  matrix products: 94.8 us -> 5.07 us
  Pallas kernels: 0 us -> 44.7 us
  between operations: 14.2 us -> 0.89 us
  starting transfers between devices: 0.08 us -> 9.88 us
  waiting for transfers between devices: 36.5 us -> 31.6 us
    dot_general x9 -> x3, matrix products: 94.8 us -> 5.07 us  [the longest x1 3.56 us: filter_matrix(): lax.dot_general(basis * gains, basis, (((1,), (1,)), ((), ())), precision...]
    gather x1 -> x0, local copies, waits for them, and re-layouts: 57.4 us -> none  [per_device(): pressure[picked_ids]]
    reshape x5 -> x4, local copies, waits for them, and re-layouts: 57.9 us -> 0.87 us  [the longest x1 0.73 us: per_device(): return (residual.reshape(share, 2, time_len), gradient)]
    pallas_call x0 -> x2, Pallas kernels: none -> 44.7 us  [the longest x1 31.1 us: forward(): pl.pallas_call(functools.partial(forward_kernel, kinds, places), grid=(st...]
    reduce_scatter x2 -> x0, waiting for transfers between devices: 36.4 us -> none  [the longest x1 36.4 us: per_device(): lax.psum_scatter(partial_grad, 'sens', scatter_dimension=1, tiled=True)]
    ppermute x0 -> x7, waiting for transfers between devices: none -> 31.6 us  [the longest x3 23.7 us: scatter_sens(): lax.ppermute(block, 'sens', [(q, q ^ step) for q in range(groups)])]
    ppermute x0 -> x7, starting transfers between devices: none -> 9.88 us  [the longest x3 5.81 us: scatter_slab(): lax.ppermute(block, 'slab', [(j, (j + 2 * step) % slabs) for j in range(s...]
    transpose x1 -> x0, local copies, waits for them, and re-layouts: 3.73 us -> none  [per_device(): jnp.einsum('swt,cvt->scwv', piece_rows, placed_kern, preferred_element_ty...]
  transfers between devices with their start and end apart: 2 -> 7, of which waited for: 1 -> 5; matrix products, arithmetic and copies ran while one was open for 36% -> 7% of each run, Pallas kernels for 0% -> 0%
where the time goes in v1:
time: 124 us; the launch traced here: 123 us
  Pallas kernels  44.7 us (36%)
  waiting for transfers between devices  31.6 us (25%)
  blocking collectives  15.9 us (13%)
  starting transfers between devices  9.88 us (8%)
  other arithmetic  9.4 us (8%)
  local copies, waits for them, and re-layouts  5.99 us (5%)
  matrix products  5.07 us (4%)
    pallas_call x1, Pallas kernels, forward(): pl.pallas_call(functools.partial(forward_kernel, kinds, places), grid=(st...  31.1 us
    ppermute x3, waiting for transfers between devices, scatter_sens(): lax.ppermute(block, 'sens', [(q, q ^ step) for q in range(groups)])  23.7 us
    all_gather x1, blocking collectives, gather_slab(): return lax.all_gather(share, 'slab', axis=0, tiled=True)  15.9 us
    pallas_call x1, Pallas kernels, backward(): pl.pallas_call(functools.partial(backward_kernel, kinds, places), grid=(s...  13.6 us
    ppermute x3, waiting for transfers between devices, scatter_slab(): lax.ppermute(block, 'slab', [(j, (j + 2 * step) % slabs) for j in range(s...  7.86 us
    ppermute x3, starting transfers between devices, scatter_slab(): lax.ppermute(block, 'slab', [(j, (j + 2 * step) % slabs) for j in range(s...  5.81 us
    sin x1, other arithmetic, filter_matrix(): basis = jnp.concatenate([jnp.cos(angles), jnp.sin(angles)], axis=1)  4.09 us
    dot_general x1, matrix products, filter_matrix(): lax.dot_general(basis * gains, basis, (((1,), (1,)), ((), ())), precision...  3.56 us
  transfers between devices with their start and end apart: 7, of which 5 were waited for; matrix products, arithmetic and copies ran while one was open for 7% of the time, Pallas kernels for 0%

profile of v1, /device:TPU:0, one launch (start us, length us, event | category | flops | bytes accessed | tf_op | source)
XLA Modules:
  0.0 123.4 jit_solution(4502267973215781018)
XLA Ops:
  0.6 0.0 copy-start
  0.7 0.1 lt.97
  0.8 0.5 broadcast.92
  1.3 1.3 %reduce.3 = s32[256]{0:T(256)S(1)} reduce(s32[256,1]{0,1:T(1,128)} %param.15, s32[]{:T(128)} %broadcast.92), dimensions={1}, to_apply=%param.15.reduce_sub_computation.3 | reduce | bytes 2052 | tf_op args[7]
  2.6 0.1 lt.99
  2.7 0.9 multiply_add_fusion
  3.6 0.1 copy.13
  3.7 0.1 add.141
  3.8 0.1 add.137
  4.0 0.0 copy-start.2
  4.0 0.1 add.138
  4.1 0.1 lt.100
  4.2 0.1 lt.101
  4.4 0.9 copy.12
  5.3 0.1 squeeze.38
  5.4 0.7 fusion.29.code_ref
  6.1 31.1 %forward.1 = (bf16[3072,4096]{1,0:T(8,128)(2,1)}, f32[256,1024]{1,0:T(8,128)}) custom-call(s32[64,256]{1,0:T(8,128)} %fusion.29.code_ref, bf16[4096,128]{1,0:T(8,128)(2,1)} %pressure_ref.1, bf16[256,256]{1,0:T(8,128)(2,1)} %bitcast.48), custom_call_target="tpu_custom_call" | custom-call | tf_op jit(solution)/shard_map/forward/pallas_call | solution.py:114
  37.2 0.0 copy-start.1
  37.2 1.2 dynamic-slice_bitcast_fusion.3
  38.4 0.5 collective-permute-start
  38.9 0.0 copy-done
  38.9 0.1 reshape.60
  39.0 0.0 copy-done.2
  39.1 4.1 %fusion.20 = (f32[512,512]{1,0:T(8,128)S(1)}, f32[512,512]{1,0:T(8,128)S(1)}) fusion(), kind=kLoop, calls=%fused_computation.26 | loop fusion | flops 3670016 | bytes 2097152 | tf_op jit(solution)/shard_map/sin | solution.py:20
  43.2 0.0 collective-permute-done
  43.2 0.0 copy-done.1
  43.2 0.1 bitcast_add_fusion.1
  43.3 2.8 %collective-permute-start.1 = (f32[32,1024]{1,0:T(8,128)S(1)}, f32[32,1024]{1,0:T(8,128)S(1)}, u32[]{:S(2)}, u32[]{:S(2)}) collective-permute-start(f32[32,1024]{1,0:T(8,128)S(1)} %get-tuple-element.9), channel_id=1, source_target_pairs={{0,2},{1,3},{2,4},{3,5},{4,6},{5,7},{6,0},{7,1},{8,10},{9,11},{10,... | collective-permute-start | bytes 393224 | tf_op jit(solution)/shard_map/ppermute | solution.py:212
  46.1 2.1 %collective-permute-start.3 = (f32[32,1024]{1,0:T(8,128)S(1)}, f32[32,1024]{1,0:T(8,128)S(1)}, u32[]{:S(2)}, u32[]{:S(2)}) collective-permute-start(f32[32,1024]{1,0:T(8,128)S(1)} %get-tuple-element.10), channel_id=1, source_target_pairs={{0,6},{1,7},{2,0},{3,1},{4,2},{5,3},{6,4},{7,5},{8,14},{9,15},{10,... | collective-permute-start | bytes 393224 | tf_op jit(solution)/shard_map/ppermute | solution.py:212
  48.2 0.9 collective-permute-start.2
  49.1 3.6 %fusion.5 = f32[512,512]{1,0:T(8,128)S(1)} fusion(f32[512,512]{1,0:T(8,128)S(1)} %get-tuple-element.12, f32[512,512]{1,0:T(8,128)S(1)} %get-tuple-element.13, f32[1024]{0:T(1024)S(1)} %pad_maximum_fusion), kind=kOutput, calls=%fused_computation.8 | convolution fusion | flops 3223060480 | bytes 3149824 | tf_op jit(solution)/shard_map/dot_general | solution.py:22
  52.7 0.0 collective-permute-done.1
  52.7 1.7 %collective-permute-done.3 = f32[32,1024]{1,0:T(8,128)S(1)} collective-permute-done((f32[32,1024]{1,0:T(8,128)S(1)}, f32[32,1024]{1,0:T(8,128)S(1)}, u32[]{:S(2)}, u32[]{:S(2)}) %collective-permute-start.3) | collective-permute-done | bytes 131104 | tf_op jit(solution)/shard_map/ppermute | solution.py:212
  54.4 6.2 %collective-permute-done.2 = f32[32,1024]{1,0:T(8,128)S(1)} collective-permute-done((f32[32,1024]{1,0:T(8,128)S(1)}, f32[32,1024]{1,0:T(8,128)S(1)}, u32[]{:S(2)}, u32[]{:S(2)}) %collective-permute-start.2) | collective-permute-done | bytes 131104 | tf_op jit(solution)/shard_map/ppermute | solution.py:212
  60.6 0.8 convolution_subtract_fusion
  61.4 0.8 convolution_convert_fusion
  62.2 15.9 %all_gather.3.back_ref = bf16[256,1024]{1,0:T(8,128)(2,1)} all-gather(bf16[32,1024]{1,0:T(8,128)(2,1)S(1)} %reshape.62), channel_id=1, replica_groups=mesh['sens'=4,'slab'=8] {'slab'}, dimensions={0}, use_global_device_ids=true | all-gather | bytes 589824 | tf_op jit(solution)/shard_map/all_gather | solution.py:219
  78.1 13.6 %backward.1 = f32[128,4096]{1,0:T(8,128)} custom-call(bf16[256,1024]{1,0:T(8,128)(2,1)} %all_gather.3.back_ref, bf16[256,256]{1,0:T(8,128)(2,1)} %bitcast.49, bf16[3072,4096]{1,0:T(8,128)(2,1)} %get-tuple-element.5.tally_ref), custom_call_target="tpu_custom_call" | custom-call | tf_op jit(solution)/shard_map/backward/pallas_call | solution.py:178
  91.7 1.5 %dynamic-slice_bitcast_fusion.2 = (f32[32,4096]{1,0:T(8,128)S(1)}, f32[32,4096]{1,0:T(8,128)S(1)}, f32[32,4096]{1,0:T(8,128)S(1)}) fusion(f32[4,32,4096]{2,1,0:T(8,128)} %bitcast.44, s32[]{:T(128)S(6)} %select_n.114, s32[]{:T(128)S(6)} %select_n.116, s32[]{:T(128)S(6)} %select_n.115), kind=kLoop, calls=%fused_computation.25 | loop fusion | bytes 3145740 | tf_op jit(solution)/shard_map/jit(dynamic_index_in_dim)/squeeze | solution.py:228
  93.2 1.6 %collective-permute-start.4 = (f32[32,4096]{1,0:T(8,128)S(1)}, f32[32,4096]{1,0:T(8,128)S(1)}, u32[]{:S(2)}, u32[]{:S(2)}) collective-permute-start(f32[32,4096]{1,0:T(8,128)S(1)} %get-tuple-element.6), channel_id=1, source_target_pairs={{0,8},{8,0},{16,24},{24,16},{1,9},{9,1},{17,25},{25,17},{2,10},{10... | collective-permute-start | bytes 1572872 | tf_op jit(solution)/shard_map/ppermute | solution.py:229
  94.7 1.5 %collective-permute-start.6 = (f32[32,4096]{1,0:T(8,128)S(1)}, f32[32,4096]{1,0:T(8,128)}, u32[]{:S(2)}, u32[]{:S(2)}) collective-permute-start(f32[32,4096]{1,0:T(8,128)S(1)} %get-tuple-element.7), channel_id=1, source_target_pairs={{0,24},{8,16},{16,8},{24,0},{1,25},{9,17},{17,9},{25,1},{2,26},{10... | collective-permute-start | bytes 1572872 | tf_op jit(solution)/shard_map/ppermute | solution.py:229
  96.2 0.5 collective-permute-start.5
  96.7 0.7 reshape.61
  97.4 10.5 %collective-permute-done.4 = f32[32,4096]{1,0:T(8,128)S(1)} collective-permute-done((f32[32,4096]{1,0:T(8,128)S(1)}, f32[32,4096]{1,0:T(8,128)S(1)}, u32[]{:S(2)}, u32[]{:S(2)}) %collective-permute-start.4) | collective-permute-done | bytes 524320 | tf_op jit(solution)/shard_map/ppermute | solution.py:229
  108.0 11.8 %collective-permute-done.6 = f32[32,4096]{1,0:T(8,128)} collective-permute-done((f32[32,4096]{1,0:T(8,128)S(1)}, f32[32,4096]{1,0:T(8,128)}, u32[]{:S(2)}, u32[]{:S(2)}) %collective-permute-start.6) | collective-permute-done | bytes 524320 | tf_op jit(solution)/shard_map/ppermute | solution.py:229
  119.8 1.4 %collective-permute-done.5 = f32[32,4096]{1,0:T(8,128)} collective-permute-done((f32[32,4096]{1,0:T(8,128)S(1)}, f32[32,4096]{1,0:T(8,128)}, u32[]{:S(2)}, u32[]{:S(2)}) %collective-permute-start.5) | collective-permute-done | bytes 524320 | tf_op jit(solution)/shard_map/ppermute | solution.py:229
  121.2 2.2 %fusion.19 = f32[4096,32]{0,1:T(8,128)} fusion(f32[32,4096]{1,0:T(8,128)} %collective-permute-done.6, f32[32,4096]{1,0:T(8,128)} %collective-permute-done.5, f32[32,4096]{1,0:T(8,128)S(1)} %collective-permute-done.4, f32[4,32,4096]{2,1,0:T(8,128)} %bitcast.45, s32[]{:T(128)S(6)} %select_n.113), kind=kLoop, calls=%fused_computation.21 | loop fusion | flops 393216 | bytes 2621444 | tf_op jit(solution)/shard_map/transpose | solution.py:263
  (8 shorter events, 0.2 us)
Async XLA Ops:
  0.6 38.3 %copy-start = (f32[256,2,512]{2,1,0:T(2,128)S(1)}, f32[256,2,512]{2,1,0:T(2,128)}, u32[]{:S(2)}) copy-start(f32[256,2,512]{2,1,0:T(2,128)} %param.11) | copy-start | bytes 3145732
  4.0 35.1 %copy-start.2 = (f32[512]{0:T(512)S(1)}, f32[512]{0:T(512)}, u32[]{:S(2)}) copy-start(f32[512]{0:T(512)} %param.10) | copy-start | bytes 6148
  37.2 6.0 %copy-start.1 = (f32[256,1024]{1,0:T(8,128)S(1)}, f32[256,1024]{1,0:T(8,128)}, u32[]{:S(2)}) copy-start(f32[256,1024]{1,0:T(8,128)} %get-tuple-element.4) | copy-start | bytes 3145732
  38.4 4.8 %collective-permute-start = (f32[4,32,1024]{2,1,0:T(8,128)S(1)}, f32[4,32,1024]{2,1,0:T(8,128)S(1)}, u32[]{:S(2)}, u32[]{:S(2)}) collective-permute-start(f32[4,32,1024]{2,1,0:T(8,128)S(1)} %dynamic-slice_bitcast_fusion.3), channel_id=1, source_target_pairs={{0,1},{1,0},{2,3},{3,2},{4,5},{5,4},{6,7},{7,6},{8,9},{9,8},{10,11... | collective-permute-start | bytes 1572872 | tf_op jit(solution)/shard_map/ppermute | solution.py:208
  43.3 9.4 %collective-permute-start.1 = (f32[32,1024]{1,0:T(8,128)S(1)}, f32[32,1024]{1,0:T(8,128)S(1)}, u32[]{:S(2)}, u32[]{:S(2)}) collective-permute-start(f32[32,1024]{1,0:T(8,128)S(1)} %get-tuple-element.9), channel_id=1, source_target_pairs={{0,2},{1,3},{2,4},{3,5},{4,6},{5,7},{6,0},{7,1},{8,10},{9,11},{10,... | collective-permute-start | bytes 393224 | tf_op jit(solution)/shard_map/ppermute | solution.py:212
  46.1 8.3 %collective-permute-start.3 = (f32[32,1024]{1,0:T(8,128)S(1)}, f32[32,1024]{1,0:T(8,128)S(1)}, u32[]{:S(2)}, u32[]{:S(2)}) collective-permute-start(f32[32,1024]{1,0:T(8,128)S(1)} %get-tuple-element.10), channel_id=1, source_target_pairs={{0,6},{1,7},{2,0},{3,1},{4,2},{5,3},{6,4},{7,5},{8,14},{9,15},{10,... | collective-permute-start | bytes 393224 | tf_op jit(solution)/shard_map/ppermute | solution.py:212
  48.2 12.4 %collective-permute-start.2 = (f32[32,1024]{1,0:T(8,128)S(1)}, f32[32,1024]{1,0:T(8,128)S(1)}, u32[]{:S(2)}, u32[]{:S(2)}) collective-permute-start(f32[32,1024]{1,0:T(8,128)S(1)} %get-tuple-element.11), channel_id=1, source_target_pairs={{0,4},{1,5},{2,6},{3,7},{4,0},{5,1},{6,2},{7,3},{8,12},{9,13},{10,... | collective-permute-start | bytes 393224 | tf_op jit(solution)/shard_map/ppermute | solution.py:212
  93.2 14.8 %collective-permute-start.4 = (f32[32,4096]{1,0:T(8,128)S(1)}, f32[32,4096]{1,0:T(8,128)S(1)}, u32[]{:S(2)}, u32[]{:S(2)}) collective-permute-start(f32[32,4096]{1,0:T(8,128)S(1)} %get-tuple-element.6), channel_id=1, source_target_pairs={{0,8},{8,0},{16,24},{24,16},{1,9},{9,1},{17,25},{25,17},{2,10},{10... | collective-permute-start | bytes 1572872 | tf_op jit(solution)/shard_map/ppermute | solution.py:229
  94.7 25.1 %collective-permute-start.6 = (f32[32,4096]{1,0:T(8,128)S(1)}, f32[32,4096]{1,0:T(8,128)}, u32[]{:S(2)}, u32[]{:S(2)}) collective-permute-start(f32[32,4096]{1,0:T(8,128)S(1)} %get-tuple-element.7), channel_id=1, source_target_pairs={{0,24},{8,16},{16,8},{24,0},{1,25},{9,17},{17,9},{25,1},{2,26},{10... | collective-permute-start | bytes 1572872 | tf_op jit(solution)/shard_map/ppermute | solution.py:229
  96.2 24.9 %collective-permute-start.5 = (f32[32,4096]{1,0:T(8,128)S(1)}, f32[32,4096]{1,0:T(8,128)}, u32[]{:S(2)}, u32[]{:S(2)}) collective-permute-start(f32[32,4096]{1,0:T(8,128)S(1)} %get-tuple-element.8), channel_id=1, source_target_pairs={{0,16},{8,24},{16,0},{24,8},{1,17},{9,25},{17,1},{25,9},{2,18},{10... | collective-permute-start | bytes 1572872 | tf_op jit(solution)/shard_map/ppermute | solution.py:229

commit v2 on v0

v2 whole, which is shorter than its diff:
```python
import functools
import math

import jax
import jax.numpy as jnp
import numpy as np
from jax import lax
from jax.experimental import pallas as pl
from jax.experimental.pallas import tpu as pltpu
from jax.sharding import PartitionSpec as P

LANES = 256
UNIT = 4
HOT = jnp.float8_e4m3fn
CODE = 32766.0
TINY = 1e-37
RATE = 256 / math.log(2.0)
GRAIN = 256
PARTS = 2


def in_hbm(array):
    return pltpu.with_memory_space_constraint(array, pltpu.HBM)


def to_bf16(array):
    return array.astype(jnp.float32).astype(jnp.bfloat16)


def filter_kernel(gains_ref, cosine_ref, matrix_ref):
    time_len = cosine_ref.shape[0]
    row = jnp.dot(
        jnp.broadcast_to(gains_ref[...], (8, time_len)),
        cosine_ref[...],
        precision=lax.Precision.HIGHEST,
        preferred_element_type=jnp.float32,
    )
    wide = jnp.broadcast_to(row[:1] / time_len, (time_len, time_len))
    matrix_ref[...] = pltpu.roll(wide, 0, axis=1, stride=1, stride_axis=0)


def filter_matrix(filter_gains):
    time_len = filter_gains.shape[0]
    ids = np.arange(time_len)
    cosine = np.cos(np.outer(ids, ids) % time_len * (2.0 * math.pi / time_len))
    return pl.pallas_call(
        filter_kernel,
        out_shape=pltpu.VMEM((time_len, time_len), jnp.float32),
        compiler_params=pltpu.CompilerParams(vmem_limit_bytes=8 << 20),
        name="filter_matrix",
    )(filter_gains[None, :], jnp.asarray(cosine, jnp.float32))


def split_parts(array, count):
    parts = []
    for _ in range(count):
        part = array.astype(jnp.bfloat16)
        parts.append(part)
        array = array - part.astype(jnp.float32)
    return parts


def forward_kernel(
    kinds,
    places,
    core_ref,
    blocks_hbm,
    frames_hbm,
    classes_hbm,
    counts_hbm,
    pressure_hbm,
    kernel_hbm,
    *refs,
):
    tally_hbms = refs[:PARTS]
    (
        mine_ref,
        other_ref,
        blocks_ref,
        frames_ref,
        classes_ref,
        counts_ref,
        pressure_ref,
        kernel_ref,
        tally_ref,
        code_ref,
        grouped_ref,
        in_sems,
        out_sems,
    ) = refs[PARTS:]
    loads = [
        pltpu.make_async_copy(source, target, in_sems.at[spot])
        for spot, (source, target) in enumerate(
            (
                (blocks_hbm, blocks_ref),
                (frames_hbm, frames_ref),
                (classes_hbm, classes_ref),
                (counts_hbm, counts_ref),
                (pressure_hbm, pressure_ref),
                (kernel_hbm, kernel_ref),
            )
        )
    ]
    for load in loads:
        load.start()
    for load in loads[:4]:
        load.wait()
    combos = kinds * places
    rows = UNIT * combos
    block_count = pressure_ref.shape[0]
    tops = block_count // LANES
    slots, sensors = blocks_ref.shape
    units = sensors // UNIT
    voxels = pressure_ref.shape[1] // 2
    frame = kernel_ref.shape[1] // 2

    block_ids = blocks_ref[...]
    lane = lax.broadcasted_iota(jnp.int32, (slots, sensors), 1) // units
    row_ids = lane * combos + frames_ref[...] * kinds + classes_ref[...]
    live = lax.broadcasted_iota(jnp.int32, (slots, sensors), 0) < counts_ref[...]
    code = jnp.where(live, row_ids * block_count + block_ids, -1).T
    code_ref[...] = jnp.concatenate(
        [code[part * units : (part + 1) * units] for part in range(UNIT)], axis=1
    )

    width = UNIT * slots
    row_iota = to_bf16(lax.broadcasted_iota(jnp.int32, (rows, width), 0))
    low_iota = to_bf16(lax.broadcasted_iota(jnp.int32, (LANES, width), 0))
    one, zero = jnp.ones((), jnp.bfloat16), jnp.zeros((), jnp.bfloat16)

    def unit_step(unit, _):
        code = code_ref[pl.ds(unit, 1), :]
        row_code = lax.div(code, block_count)
        block_code = code & (block_count - 1)
        top_code = jnp.where(code < 0, -1, lax.div(block_code, LANES))
        low_code = to_bf16(block_code & (LANES - 1))
        row_hot = []
        for top in range(tops):
            picked = to_bf16(jnp.where(top_code == top, row_code, -1))
            row_hot.append(jnp.where(row_iota == picked, one, zero))
        row_hot = jnp.concatenate(row_hot, axis=0).astype(HOT)
        low_hot = jnp.where(low_iota == low_code, one, zero).astype(HOT)
        tally = lax.dot_general(
            row_hot, low_hot, (((1,), (1,)), ((), ())), preferred_element_type=jnp.float32
        ).astype(jnp.bfloat16)
        base = pl.multiple_of(unit * rows, rows)
        for top in range(tops):
            tally_ref[pl.ds(base, rows), top * LANES : (top + 1) * LANES] = tally[
                top * rows : (top + 1) * rows
            ]
        return 0

    chunks = out_sems.shape[0]
    span = units // chunks
    stores = []
    for chunk in range(chunks):
        lax.fori_loop(chunk * span, (chunk + 1) * span, unit_step, 0, unroll=4)
        part = pl.ds(chunk * span * rows, span * rows)
        for spot, tally_hbm in enumerate(tally_hbms):
            width = tally_hbm.shape[1]
            store = pltpu.make_async_copy(
                tally_ref.at[part, pl.ds(spot * width, width)],
                tally_hbm.at[part],
                out_sems.at[chunk, spot],
            )
            store.start()
            stores.append(store)
    for load in loads[4:]:
        load.wait()
    grouped_ref[...] = jnp.dot(
        tally_ref[...], pressure_ref[...], preferred_element_type=jnp.float32
    )
    core = core_ref[0]
    share = mine_ref.shape[1]
    for part in range(UNIT):
        sums = [None] * (places + 1)
        for place in range(places):
            first = part * combos + place * kinds
            picked = [
                grouped_ref[pl.ds(first + kind, units, stride=rows), :] for kind in range(kinds)
            ]
            wide = jnp.concatenate(
                [
                    jnp.concatenate([g[:, w * voxels : (w + 1) * voxels] for g in picked], axis=1)
                    for w in range(2)
                ],
                axis=0,
            )
            taps = jnp.dot(
                jnp.concatenate(split_parts(wide, 3), axis=0),
                kernel_ref[...],
                preferred_element_type=jnp.float32,
            )
            count = 2 * units
            taps = taps[:count] + (taps[count : 2 * count] + taps[2 * count :])
            for half in range(2):
                piece = taps[:, half * frame : (half + 1) * frame]
                spot = place + half
                sums[spot] = piece if sums[spot] is None else sums[spot] + piece
        total = jnp.concatenate(sums, axis=1)
        total = jnp.concatenate([total[:units], total[units:]], axis=1)
        pairs = units // (2 * share)
        for pair in range(pairs):
            even = total[2 * pair * share : (2 * pair + 1) * share]
            odd = total[(2 * pair + 1) * share : (2 * pair + 2) * share]
            mine_ref[part * pairs + pair] = jnp.where(core == 0, even, odd)
            other_ref[part * pairs + pair] = jnp.where(core == 0, odd, even)
    for store in stores:
        store.wait()


def forward(blocks, frames, classes, counts, pressure, kern_rows, kinds, places, time_len):
    slots, sensors = blocks.shape
    combos = kinds * places
    block_count = pressure.shape[0]
    slabs = lax.axis_size("slab")
    core = (lax.axis_index("slab") % 2).reshape(1)
    anywhere = pl.BlockSpec(memory_space=pltpu.HBM)
    vmem = pl.BlockSpec(memory_space=pltpu.VMEM)
    half = (slabs // 2, sensors // slabs, 2 * time_len)
    tally = jax.ShapeDtypeStruct((sensors * combos, block_count // PARTS), jnp.bfloat16)
    operands = (blocks, frames, classes, counts, pressure, kern_rows)
    *tallies, mine, other = pl.pallas_call(
        functools.partial(forward_kernel, kinds, places),
        in_specs=[pl.BlockSpec(memory_space=pltpu.SMEM)] + [anywhere] * 6,
        out_specs=[anywhere] * PARTS + [vmem, vmem],
        out_shape=[tally] * PARTS
        + [
            jax.ShapeDtypeStruct(half, jnp.float32),
            jax.ShapeDtypeStruct(half, jnp.float32),
        ],
        scratch_shapes=[pltpu.VMEM(operand.shape, operand.dtype) for operand in operands]
        + [
            pltpu.VMEM((tally.shape[0], block_count), tally.dtype),
            pltpu.VMEM((sensors // UNIT, UNIT * slots), jnp.int32),
            pltpu.VMEM((sensors * combos, pressure.shape[1]), jnp.float32),
            pltpu.SemaphoreType.DMA((len(operands),)),
            pltpu.SemaphoreType.DMA((8, PARTS)),
        ],
        compiler_params=pltpu.CompilerParams(vmem_limit_bytes=48 << 20),
        name="forward",
    )(core, *[in_hbm(operand) for operand in operands])
    return tallies, mine, other


def fill_responses(kinds, places, order_ref, piece_refs, kernel_ref, resp_ref, back_ref, wide_ref):
    combos = kinds * places
    rows = UNIT * combos
    share = piece_refs[0].shape[0]
    sensors = back_ref.shape[0]
    units = sensors // UNIT
    time_len = back_ref.shape[1] // 2
    taps = kernel_ref.shape[1]
    frame = taps // 2
    width = wide_ref.shape[1]
    voxels = width // 2
    for spot, piece_ref in enumerate(piece_refs):
        start = pl.multiple_of(order_ref[spot] * share, share)
        back_ref[pl.ds(start, share), :] = piece_ref[...]
    for place in range(places):
        waves = []
        for w in range(2):
            start = w * time_len + place * frame
            waves.append(
                lax.dot_general(
                    back_ref[:, start : start + taps],
                    kernel_ref[...],
                    (((1,), (1,)), ((), ())),
                    preferred_element_type=jnp.float32,
                )
            )
        for kind in range(kinds):
            cut = slice(kind * voxels, (kind + 1) * voxels)
            both = jnp.concatenate([waves[0][:, cut], waves[1][:, cut]], axis=1)
            for part in range(UNIT):
                first = part * combos + place * kinds + kind
                wide_ref[pl.ds(first, units, stride=rows), :] = both[
                    part * units : (part + 1) * units
                ]
    high, low = split_parts(wide_ref[...].T, 2)
    resp_ref[:width] = high
    resp_ref[width:] = low


def backward_kernel(kinds, places, pieces, own_ref, tally_hbm, *refs):
    if pieces:
        order_ref, *piece_refs = refs[: pieces + 1]
        kernel_ref, resp_ref, kept_ref, *code_refs = refs[pieces + 1 : -5]
        tally_ref, grad_ref, sems, back_ref, wide_ref = refs[-5:]
    else:
        resp_ref, kept_ref, *code_refs = refs[:-3]
        tally_ref, grad_ref, sems = refs[-3:]
    groups, share, span = grad_ref.shape
    cuts = sems.shape[0]
    loads = []
    for cut in range(cuts):
        here = pl.ds(cut * (span // cuts), span // cuts)
        loads.append(
            pltpu.make_async_copy(tally_hbm.at[:, here], tally_ref.at[:, here], sems.at[cut])
        )
        loads[-1].start()
    if pieces:
        fill_responses(
            kinds, places, order_ref, piece_refs, kernel_ref, resp_ref, back_ref, wide_ref
        )
    width = groups * share
    for cut, load in enumerate(loads):
        load.wait()
        here = slice(cut * (span // cuts), (cut + 1) * (span // cuts))
        both = jnp.dot(resp_ref[...], tally_ref[:, here], preferred_element_type=jnp.float32)
        both = both[:width] + both[width:]
        for group in range(groups):
            grad_ref[group, :, here] = both[group * share : (group + 1) * share]
    own = own_ref[0]
    kept_ref[...] = grad_ref[own]
    lanes = code_refs[0].shape[1] - span
    lane = lax.broadcasted_iota(jnp.int32, (share, lanes), 1)
    for step, code_ref in enumerate(code_refs, 1):
        levels = jnp.zeros((share, lanes), jnp.int32)
        for spot in range(span // GRAIN):
            cut = slice(spot * GRAIN, (spot + 1) * GRAIN)
            block = grad_ref[own ^ step, :, cut]
            top = jnp.maximum(jnp.max(jnp.abs(block), axis=1, keepdims=True), TINY)
            level = jnp.minimum(jnp.floor(jnp.log(top) * RATE) + 2.0, CODE)
            code = block * jnp.exp(level * (-1.0 / RATE)) * CODE
            code_ref[:, cut] = jnp.floor(code + 0.5).astype(jnp.int32).astype(jnp.int16)
            levels = jnp.where(lane == spot, level.astype(jnp.int32), levels)
        code_ref[:, span:] = levels.astype(jnp.int16)


def backward(own, tally, width, resp=None, order=None, pieces=(), kern_rows=None, combos=None):
    groups = lax.axis_size("sens")
    share, (rows, span) = width // groups, tally.shape
    vmem = pl.BlockSpec(memory_space=pltpu.VMEM)
    smem = pl.BlockSpec(memory_space=pltpu.SMEM)
    hbm = pl.BlockSpec(memory_space=pltpu.HBM)
    out_shape = [jax.ShapeDtypeStruct((share, span), jnp.float32)] + [
        jax.ShapeDtypeStruct((share, span + 128), jnp.int16)
    ] * (groups - 1)
    scratch = [
        pltpu.VMEM((rows, span), tally.dtype),
        pltpu.VMEM((groups, share, span), jnp.float32),
        pltpu.SemaphoreType.DMA((4,)),
    ]
    if resp is None:
        operands = (order, *pieces, kern_rows)
        specs = [smem] + [vmem] * (len(pieces) + 1)
        out_shape = [jax.ShapeDtypeStruct((2 * width, rows), jnp.bfloat16)] + out_shape
        length = pieces[0].shape[1]
        sensors = pieces[0].shape[0] * len(pieces)
        scratch += [
            pltpu.VMEM((sensors, length), jnp.bfloat16),
            pltpu.VMEM((rows, width), jnp.float32),
        ]
    else:
        operands, specs = (resp,), [vmem]
    outs = pl.pallas_call(
        functools.partial(backward_kernel, *(combos or (0, 0)), len(pieces)),
        in_specs=[smem, hbm] + specs,
        out_specs=[vmem] * len(out_shape),
        out_shape=out_shape,
        scratch_shapes=scratch,
        compiler_params=pltpu.CompilerParams(vmem_limit_bytes=32 << 20),
        cost_estimate=pl.CostEstimate(
            flops=4 * width * rows * span, bytes_accessed=2 * rows * span, transcendentals=0
        ),
        name="backward",
    )(own, in_hbm(tally), *operands)
    if resp is None:
        resp, *outs = outs
    kept, *codes = outs
    received = []
    for step, code in enumerate(codes, 1):
        received.append(lax.ppermute(code, "sens", [(q, q ^ step) for q in range(groups)]))
    return resp, [kept, *received]


def finish_kernel(*refs):
    part_refs, out_ref = refs[:-1], refs[-1]
    count = len(part_refs) // PARTS
    for part in range(PARTS):
        kept_ref, *code_refs = part_refs[part * count : (part + 1) * count]
        span = kept_ref.shape[1]
        for spot in range(span // GRAIN):
            cut = slice(spot * GRAIN, (spot + 1) * GRAIN)
            total = kept_ref[:, cut]
            for code_ref in code_refs:
                level = code_ref[:, span:].astype(jnp.int32).astype(jnp.float32)[:, spot : spot + 1]
                scale = jnp.exp(level * (1.0 / RATE)) * (1.0 / CODE)
                total = total + code_ref[:, cut].astype(jnp.int32).astype(jnp.float32) * scale
            start = part * span + spot * GRAIN
            out_ref[:, start : start + GRAIN] = total


def finish(parts):
    share, span = parts[0].shape
    return pl.pallas_call(
        finish_kernel,
        out_shape=jax.ShapeDtypeStruct((share, PARTS * span), jnp.float32),
        compiler_params=pltpu.CompilerParams(vmem_limit_bytes=8 << 20),
        name="finish",
    )(*parts)


def scatter_slab(mine, other, gains):
    slabs = lax.axis_size("slab")
    chips = slabs // 2
    place = lax.axis_index("slab")
    chip = place // 2
    paired = mine + lax.ppermute(other, "slab", [(j, j ^ 1) for j in range(slabs)])
    paired, gains = lax.optimization_barrier((paired, gains))
    total = lax.dynamic_index_in_dim(paired, chip, 0, keepdims=False)
    for step in (2, 1, 3) if chips == 4 else range(1, chips):
        block = lax.dynamic_index_in_dim(paired, chip ^ step, 0, keepdims=False)
        total = total + lax.ppermute(block, "slab", [(j, j ^ (2 * step)) for j in range(slabs)])
    return total, gains


def gather_slab(share):
    slabs = lax.axis_size("slab")
    place = lax.axis_index("slab")
    pieces, order = [share], [place]
    for step in range(1, slabs // 2):
        pieces.append(lax.ppermute(share, "slab", [(j, j ^ (2 * step)) for j in range(slabs)]))
        order.append(place ^ (2 * step))
    for spot in range(slabs // 2):
        pieces.append(lax.ppermute(pieces[spot], "slab", [(j, j ^ 1) for j in range(slabs)]))
        order.append(order[spot] ^ 1)
    return pieces, jnp.stack(order).astype(jnp.int32)


def per_device(pressure, kernels, filter_gains, measured, blocks, frames, classes, counts):
    kinds, voxels, taps = kernels.shape
    block_count, width = pressure.shape
    frame = taps // 2
    time_len = filter_gains.shape[0]
    places = time_len // frame - 1
    combos = kinds * places
    sensors, slots = blocks.shape[0], blocks.shape[2]
    share = sensors // lax.axis_size("slab")

    kern_rows = kernels.reshape(kinds * voxels, taps)

    tallies, mine, other = forward(
        blocks[:, 0, :].T,
        frames[:, 0, :].T,
        classes[:, 0, :].T,
        counts.T,
        pressure,
        kern_rows,
        kinds,
        places,
        time_len,
    )
    traces, gains = scatter_slab(mine, other, filter_gains)
    traces = traces.reshape(share * 2, time_len)
    matrix = filter_matrix(gains)
    measured_share = lax.dynamic_slice_in_dim(measured, lax.axis_index("slab") * share, share, 0)
    dot = functools.partial(
        jnp.dot, precision=lax.Precision.HIGHEST, preferred_element_type=jnp.float32
    )
    residual = dot(traces, matrix) - measured_share.reshape(share * 2, time_len)
    back = dot(residual, matrix).astype(jnp.bfloat16)
    back = back.reshape(share, 2 * time_len)
    pieces, order = gather_slab(back)
    own = lax.axis_index("sens").reshape(1)
    resp, parts = backward(
        own, tallies[0], width, None, order, pieces, kern_rows, (kinds, places)
    )
    for tally in tallies[1:]:
        parts = parts + backward(own, tally, width, resp)[1]
    gradient = finish(parts).T
    return (residual.reshape(share, 2, time_len), gradient)


def solution(mesh):
    return jax.shard_map(
        per_device,
        mesh=mesh,
        in_specs=(
            P("slab", None),
            P(),
            P(),
            P("sens", None, None),
            P("sens", "slab", None),
            P("sens", "slab", None),
            P("sens", "slab", None),
            P("sens", "slab"),
        ),
        out_specs=(P(("sens", "slab"), None, None), P("slab", "sens")),
        check_vma=False,
    )
```

time: 295 us -> 77.8 us (0.26)
  local copies, waits for them, and re-layouts: 125 us -> 3.81 us
  matrix products: 94.8 us -> 1.51 us
  Pallas kernels: 0 us -> 33.5 us
  starting transfers between devices: 0.08 us -> 18.5 us
  waiting for transfers between devices: 36.5 us -> 19.4 us
  blocking collectives: 16.6 us -> 0 us
  between operations: 14.2 us -> 0.78 us
  other arithmetic: 6.99 us -> 0.09 us
    dot_general x9 -> x2, matrix products: 94.8 us -> 1.51 us  [the longest x1 0.76 us: per_device(): back = dot(residual, matrix).astype(jnp.bfloat16)]
    gather x1 -> x0, local copies, waits for them, and re-layouts: 57.4 us -> none  [per_device(): pressure[picked_ids]]
    reshape x5 -> x4, local copies, waits for them, and re-layouts: 57.9 us -> 0.87 us  [the longest x1 0.73 us: per_device(): return (residual.reshape(share, 2, time_len), gradient)]
    reduce_scatter x2 -> x0, waiting for transfers between devices: 36.4 us -> none  [the longest x1 36.4 us: per_device(): lax.psum_scatter(partial_grad, 'sens', scatter_dimension=1, tiled=True)]
    pallas_call x0 -> x5, Pallas kernels: none -> 33.5 us  [the longest x1 18.2 us: forward(): pl.pallas_call(functools.partial(forward_kernel, kinds, places), in_specs...]
    ppermute x0 -> x17, waiting for transfers between devices: none -> 19.4 us  [the longest x3 6.46 us: scatter_slab(): lax.ppermute(block, 'slab', [(j, j ^ 2 * step) for j in range(slabs)])]
    ppermute x0 -> x17, starting transfers between devices: none -> 18.5 us  [the longest x6 7.11 us: backward(): lax.ppermute(code, 'sens', [(q, q ^ step) for q in range(groups)])]
    all_gather x1 -> x0, blocking collectives: 16.6 us -> none  [per_device(): piece_rows = lax.all_gather(back_share, 'slab', axis=0, tiled=True)]
  transfers between devices with their start and end apart: 2 -> 17, of which waited for: 1 -> 9; matrix products, arithmetic and copies ran while one was open for 36% -> 1% of each run, Pallas kernels for 0% -> 9%
where the time goes in v2:
time: 77.8 us; the launch traced here: 77.5 us
  Pallas kernels  33.5 us (43%)
  waiting for transfers between devices  19.4 us (25%)
  starting transfers between devices  18.5 us (24%)
  local copies, waits for them, and re-layouts  3.81 us (5%)
  matrix products  1.51 us (2%)
  between operations  0.78 us (1%)
    pallas_call x1, Pallas kernels, forward(): pl.pallas_call(functools.partial(forward_kernel, kinds, places), in_specs...  18.2 us
    pallas_call x2, Pallas kernels, backward(): pl.pallas_call(functools.partial(backward_kernel, *(combos or (0, 0)), le...  13.4 us
    ppermute x6, starting transfers between devices, backward(): lax.ppermute(code, 'sens', [(q, q ^ step) for q in range(groups)])  7.11 us
    ppermute x3, waiting for transfers between devices, scatter_slab(): lax.ppermute(block, 'slab', [(j, j ^ 2 * step) for j in range(slabs)])  6.46 us
    ppermute x3, starting transfers between devices, scatter_slab(): lax.ppermute(block, 'slab', [(j, j ^ 2 * step) for j in range(slabs)])  5.6 us
    ppermute x6, waiting for transfers between devices, backward(): lax.ppermute(code, 'sens', [(q, q ^ step) for q in range(groups)])  5.32 us
    ppermute x3, waiting for transfers between devices, gather_slab(): lax.ppermute(share, 'slab', [(j, j ^ 2 * step) for j in range(slabs)])  5.23 us
    ppermute x3, starting transfers between devices, gather_slab(): lax.ppermute(share, 'slab', [(j, j ^ 2 * step) for j in range(slabs)])  4.75 us
  transfers between devices with their start and end apart: 17, of which 9 were waited for; matrix products, arithmetic and copies ran while one was open for 1% of the time, Pallas kernels for 9%

profile of v2, /device:TPU:0, one launch (start us, length us, event | category | flops | bytes accessed | tf_op | source)
XLA Modules:
  0.0 77.5 jit_solution(2825556098953476245)
XLA Ops:
  0.6 0.0 copy-start
  0.7 18.2 %forward.1 = (bf16[3072,2048]{1,0:T(8,128)(2,1)}, bf16[3072,2048]{1,0:T(8,128)(2,1)}, f32[4,32,1024]{2,1,0:T(8,128)S(1)}, f32[4,32,1024]{2,1,0:T(8,128)S(1)}) custom-call(s32[1]{0:T(128)} %bitcast.core_ref, s32[64,256]{1,0:T(8,128)} %bitcast.43, s32[64,256]{1,0:T(8,128)} %bitcast.44, s32[64,256]{1,0:T(8,128)} %bitcast.45, s32[1,256]{1,0:T(1,128)} %bitcast.46, ...), custom_call_target="tpu_custom_call" | custom-call | tf_op jit(solution)/shard_map/forward/pallas_call | solution.py:223
  18.9 0.5 collective-permute-start
  19.4 1.5 %collective-permute-done = f32[4,32,1024]{2,1,0:T(8,128)S(1)} collective-permute-done((f32[4,32,1024]{2,1,0:T(8,128)S(1)}, f32[4,32,1024]{2,1,0:T(8,128)S(1)}, u32[]{:S(2)}, u32[]{:S(2)}) %collective-permute-start) | collective-permute-done | bytes 524320 | tf_op jit(solution)/shard_map/ppermute | solution.py:410
  20.9 0.1 add.34
  21.1 4.0 %collective-permute-start.1 = (f32[32,1024]{1,0:T(8,128)S(1)}, f32[32,1024]{1,0:T(8,128)S(1)}, u32[]{:S(2)}, u32[]{:S(2)}) collective-permute-start(f32[32,1024]{1,0:T(8,128)S(1)} %get-tuple-element.32), channel_id=1, source_target_pairs={{0,4},{1,5},{2,6},{3,7},{4,0},{5,1},{6,2},{7,3},{8,12},{9,13},{10,... | collective-permute-start | bytes 393224 | tf_op jit(solution)/shard_map/ppermute | solution.py:415
  25.1 1.4 %collective-permute-start.3 = (f32[32,1024]{1,0:T(8,128)S(1)}, f32[32,1024]{1,0:T(8,128)S(1)}, u32[]{:S(2)}, u32[]{:S(2)}) collective-permute-start(f32[32,1024]{1,0:T(8,128)S(1)} %get-tuple-element.33), channel_id=1, source_target_pairs={{0,6},{1,7},{2,4},{3,5},{4,2},{5,3},{6,0},{7,1},{8,14},{9,15},{10,... | collective-permute-start | bytes 393224 | tf_op jit(solution)/shard_map/ppermute | solution.py:415
  26.4 0.2 collective-permute-start.2
  26.6 0.0 copy-done
  26.7 0.1 reshape.28
  26.8 0.0 copy-start.1
  26.8 1.2 %copy-done.1 = f32[512,512]{1,0:T(8,128)S(1)} copy-done((f32[512,512]{1,0:T(8,128)S(1)}, f32[512,512]{1,0:T(8,128)}, u32[]{:S(2)}) %copy-start.1) | copy-done | bytes 1048600
  28.0 0.0 copy-start.3
  28.0 0.7 copy-done.3
  28.7 0.7 filter_matrix.1
  29.4 5.6 %collective-permute-done.1 = f32[32,1024]{1,0:T(8,128)S(1)} collective-permute-done((f32[32,1024]{1,0:T(8,128)S(1)}, f32[32,1024]{1,0:T(8,128)S(1)}, u32[]{:S(2)}, u32[]{:S(2)}) %collective-permute-start.1) | collective-permute-done | bytes 131104 | tf_op jit(solution)/shard_map/ppermute | solution.py:415
  35.0 0.0 collective-permute-done.3
  35.0 0.8 %collective-permute-done.2 = f32[32,1024]{1,0:T(8,128)S(1)} collective-permute-done((f32[32,1024]{1,0:T(8,128)S(1)}, f32[32,1024]{1,0:T(8,128)S(1)}, u32[]{:S(2)}, u32[]{:S(2)}) %collective-permute-start.2) | collective-permute-done | bytes 131104 | tf_op jit(solution)/shard_map/ppermute | solution.py:415
  35.9 0.8 convolution_subtract_fusion
  36.7 0.8 convolution_convert_fusion
  37.5 3.6 %collective-permute-start.6 = (bf16[32,1024]{1,0:T(8,128)(2,1)S(1)}, bf16[32,1024]{1,0:T(8,128)(2,1)S(1)}, u32[]{:S(2)}, u32[]{:S(2)}) collective-permute-start(bf16[32,1024]{1,0:T(8,128)(2,1)S(1)} %reshape.31.refs_1_), channel_id=1, source_target_pairs={{0,6},{1,7},{2,4},{3,5},{4,2},{5,3},{6,0},{7,1},{8,14},{9,15},{10,... | collective-permute-start | bytes 196616 | tf_op jit(solution)/shard_map/ppermute | solution.py:424
  41.1 0.7 collective-permute-start.5
  41.7 0.5 collective-permute-start.4
  42.2 0.0 collective-permute-start.7
  42.2 1.5 %collective-permute-done.6.refs_4_ = bf16[32,1024]{1,0:T(8,128)(2,1)S(1)} collective-permute-done((bf16[32,1024]{1,0:T(8,128)(2,1)S(1)}, bf16[32,1024]{1,0:T(8,128)(2,1)S(1)}, u32[]{:S(2)}, u32[]{:S(2)}) %collective-permute-start.6) | collective-permute-done | bytes 65568 | tf_op jit(solution)/shard_map/ppermute | solution.py:424
  43.7 0.0 collective-permute-start.10
  43.7 3.7 %collective-permute-done.5.refs_3_ = bf16[32,1024]{1,0:T(8,128)(2,1)S(1)} collective-permute-done((bf16[32,1024]{1,0:T(8,128)(2,1)S(1)}, bf16[32,1024]{1,0:T(8,128)(2,1)S(1)}, u32[]{:S(2)}, u32[]{:S(2)}) %collective-permute-start.5) | collective-permute-done | bytes 65568 | tf_op jit(solution)/shard_map/ppermute | solution.py:424
  47.5 0.0 collective-permute-start.9
  47.5 0.0 collective-permute-done.4.refs_2_
  47.5 0.5 collective-permute-start.8
  48.0 0.1 stack.35.refs_0_
  48.1 0.0 collective-permute-done.7.refs_5_
  48.1 0.0 collective-permute-done.10.refs_8_
  48.1 0.6 collective-permute-done.9.refs_7_
  48.7 0.2 collective-permute-done.8.refs_6_
  48.9 0.0 copy-start.2
  48.9 0.9 %copy-done.2 = bf16[4,64,256]{2,1,0:T(8,128)(2,1)S(1)} copy-done((bf16[4,64,256]{2,1,0:T(8,128)(2,1)S(1)}, bf16[4,64,256]{2,1,0:T(8,128)(2,1)}, u32[]{:S(2)}) %copy-start.2) | copy-done | bytes 131096
  49.8 7.2 %backward.2 = (bf16[256,3072]{1,0:T(8,128)(2,1)S(1)}, f32[32,2048]{1,0:T(8,128)S(1)}, s16[32,2176]{1,0:T(8,128)(2,1)S(1)}, s16[32,2176]{1,0:T(8,128)(2,1)S(1)}, s16[32,2176]{1,0:T(8,128)(2,1)S(1)}) custom-call(s32[1]{0:T(128)} %bitcast.14.own_ref, bf16[3072,2048]{1,0:T(8,128)(2,1)} %get-tuple-element.21.tally_hbm, s32[8]{0:T(128)S(1)} %stack.35.refs_0_, ...), custom_call_target="tpu_custom_call" | custom-call | flops 3221225472 | bytes 12582912 | tf_op jit(solution)/shard_map/backward/pallas_call | solution.py:357
  57.0 1.6 %collective-permute-start.11 = (s16[32,2176]{1,0:T(8,128)(2,1)S(1)}, s16[32,2176]{1,0:T(8,128)(2,1)S(1)}, u32[]{:S(2)}, u32[]{:S(2)}) collective-permute-start(s16[32,2176]{1,0:T(8,128)(2,1)S(1)} %get-tuple-element.23), channel_id=1, source_target_pairs={{0,8},{8,0},{16,24},{24,16},{1,9},{9,1},{17,25},{25,17},{2,10},{10... | collective-permute-start | bytes 417800 | tf_op jit(solution)/shard_map/ppermute | solution.py:374
  58.5 1.5 %collective-permute-start.12 = (s16[32,2176]{1,0:T(8,128)(2,1)S(1)}, s16[32,2176]{1,0:T(8,128)(2,1)S(1)}, u32[]{:S(2)}, u32[]{:S(2)}) collective-permute-start(s16[32,2176]{1,0:T(8,128)(2,1)S(1)} %get-tuple-element.24), channel_id=1, source_target_pairs={{0,16},{8,24},{16,0},{24,8},{1,17},{9,25},{17,1},{25,9},{2,18},{10... | collective-permute-start | bytes 417800 | tf_op jit(solution)/shard_map/ppermute | solution.py:374
  60.0 0.5 collective-permute-start.13
  60.5 6.3 %backward.3 = (f32[32,2048]{1,0:T(8,128)S(1)}, s16[32,2176]{1,0:T(8,128)(2,1)S(1)}, s16[32,2176]{1,0:T(8,128)(2,1)S(1)}, s16[32,2176]{1,0:T(8,128)(2,1)S(1)}) custom-call(s32[1]{0:T(128)} %bitcast.14.own_ref, bf16[3072,2048]{1,0:T(8,128)(2,1)} %get-tuple-element.26.tally_hbm, bf16[256,3072]{1,0:T(8,128)(2,1)S(1)} %get-tuple-element.27.refs_0_), custom_call_target="tpu_custom_call" | custom-call | flops 3221225472 | bytes 12582912 | tf_op jit(solution)/shard_map/backward/pallas_call | solution.py:357
  66.8 1.6 %collective-permute-start.14 = (s16[32,2176]{1,0:T(8,128)(2,1)S(1)}, s16[32,2176]{1,0:T(8,128)(2,1)S(1)}, u32[]{:S(2)}, u32[]{:S(2)}) collective-permute-start(s16[32,2176]{1,0:T(8,128)(2,1)S(1)} %get-tuple-element.29), channel_id=1, source_target_pairs={{0,8},{8,0},{16,24},{24,16},{1,9},{9,1},{17,25},{25,17},{2,10},{10... | collective-permute-start | bytes 417800 | tf_op jit(solution)/shard_map/ppermute | solution.py:374
  68.4 1.5 %collective-permute-start.15 = (s16[32,2176]{1,0:T(8,128)(2,1)S(1)}, s16[32,2176]{1,0:T(8,128)(2,1)S(1)}, u32[]{:S(2)}, u32[]{:S(2)}) collective-permute-start(s16[32,2176]{1,0:T(8,128)(2,1)S(1)} %get-tuple-element.30), channel_id=1, source_target_pairs={{0,16},{8,24},{16,0},{24,8},{1,17},{9,25},{17,1},{25,9},{2,18},{10... | collective-permute-start | bytes 417800 | tf_op jit(solution)/shard_map/ppermute | solution.py:374
  69.9 0.0 collective-permute-done.11.refs_1_
  69.9 0.5 collective-permute-start.16
  70.4 0.7 reshape.29
  71.1 0.0 collective-permute-done.12.refs_2_
  71.1 0.0 collective-permute-done.13.refs_3_
  71.1 1.5 %collective-permute-done.14.refs_5_ = s16[32,2176]{1,0:T(8,128)(2,1)S(1)} collective-permute-done((s16[32,2176]{1,0:T(8,128)(2,1)S(1)}, s16[32,2176]{1,0:T(8,128)(2,1)S(1)}, u32[]{:S(2)}, u32[]{:S(2)}) %collective-permute-start.14) | collective-permute-done | bytes 139296 | tf_op jit(solution)/shard_map/ppermute | solution.py:374
  72.5 3.9 %collective-permute-done.15.refs_6_ = s16[32,2176]{1,0:T(8,128)(2,1)S(1)} collective-permute-done((s16[32,2176]{1,0:T(8,128)(2,1)S(1)}, s16[32,2176]{1,0:T(8,128)(2,1)S(1)}, u32[]{:S(2)}, u32[]{:S(2)}) %collective-permute-start.15) | collective-permute-done | bytes 139296 | tf_op jit(solution)/shard_map/ppermute | solution.py:374
  76.4 0.0 collective-permute-done.16.refs_7_
  76.4 1.1 %finish.1 = f32[32,4096]{1,0:T(8,128)} custom-call(f32[32,2048]{1,0:T(8,128)S(1)} %get-tuple-element.22.refs_0_, s16[32,2176]{1,0:T(8,128)(2,1)S(1)} %collective-permute-done.11.refs_1_, s16[32,2176]{1,0:T(8,128)(2,1)S(1)} %collective-permute-done.12.refs_2_, s16[32,2176]{1,0:T(8,128)(2,1)S(1)} %collective-permute-done.13.refs_3_, ...), custom_call_target="tpu_custom_call" | custom-call | tf_op jit(solution)/shard_map/finish/pallas_call | solution.py:397
  (5 shorter events, 0.1 us)
Async XLA Ops:
  0.6 26.0 %copy-start = (f32[256,2,512]{2,1,0:T(2,128)S(1)}, f32[256,2,512]{2,1,0:T(2,128)}, u32[]{:S(2)}) copy-start(f32[256,2,512]{2,1,0:T(2,128)} %param.12) | copy-start | bytes 3145732
  18.9 2.1 %collective-permute-start = (f32[4,32,1024]{2,1,0:T(8,128)S(1)}, f32[4,32,1024]{2,1,0:T(8,128)S(1)}, u32[]{:S(2)}, u32[]{:S(2)}) collective-permute-start(f32[4,32,1024]{2,1,0:T(8,128)S(1)} %get-tuple-element.18), channel_id=1, source_target_pairs={{0,1},{1,0},{2,3},{3,2},{4,5},{5,4},{6,7},{7,6},{8,9},{9,8},{10,11... | collective-permute-start | bytes 1572872 | tf_op jit(solution)/shard_map/ppermute | solution.py:410
  21.1 14.0 %collective-permute-start.1 = (f32[32,1024]{1,0:T(8,128)S(1)}, f32[32,1024]{1,0:T(8,128)S(1)}, u32[]{:S(2)}, u32[]{:S(2)}) collective-permute-start(f32[32,1024]{1,0:T(8,128)S(1)} %get-tuple-element.32), channel_id=1, source_target_pairs={{0,4},{1,5},{2,6},{3,7},{4,0},{5,1},{6,2},{7,3},{8,12},{9,13},{10,... | collective-permute-start | bytes 393224 | tf_op jit(solution)/shard_map/ppermute | solution.py:415
  25.1 9.9 %collective-permute-start.3 = (f32[32,1024]{1,0:T(8,128)S(1)}, f32[32,1024]{1,0:T(8,128)S(1)}, u32[]{:S(2)}, u32[]{:S(2)}) collective-permute-start(f32[32,1024]{1,0:T(8,128)S(1)} %get-tuple-element.33), channel_id=1, source_target_pairs={{0,6},{1,7},{2,4},{3,5},{4,2},{5,3},{6,0},{7,1},{8,14},{9,15},{10,... | collective-permute-start | bytes 393224 | tf_op jit(solution)/shard_map/ppermute | solution.py:415
  26.4 9.4 %collective-permute-start.2 = (f32[32,1024]{1,0:T(8,128)S(1)}, f32[32,1024]{1,0:T(8,128)S(1)}, u32[]{:S(2)}, u32[]{:S(2)}) collective-permute-start(f32[32,1024]{1,0:T(8,128)S(1)} %get-tuple-element.34), channel_id=1, source_target_pairs={{0,2},{1,3},{2,0},{3,1},{4,6},{5,7},{6,4},{7,5},{8,10},{9,11},{10,... | collective-permute-start | bytes 393224 | tf_op jit(solution)/shard_map/ppermute | solution.py:415
  26.8 1.2 %copy-start.1 = (f32[512,512]{1,0:T(8,128)S(1)}, f32[512,512]{1,0:T(8,128)}, u32[]{:S(2)}) copy-start(f32[512,512]{1,0:T(8,128)} %constant.56.clone.cosine_ref) | copy-start | bytes 3145732
  28.0 0.7 copy-start.3
  37.5 6.2 %collective-permute-start.6 = (bf16[32,1024]{1,0:T(8,128)(2,1)S(1)}, bf16[32,1024]{1,0:T(8,128)(2,1)S(1)}, u32[]{:S(2)}, u32[]{:S(2)}) collective-permute-start(bf16[32,1024]{1,0:T(8,128)(2,1)S(1)} %reshape.31.refs_1_), channel_id=1, source_target_pairs={{0,6},{1,7},{2,4},{3,5},{4,2},{5,3},{6,0},{7,1},{8,14},{9,15},{10,... | collective-permute-start | bytes 196616 | tf_op jit(solution)/shard_map/ppermute | solution.py:424
  41.1 6.4 %collective-permute-start.5 = (bf16[32,1024]{1,0:T(8,128)(2,1)S(1)}, bf16[32,1024]{1,0:T(8,128)(2,1)S(1)}, u32[]{:S(2)}, u32[]{:S(2)}) collective-permute-start(bf16[32,1024]{1,0:T(8,128)(2,1)S(1)} %reshape.31.refs_1_), channel_id=1, source_target_pairs={{0,4},{1,5},{2,6},{3,7},{4,0},{5,1},{6,2},{7,3},{8,12},{9,13},{10,... | collective-permute-start | bytes 196616 | tf_op jit(solution)/shard_map/ppermute | solution.py:424
  41.7 5.7 %collective-permute-start.4 = (bf16[32,1024]{1,0:T(8,128)(2,1)S(1)}, bf16[32,1024]{1,0:T(8,128)(2,1)S(1)}, u32[]{:S(2)}, u32[]{:S(2)}) collective-permute-start(bf16[32,1024]{1,0:T(8,128)(2,1)S(1)} %reshape.31.refs_1_), channel_id=1, source_target_pairs={{0,2},{1,3},{2,0},{3,1},{4,6},{5,7},{6,4},{7,5},{8,10},{9,11},{10,... | collective-permute-start | bytes 196616 | tf_op jit(solution)/shard_map/ppermute | solution.py:424
  42.2 5.8 %collective-permute-start.7 = (bf16[32,1024]{1,0:T(8,128)(2,1)S(1)}, bf16[32,1024]{1,0:T(8,128)(2,1)S(1)}, u32[]{:S(2)}, u32[]{:S(2)}) collective-permute-start(bf16[32,1024]{1,0:T(8,128)(2,1)S(1)} %reshape.31.refs_1_), channel_id=1, source_target_pairs={{0,1},{1,0},{2,3},{3,2},{4,5},{5,4},{6,7},{7,6},{8,9},{9,8},{10,11... | collective-permute-start | bytes 196616 | tf_op jit(solution)/shard_map/ppermute | solution.py:427
  43.7 4.4 %collective-permute-start.10 = (bf16[32,1024]{1,0:T(8,128)(2,1)S(1)}, bf16[32,1024]{1,0:T(8,128)(2,1)S(1)}, u32[]{:S(2)}, u32[]{:S(2)}) collective-permute-start(bf16[32,1024]{1,0:T(8,128)(2,1)S(1)} %collective-permute-done.6.refs_4_), channel_id=1, source_target_pairs={{0,1},{1,0},{2,3},{3,2},{4,5},{5,4},{6,7},{7,6},{8,9},{9,8},{10,11... | collective-permute-start | bytes 196616 | tf_op jit(solution)/shard_map/ppermute | solution.py:427
  47.5 1.3 %collective-permute-start.9 = (bf16[32,1024]{1,0:T(8,128)(2,1)S(1)}, bf16[32,1024]{1,0:T(8,128)(2,1)S(1)}, u32[]{:S(2)}, u32[]{:S(2)}) collective-permute-start(bf16[32,1024]{1,0:T(8,128)(2,1)S(1)} %collective-permute-done.5.refs_3_), channel_id=1, source_target_pairs={{0,1},{1,0},{2,3},{3,2},{4,5},{5,4},{6,7},{7,6},{8,9},{9,8},{10,11... | collective-permute-start | bytes 196616 | tf_op jit(solution)/shard_map/ppermute | solution.py:427
  47.5 1.4 %collective-permute-start.8 = (bf16[32,1024]{1,0:T(8,128)(2,1)S(1)}, bf16[32,1024]{1,0:T(8,128)(2,1)S(1)}, u32[]{:S(2)}, u32[]{:S(2)}) collective-permute-start(bf16[32,1024]{1,0:T(8,128)(2,1)S(1)} %collective-permute-done.4.refs_2_), channel_id=1, source_target_pairs={{0,1},{1,0},{2,3},{3,2},{4,5},{5,4},{6,7},{7,6},{8,9},{9,8},{10,11... | collective-permute-start | bytes 196616 | tf_op jit(solution)/shard_map/ppermute | solution.py:427
  48.9 0.9 %copy-start.2 = (bf16[4,64,256]{2,1,0:T(8,128)(2,1)S(1)}, bf16[4,64,256]{2,1,0:T(8,128)(2,1)}, u32[]{:S(2)}) copy-start(bf16[4,64,256]{2,1,0:T(8,128)(2,1)} %param.10) | copy-start | bytes 393220
  57.0 12.9 %collective-permute-start.11 = (s16[32,2176]{1,0:T(8,128)(2,1)S(1)}, s16[32,2176]{1,0:T(8,128)(2,1)S(1)}, u32[]{:S(2)}, u32[]{:S(2)}) collective-permute-start(s16[32,2176]{1,0:T(8,128)(2,1)S(1)} %get-tuple-element.23), channel_id=1, source_target_pairs={{0,8},{8,0},{16,24},{24,16},{1,9},{9,1},{17,25},{25,17},{2,10},{10... | collective-permute-start | bytes 417800 | tf_op jit(solution)/shard_map/ppermute | solution.py:374
  58.5 12.6 %collective-permute-start.12 = (s16[32,2176]{1,0:T(8,128)(2,1)S(1)}, s16[32,2176]{1,0:T(8,128)(2,1)S(1)}, u32[]{:S(2)}, u32[]{:S(2)}) collective-permute-start(s16[32,2176]{1,0:T(8,128)(2,1)S(1)} %get-tuple-element.24), channel_id=1, source_target_pairs={{0,16},{8,24},{16,0},{24,8},{1,17},{9,25},{17,1},{25,9},{2,18},{10... | collective-permute-start | bytes 417800 | tf_op jit(solution)/shard_map/ppermute | solution.py:374
  60.0 11.1 %collective-permute-start.13 = (s16[32,2176]{1,0:T(8,128)(2,1)S(1)}, s16[32,2176]{1,0:T(8,128)(2,1)S(1)}, u32[]{:S(2)}, u32[]{:S(2)}) collective-permute-start(s16[32,2176]{1,0:T(8,128)(2,1)S(1)} %get-tuple-element.25), channel_id=1, source_target_pairs={{0,24},{8,16},{16,8},{24,0},{1,25},{9,17},{17,9},{25,1},{2,26},{10... | collective-permute-start | bytes 417800 | tf_op jit(solution)/shard_map/ppermute | solution.py:374
  66.8 5.7 %collective-permute-start.14 = (s16[32,2176]{1,0:T(8,128)(2,1)S(1)}, s16[32,2176]{1,0:T(8,128)(2,1)S(1)}, u32[]{:S(2)}, u32[]{:S(2)}) collective-permute-start(s16[32,2176]{1,0:T(8,128)(2,1)S(1)} %get-tuple-element.29), channel_id=1, source_target_pairs={{0,8},{8,0},{16,24},{24,16},{1,9},{9,1},{17,25},{25,17},{2,10},{10... | collective-permute-start | bytes 417800 | tf_op jit(solution)/shard_map/ppermute | solution.py:374
  68.4 8.0 %collective-permute-start.15 = (s16[32,2176]{1,0:T(8,128)(2,1)S(1)}, s16[32,2176]{1,0:T(8,128)(2,1)S(1)}, u32[]{:S(2)}, u32[]{:S(2)}) collective-permute-start(s16[32,2176]{1,0:T(8,128)(2,1)S(1)} %get-tuple-element.30), channel_id=1, source_target_pairs={{0,16},{8,24},{16,0},{24,8},{1,17},{9,25},{17,1},{25,9},{2,18},{10... | collective-permute-start | bytes 417800 | tf_op jit(solution)/shard_map/ppermute | solution.py:374
  69.9 6.5 %collective-permute-start.16 = (s16[32,2176]{1,0:T(8,128)(2,1)S(1)}, s16[32,2176]{1,0:T(8,128)(2,1)S(1)}, u32[]{:S(2)}, u32[]{:S(2)}) collective-permute-start(s16[32,2176]{1,0:T(8,128)(2,1)S(1)} %get-tuple-element.31), channel_id=1, source_target_pairs={{0,24},{8,16},{16,8},{24,0},{1,25},{9,17},{17,9},{25,1},{2,26},{10... | collective-permute-start | bytes 417800 | tf_op jit(solution)/shard_map/ppermute | solution.py:374

commit v3 on v2

--- a/solution.py
+++ b/solution.py
@@ -16,7 +16,8 @@
 TINY = 1e-37
 RATE = 256 / math.log(2.0)
 GRAIN = 256
-PARTS = 2
+SPANS = (4, 4)
+CUT = 512
 
 
 def in_hbm(array):
@@ -27,7 +28,17 @@
     return array.astype(jnp.float32).astype(jnp.bfloat16)
 
 
-def filter_kernel(gains_ref, cosine_ref, matrix_ref):
+def filter_kernel(gains_hbm, cosine_hbm, kernel_hbm, matrix_ref, fast_ref, *refs):
+    gains_ref, cosine_ref, sems = refs
+    pairs = [(gains_hbm, gains_ref), (cosine_hbm, cosine_ref), (kernel_hbm, fast_ref)]
+    copies = [
+        pltpu.make_async_copy(source, target, sems.at[spot])
+        for spot, (source, target) in enumerate(pairs)
+    ]
+    for copy in copies:
+        copy.start()
+    for copy in copies[:2]:
+        copy.wait()
     time_len = cosine_ref.shape[0]
     row = jnp.dot(
         jnp.broadcast_to(gains_ref[...], (8, time_len)),
@@ -37,18 +48,31 @@
     )
     wide = jnp.broadcast_to(row[:1] / time_len, (time_len, time_len))
     matrix_ref[...] = pltpu.roll(wide, 0, axis=1, stride=1, stride_axis=0)
-
-
-def filter_matrix(filter_gains):
+    for copy in copies[2:]:
+        copy.wait()
+
+
+def filter_matrix(filter_gains, kern_rows):
     time_len = filter_gains.shape[0]
     ids = np.arange(time_len)
     cosine = np.cos(np.outer(ids, ids) % time_len * (2.0 * math.pi / time_len))
+    operands = (filter_gains[None, :], jnp.asarray(cosine, jnp.float32), kern_rows)
     return pl.pallas_call(
         filter_kernel,
-        out_shape=pltpu.VMEM((time_len, time_len), jnp.float32),
+        in_specs=[pl.BlockSpec(memory_space=pltpu.HBM)] * 3,
+        out_specs=[pl.BlockSpec(memory_space=pltpu.VMEM)] * 2,
+        out_shape=[
+            pltpu.VMEM((time_len, time_len), jnp.float32),
+            pltpu.VMEM(kern_rows.shape, kern_rows.dtype),
+        ],
+        scratch_shapes=[
+            pltpu.VMEM((1, time_len), jnp.float32),
+            pltpu.VMEM((time_len, time_len), jnp.float32),
+            pltpu.SemaphoreType.DMA((3,)),
+        ],
         compiler_params=pltpu.CompilerParams(vmem_limit_bytes=8 << 20),
         name="filter_matrix",
-    )(filter_gains[None, :], jnp.asarray(cosine, jnp.float32))
+    )(*[in_hbm(operand) for operand in operands])
 
 
 def split_parts(array, count):
@@ -72,7 +96,7 @@
     kernel_hbm,
     *refs,
 ):
-    tally_hbms = refs[:PARTS]
+    tally_hbms = refs[: len(SPANS)]
     (
         mine_ref,
         other_ref,
@@ -87,7 +111,7 @@
         grouped_ref,
         in_sems,
         out_sems,
-    ) = refs[PARTS:]
+    ) = refs[len(SPANS) :]
     loads = [
         pltpu.make_async_copy(source, target, in_sems.at[spot])
         for spot, (source, target) in enumerate(
@@ -124,20 +148,25 @@
     )
 
     width = UNIT * slots
+    step = 16
     row_iota = to_bf16(lax.broadcasted_iota(jnp.int32, (rows, width), 0))
     low_iota = to_bf16(lax.broadcasted_iota(jnp.int32, (LANES, width), 0))
     one, zero = jnp.ones((), jnp.bfloat16), jnp.zeros((), jnp.bfloat16)
+    shift = LANES.bit_length() - 1
+    depth = block_count.bit_length() - 1
 
     def unit_step(unit, _):
         code = code_ref[pl.ds(unit, 1), :]
-        row_code = lax.div(code, block_count)
-        block_code = code & (block_count - 1)
-        top_code = jnp.where(code < 0, -1, lax.div(block_code, LANES))
-        low_code = to_bf16(block_code & (LANES - 1))
+        row_code = to_bf16(lax.shift_right_arithmetic(code, depth))
+        top_code = to_bf16(lax.shift_right_arithmetic(code & (block_count - 1), shift))
+        low_code = to_bf16(code & (LANES - 1))
+        picked = jnp.where(row_iota == row_code, one, zero)
+        top_code = jnp.broadcast_to(top_code, (step, width))
         row_hot = []
         for top in range(tops):
-            picked = to_bf16(jnp.where(top_code == top, row_code, -1))
-            row_hot.append(jnp.where(row_iota == picked, one, zero))
+            here = top_code == jnp.bfloat16(top)
+            for cut in range(0, rows, step):
+                row_hot.append(jnp.where(here, picked[cut : cut + step], zero))
         row_hot = jnp.concatenate(row_hot, axis=0).astype(HOT)
         low_hot = jnp.where(low_iota == low_code, one, zero).astype(HOT)
         tally = lax.dot_general(
@@ -156,15 +185,17 @@
     for chunk in range(chunks):
         lax.fori_loop(chunk * span, (chunk + 1) * span, unit_step, 0, unroll=4)
         part = pl.ds(chunk * span * rows, span * rows)
+        begin = 0
         for spot, tally_hbm in enumerate(tally_hbms):
-            width = tally_hbm.shape[1]
+            size = tally_hbm.shape[1]
             store = pltpu.make_async_copy(
-                tally_ref.at[part, pl.ds(spot * width, width)],
+                tally_ref.at[part, pl.ds(begin, size)],
                 tally_hbm.at[part],
                 out_sems.at[chunk, spot],
             )
             store.start()
             stores.append(store)
+            begin += size
     for load in loads[4:]:
         load.wait()
     grouped_ref[...] = jnp.dot(
@@ -218,24 +249,27 @@
     anywhere = pl.BlockSpec(memory_space=pltpu.HBM)
     vmem = pl.BlockSpec(memory_space=pltpu.VMEM)
     half = (slabs // 2, sensors // slabs, 2 * time_len)
-    tally = jax.ShapeDtypeStruct((sensors * combos, block_count // PARTS), jnp.bfloat16)
+    tallies = [
+        jax.ShapeDtypeStruct((sensors * combos, block_count * cuts // sum(SPANS)), jnp.bfloat16)
+        for cuts in SPANS
+    ]
     operands = (blocks, frames, classes, counts, pressure, kern_rows)
     *tallies, mine, other = pl.pallas_call(
         functools.partial(forward_kernel, kinds, places),
         in_specs=[pl.BlockSpec(memory_space=pltpu.SMEM)] + [anywhere] * 6,
-        out_specs=[anywhere] * PARTS + [vmem, vmem],
-        out_shape=[tally] * PARTS
+        out_specs=[anywhere] * len(SPANS) + [vmem, vmem],
+        out_shape=tallies
         + [
             jax.ShapeDtypeStruct(half, jnp.float32),
             jax.ShapeDtypeStruct(half, jnp.float32),
         ],
         scratch_shapes=[pltpu.VMEM(operand.shape, operand.dtype) for operand in operands]
         + [
-            pltpu.VMEM((tally.shape[0], block_count), tally.dtype),
+            pltpu.VMEM((sensors * combos, block_count), jnp.bfloat16),
             pltpu.VMEM((sensors // UNIT, UNIT * slots), jnp.int32),
             pltpu.VMEM((sensors * combos, pressure.shape[1]), jnp.float32),
             pltpu.SemaphoreType.DMA((len(operands),)),
-            pltpu.SemaphoreType.DMA((8, PARTS)),
+            pltpu.SemaphoreType.DMA((8, len(SPANS))),
         ],
         compiler_params=pltpu.CompilerParams(vmem_limit_bytes=48 << 20),
         name="forward",
@@ -288,25 +322,28 @@
         kernel_ref, resp_ref, kept_ref, *code_refs = refs[pieces + 1 : -5]
         tally_ref, grad_ref, sems, back_ref, wide_ref = refs[-5:]
     else:
-        resp_ref, kept_ref, *code_refs = refs[:-3]
-        tally_ref, grad_ref, sems = refs[-3:]
+        tally_ref = tally_hbm
+        resp_ref, kept_ref, *code_refs, grad_ref = refs
     groups, share, span = grad_ref.shape
-    cuts = sems.shape[0]
-    loads = []
-    for cut in range(cuts):
-        here = pl.ds(cut * (span // cuts), span // cuts)
-        loads.append(
-            pltpu.make_async_copy(tally_hbm.at[:, here], tally_ref.at[:, here], sems.at[cut])
-        )
-        loads[-1].start()
+    loads = [None]
+    if pieces:
+        cuts = sems.shape[0]
+        loads = []
+        for cut in range(cuts):
+            here = pl.ds(cut * (span // cuts), span // cuts)
+            loads.append(
+                pltpu.make_async_copy(tally_hbm.at[:, here], tally_ref.at[:, here], sems.at[cut])
+            )
+            loads[-1].start()
     if pieces:
         fill_responses(
             kinds, places, order_ref, piece_refs, kernel_ref, resp_ref, back_ref, wide_ref
         )
     width = groups * share
     for cut, load in enumerate(loads):
-        load.wait()
-        here = slice(cut * (span // cuts), (cut + 1) * (span // cuts))
+        if load is not None:
+            load.wait()
+        here = slice(cut * (span // len(loads)), (cut + 1) * (span // len(loads)))
         both = jnp.dot(resp_ref[...], tally_ref[:, here], preferred_element_type=jnp.float32)
         both = both[:width] + both[width:]
         for group in range(groups):
@@ -337,13 +374,15 @@
     out_shape = [jax.ShapeDtypeStruct((share, span), jnp.float32)] + [
         jax.ShapeDtypeStruct((share, span + 128), jnp.int16)
     ] * (groups - 1)
-    scratch = [
-        pltpu.VMEM((rows, span), tally.dtype),
-        pltpu.VMEM((groups, share, span), jnp.float32),
-        pltpu.SemaphoreType.DMA((4,)),
-    ]
+    scratch = [pltpu.VMEM((groups, share, span), jnp.float32)]
     if resp is None:
-        operands = (order, *pieces, kern_rows)
+        tally = in_hbm(tally)
+        scratch = [
+            pltpu.VMEM((rows, span), tally.dtype),
+            *scratch,
+            pltpu.SemaphoreType.DMA((span // CUT,)),
+        ]
+        operands = (order, *pieces, pltpu.with_memory_space_constraint(kern_rows, pltpu.VMEM))
         specs = [smem] + [vmem] * (len(pieces) + 1)
         out_shape = [jax.ShapeDtypeStruct((2 * width, rows), jnp.bfloat16)] + out_shape
         length = pieces[0].shape[1]
@@ -353,6 +392,7 @@
             pltpu.VMEM((rows, width), jnp.float32),
         ]
     else:
+        tally, hbm = pltpu.with_memory_space_constraint(tally, pltpu.VMEM), vmem
         operands, specs = (resp,), [vmem]
     outs = pl.pallas_call(
         functools.partial(backward_kernel, *(combos or (0, 0)), len(pieces)),
@@ -360,25 +400,27 @@
         out_specs=[vmem] * len(out_shape),
         out_shape=out_shape,
         scratch_shapes=scratch,
-        compiler_params=pltpu.CompilerParams(vmem_limit_bytes=32 << 20),
+        compiler_params=pltpu.CompilerParams(vmem_limit_bytes=24 << 20),
         cost_estimate=pl.CostEstimate(
-            flops=4 * width * rows * span, bytes_accessed=2 * rows * span, transcendentals=0
+            flops=4 * width * rows * span * 1, bytes_accessed=2 * rows * span, transcendentals=0
         ),
         name="backward",
-    )(own, in_hbm(tally), *operands)
+    )(own, tally, *operands)
     if resp is None:
         resp, *outs = outs
     kept, *codes = outs
     received = []
-    for step, code in enumerate(codes, 1):
-        received.append(lax.ppermute(code, "sens", [(q, q ^ step) for q in range(groups)]))
+    for step in range(groups - 1, 0, -1):
+        pairs = [(q, q ^ step) for q in range(groups)]
+        received.append(lax.ppermute(codes[step - 1], "sens", pairs))
     return resp, [kept, *received]
 
 
 def finish_kernel(*refs):
     part_refs, out_ref = refs[:-1], refs[-1]
-    count = len(part_refs) // PARTS
-    for part in range(PARTS):
+    count = len(part_refs) // len(SPANS)
+    begin = 0
+    for part in range(len(SPANS)):
         kept_ref, *code_refs = part_refs[part * count : (part + 1) * count]
         span = kept_ref.shape[1]
         for spot in range(span // GRAIN):
@@ -388,15 +430,14 @@
                 level = code_ref[:, span:].astype(jnp.int32).astype(jnp.float32)[:, spot : spot + 1]
                 scale = jnp.exp(level * (1.0 / RATE)) * (1.0 / CODE)
                 total = total + code_ref[:, cut].astype(jnp.int32).astype(jnp.float32) * scale
-            start = part * span + spot * GRAIN
-            out_ref[:, start : start + GRAIN] = total
-
-
-def finish(parts):
-    share, span = parts[0].shape
+            out_ref[:, begin : begin + GRAIN] = total
+            begin += GRAIN
+
+
+def finish(parts, block_count):
     return pl.pallas_call(
         finish_kernel,
-        out_shape=jax.ShapeDtypeStruct((share, PARTS * span), jnp.float32),
+        out_shape=jax.ShapeDtypeStruct((parts[0].shape[0], block_count), jnp.float32),
         compiler_params=pltpu.CompilerParams(vmem_limit_bytes=8 << 20),
         name="finish",
     )(*parts)
@@ -409,18 +450,51 @@
     chip = place // 2
     paired = mine + lax.ppermute(other, "slab", [(j, j ^ 1) for j in range(slabs)])
     paired, gains = lax.optimization_barrier((paired, gains))
-    total = lax.dynamic_index_in_dim(paired, chip, 0, keepdims=False)
+    received = [lax.dynamic_index_in_dim(paired, chip, 0, keepdims=False)]
     for step in (2, 1, 3) if chips == 4 else range(1, chips):
         block = lax.dynamic_index_in_dim(paired, chip ^ step, 0, keepdims=False)
-        total = total + lax.ppermute(block, "slab", [(j, j ^ (2 * step)) for j in range(slabs)])
-    return total, gains
+        received.append(
+            lax.ppermute(block, "slab", [(j, j ^ (2 * step)) for j in range(slabs)])
+        )
+    return received, gains
+
+
+def refine_kernel(*refs):
+    *piece_refs, matrix_ref, measured_ref, residual_ref, back_ref = refs
+    total = piece_refs[0][...]
+    for piece_ref in piece_refs[1:]:
+        total = total + piece_ref[...]
+    share, length = total.shape
+    half = length // 2
+    rows = jnp.concatenate([total[:, :half], total[:, half:]], axis=0)
+    dot = functools.partial(
+        jnp.dot, precision=lax.Precision.HIGHEST, preferred_element_type=jnp.float32
+    )
+    residual = dot(rows, matrix_ref[...]) - measured_ref[...]
+    residual_ref[...] = residual
+    back = dot(residual, matrix_ref[...]).astype(jnp.bfloat16)
+    back_ref[:, :half] = back[:share]
+    back_ref[:, half:] = back[share:]
+
+
+def refine(received, matrix, measured):
+    share, length = received[0].shape
+    return pl.pallas_call(
+        refine_kernel,
+        out_shape=[
+            jax.ShapeDtypeStruct(measured.shape, jnp.float32),
+            jax.ShapeDtypeStruct((share, length), jnp.bfloat16),
+        ],
+        compiler_params=pltpu.CompilerParams(vmem_limit_bytes=12 << 20),
+        name="refine",
+    )(*[pltpu.with_memory_space_constraint(piece, pltpu.VMEM) for piece in received], matrix, measured)
 
 
 def gather_slab(share):
     slabs = lax.axis_size("slab")
     place = lax.axis_index("slab")
     pieces, order = [share], [place]
-    for step in range(1, slabs // 2):
+    for step in range(slabs // 2 - 1, 0, -1):
         pieces.append(lax.ppermute(share, "slab", [(j, j ^ (2 * step)) for j in range(slabs)]))
         order.append(place ^ (2 * step))
     for spot in range(slabs // 2):
@@ -452,25 +526,20 @@
         places,
         time_len,
     )
-    traces, gains = scatter_slab(mine, other, filter_gains)
-    traces = traces.reshape(share * 2, time_len)
-    matrix = filter_matrix(gains)
+    received, gains = scatter_slab(mine, other, filter_gains)
+    matrix, kern_fast = filter_matrix(gains, kern_rows)
     measured_share = lax.dynamic_slice_in_dim(measured, lax.axis_index("slab") * share, share, 0)
-    dot = functools.partial(
-        jnp.dot, precision=lax.Precision.HIGHEST, preferred_element_type=jnp.float32
-    )
-    residual = dot(traces, matrix) - measured_share.reshape(share * 2, time_len)
-    back = dot(residual, matrix).astype(jnp.bfloat16)
-    back = back.reshape(share, 2 * time_len)
+    measured_share = measured_share.transpose(1, 0, 2).reshape(2 * share, time_len)
+    residual, back = refine(received, matrix, measured_share)
+    residual = residual.reshape(2, share, time_len).transpose(1, 0, 2)
     pieces, order = gather_slab(back)
     own = lax.axis_index("sens").reshape(1)
     resp, parts = backward(
-        own, tallies[0], width, None, order, pieces, kern_rows, (kinds, places)
-    )
-    for tally in tallies[1:]:
-        parts = parts + backward(own, tally, width, resp)[1]
-    gradient = finish(parts).T
-    return (residual.reshape(share, 2, time_len), gradient)
+        own, tallies[0], width, None, order, pieces, kern_fast, (kinds, places)
+    )
+    parts = parts + backward(own, tallies[1], width, resp)[1]
+    gradient = finish(parts, block_count).T
+    return (residual, gradient)
 
 
 def solution(mesh):

time: 77.8 us -> 73.9 us (0.950)
  local copies, waits for them, and re-layouts: 3.81 us -> 0.94 us
  matrix products: 1.51 us -> 0 us
    unnamed x8 -> x4, local copies, waits for them, and re-layouts: 2.81 us -> 0.01 us
    pallas_call x2 -> x3, Pallas kernels: 1.85 us -> 4.49 us  [the longest x1 1.99 us: filter_matrix(): pl.pallas_call(filter_kernel, in_specs=[pl.BlockSpec(memory_space=pltpu.H...]
    ppermute x3, waiting for transfers between devices: 6.46 us -> 8.69 us  [scatter_slab(): lax.ppermute(block, 'slab', [(j, j ^ 2 * step) for j in range(slabs)])]
    dot_general x2 -> x0, matrix products: 1.51 us -> none  [the longest x1 0.76 us: per_device(): back = dot(residual, matrix).astype(jnp.bfloat16)]
    pallas_call x2, Pallas kernels: 13.4 us -> 12.1 us  [backward(): pl.pallas_call(functools.partial(backward_kernel, *(combos or (0, 0)), le...]
    pallas_call x1, Pallas kernels: 18.2 us -> 17 us  [forward(): pl.pallas_call(functools.partial(forward_kernel, kinds, places), in_specs...]
    ppermute x3, waiting for transfers between devices: 5.23 us -> 4.2 us  [gather_slab(): lax.ppermute(share, 'slab', [(j, j ^ 2 * step) for j in range(slabs)])]
    ppermute x6, waiting for transfers between devices: 5.32 us -> 4.53 us  [backward(): received.append(lax.ppermute(codes[step - 1], 'sens', pairs))]
  transfers between devices with their start and end apart: 17 -> 17, of which waited for: 9 -> 10; matrix products, arithmetic and copies ran while one was open for 1% -> 1% of each run, Pallas kernels for 9% -> 8%
where the time goes in v3:
time: 73.9 us; the launch traced here: 73.7 us
  Pallas kernels  33.6 us (45%)
  waiting for transfers between devices  20.1 us (27%)
  starting transfers between devices  18.3 us (25%)
  local copies, waits for them, and re-layouts  0.94 us (1%)
  between operations  0.76 us (1%)
    pallas_call x1, Pallas kernels, forward(): pl.pallas_call(functools.partial(forward_kernel, kinds, places), in_specs...  17 us
    pallas_call x2, Pallas kernels, backward(): pl.pallas_call(functools.partial(backward_kernel, *(combos or (0, 0)), le...  12.1 us
    ppermute x3, waiting for transfers between devices, scatter_slab(): lax.ppermute(block, 'slab', [(j, j ^ 2 * step) for j in range(slabs)])  8.69 us
    ppermute x6, starting transfers between devices, backward(): received.append(lax.ppermute(codes[step - 1], 'sens', pairs))  7.11 us
    ppermute x3, starting transfers between devices, scatter_slab(): lax.ppermute(block, 'slab', [(j, j ^ 2 * step) for j in range(slabs)])  5.67 us
    ppermute x6, waiting for transfers between devices, backward(): received.append(lax.ppermute(codes[step - 1], 'sens', pairs))  4.53 us
    ppermute x3, starting transfers between devices, gather_slab(): lax.ppermute(share, 'slab', [(j, j ^ 2 * step) for j in range(slabs)])  4.44 us
    ppermute x3, waiting for transfers between devices, gather_slab(): lax.ppermute(share, 'slab', [(j, j ^ 2 * step) for j in range(slabs)])  4.2 us
  transfers between devices with their start and end apart: 17, of which 10 were waited for; matrix products, arithmetic and copies ran while one was open for 1% of the time, Pallas kernels for 8%

profile of v3, /device:TPU:0, one launch (start us, length us, event | category | flops | bytes accessed | tf_op | source)
XLA Modules:
  0.0 73.7 jit_solution(17255135322964872813)
XLA Ops:
  0.6 0.0 copy-start
  0.7 17.0 %forward.1 = (bf16[3072,2048]{1,0:T(8,128)(2,1)}, bf16[3072,2048]{1,0:T(8,128)(2,1)}, f32[4,32,1024]{2,1,0:T(8,128)S(1)}, f32[4,32,1024]{2,1,0:T(8,128)S(1)}) custom-call(s32[1]{0:T(128)} %bitcast.core_ref, s32[64,256]{1,0:T(8,128)} %bitcast.44, s32[64,256]{1,0:T(8,128)} %bitcast.45, s32[64,256]{1,0:T(8,128)} %bitcast.46, s32[1,256]{1,0:T(1,128)} %bitcast.48, ...), custom_call_target="tpu_custom_call" | custom-call | tf_op jit(solution)/shard_map/forward/pallas_call | solution.py:257
  17.6 0.5 collective-permute-start
  18.1 1.5 %collective-permute-done = f32[4,32,1024]{2,1,0:T(8,128)S(1)} collective-permute-done((f32[4,32,1024]{2,1,0:T(8,128)S(1)}, f32[4,32,1024]{2,1,0:T(8,128)S(1)}, u32[]{:S(2)}, u32[]{:S(2)}) %collective-permute-start) | collective-permute-done | bytes 524320 | tf_op jit(solution)/shard_map/ppermute | solution.py:451
  19.7 0.1 add.25
  19.8 5.0 %collective-permute-start.3 = (f32[32,1024]{1,0:T(8,128)S(1)}, f32[32,1024]{1,0:T(8,128)S(1)}, u32[]{:S(2)}, u32[]{:S(2)}) collective-permute-start(f32[32,1024]{1,0:T(8,128)S(1)} %get-tuple-element.40), channel_id=1, source_target_pairs={{0,6},{1,7},{2,4},{3,5},{4,2},{5,3},{6,0},{7,1},{8,14},{9,15},{10,... | collective-permute-start | bytes 393224 | tf_op jit(solution)/shard_map/ppermute | solution.py:457
  24.8 0.0 collective-permute-start.2
  24.8 0.6 collective-permute-start.1
  25.5 0.0 copy-done
  25.5 2.0 %filter_matrix.1 = (f32[512,512]{1,0:T(8,128)S(1)}, bf16[256,256]{1,0:T(8,128)(2,1)S(1)}) custom-call(f32[1,512]{1,0:T(1,128)} %bitcast.47, f32[512,512]{1,0:T(8,128)} %constant.56.clone.cosine_hbm, bf16[256,256]{1,0:T(8,128)(2,1)} %bitcast.42), custom_call_target="tpu_custom_call" | custom-call | tf_op jit(solution)/shard_map/filter_matrix/pallas_call | solution.py:60
  27.5 1.6 %collective-permute-done.3.refs_3_ = f32[32,1024]{1,0:T(8,128)S(1)} collective-permute-done((f32[32,1024]{1,0:T(8,128)S(1)}, f32[32,1024]{1,0:T(8,128)S(1)}, u32[]{:S(2)}, u32[]{:S(2)}) %collective-permute-start.3) | collective-permute-done | bytes 131104 | tf_op jit(solution)/shard_map/ppermute | solution.py:457
  29.2 3.4 %collective-permute-done.2.refs_2_ = f32[32,1024]{1,0:T(8,128)S(1)} collective-permute-done((f32[32,1024]{1,0:T(8,128)S(1)}, f32[32,1024]{1,0:T(8,128)S(1)}, u32[]{:S(2)}, u32[]{:S(2)}) %collective-permute-start.2) | collective-permute-done | bytes 131104 | tf_op jit(solution)/shard_map/ppermute | solution.py:457
  32.5 3.7 %collective-permute-done.1.refs_1_ = f32[32,1024]{1,0:T(8,128)S(1)} collective-permute-done((f32[32,1024]{1,0:T(8,128)S(1)}, f32[32,1024]{1,0:T(8,128)S(1)}, u32[]{:S(2)}, u32[]{:S(2)}) %collective-permute-start.1) | collective-permute-done | bytes 131104 | tf_op jit(solution)/shard_map/ppermute | solution.py:457
  36.2 1.4 %refine.1 = (f32[64,512]{1,0:T(8,128)S(1)}, bf16[32,1024]{1,0:T(8,128)(2,1)S(1)}) custom-call(f32[32,1024]{1,0:T(8,128)S(1)} %get-tuple-element.43.refs_0_, f32[32,1024]{1,0:T(8,128)S(1)} %collective-permute-done.1.refs_1_, f32[32,1024]{1,0:T(8,128)S(1)} %collective-permute-done.2.refs_2_, f32[32,1024]{1,0:T(8,128)S(1)} %collective-permute-done.3.refs_3_, ...), custom_call_target="tpu_custom_call" | custom-call | tf_op jit(solution)/shard_map/refine/pallas_call | solution.py:482
  37.6 0.1 collective-permute-start.6
  37.7 3.0 %collective-permute-start.5 = (bf16[32,1024]{1,0:T(8,128)(2,1)S(1)}, bf16[32,1024]{1,0:T(8,128)(2,1)S(1)}, u32[]{:S(2)}, u32[]{:S(2)}) collective-permute-start(bf16[32,1024]{1,0:T(8,128)(2,1)S(1)} %get-tuple-element.28.refs_1_), channel_id=1, source_target_pairs={{0,4},{1,5},{2,6},{3,7},{4,0},{5,1},{6,2},{7,3},{8,12},{9,13},{10,... | collective-permute-start | bytes 196616 | tf_op jit(solution)/shard_map/ppermute | solution.py:498
  40.7 1.3 %collective-permute-start.4 = (bf16[32,1024]{1,0:T(8,128)(2,1)S(1)}, bf16[32,1024]{1,0:T(8,128)(2,1)S(1)}, u32[]{:S(2)}, u32[]{:S(2)}) collective-permute-start(bf16[32,1024]{1,0:T(8,128)(2,1)S(1)} %get-tuple-element.28.refs_1_), channel_id=1, source_target_pairs={{0,6},{1,7},{2,4},{3,5},{4,2},{5,3},{6,0},{7,1},{8,14},{9,15},{10,... | collective-permute-start | bytes 196616 | tf_op jit(solution)/shard_map/ppermute | solution.py:498
  42.0 0.0 collective-permute-start.7
  42.0 0.0 collective-permute-done.6.refs_4_
  42.0 0.5 collective-permute-start.10
  42.6 2.2 %collective-permute-done.5.refs_3_ = bf16[32,1024]{1,0:T(8,128)(2,1)S(1)} collective-permute-done((bf16[32,1024]{1,0:T(8,128)(2,1)S(1)}, bf16[32,1024]{1,0:T(8,128)(2,1)S(1)}, u32[]{:S(2)}, u32[]{:S(2)}) %collective-permute-start.5) | collective-permute-done | bytes 65568 | tf_op jit(solution)/shard_map/ppermute | solution.py:498
  44.7 0.0 collective-permute-start.9
  44.7 2.0 %collective-permute-done.4.refs_2_ = bf16[32,1024]{1,0:T(8,128)(2,1)S(1)} collective-permute-done((bf16[32,1024]{1,0:T(8,128)(2,1)S(1)}, bf16[32,1024]{1,0:T(8,128)(2,1)S(1)}, u32[]{:S(2)}, u32[]{:S(2)}) %collective-permute-start.4) | collective-permute-done | bytes 65568 | tf_op jit(solution)/shard_map/ppermute | solution.py:498
  46.8 0.0 collective-permute-start.8
  46.8 0.1 stack.35.refs_0_
  46.8 0.0 copy-start.1
  46.8 0.0 collective-permute-done.7.refs_5_
  46.8 0.0 collective-permute-done.10.refs_8_
  46.9 0.0 collective-permute-done.9.refs_7_
  46.9 1.1 %collective-permute-done.8.refs_6_ = bf16[32,1024]{1,0:T(8,128)(2,1)S(1)} collective-permute-done((bf16[32,1024]{1,0:T(8,128)(2,1)S(1)}, bf16[32,1024]{1,0:T(8,128)(2,1)S(1)}, u32[]{:S(2)}, u32[]{:S(2)}) %collective-permute-start.8) | collective-permute-done | bytes 65568 | tf_op jit(solution)/shard_map/ppermute | solution.py:501
  48.0 8.2 %backward.2 = (bf16[256,3072]{1,0:T(8,128)(2,1)S(1)}, f32[32,2048]{1,0:T(8,128)S(1)}, s16[32,2176]{1,0:T(8,128)(2,1)S(1)}, s16[32,2176]{1,0:T(8,128)(2,1)S(1)}, s16[32,2176]{1,0:T(8,128)(2,1)S(1)}) custom-call(s32[1]{0:T(128)} %bitcast.18.own_ref, bf16[3072,2048]{1,0:T(8,128)(2,1)} %get-tuple-element.27.tally_hbm, s32[8]{0:T(128)S(1)} %stack.35.refs_0_, ...), custom_call_target="tpu_custom_call" | custom-call | flops 3221225472 | bytes 12582912 | tf_op jit(solution)/shard_map/backward/pallas_call | solution.py:397
  56.2 2.5 %collective-permute-start.11 = (s16[32,2176]{1,0:T(8,128)(2,1)S(1)}, s16[32,2176]{1,0:T(8,128)(2,1)S(1)}, u32[]{:S(2)}, u32[]{:S(2)}) collective-permute-start(s16[32,2176]{1,0:T(8,128)(2,1)S(1)} %get-tuple-element.31), channel_id=1, source_target_pairs={{0,24},{8,16},{16,8},{24,0},{1,25},{9,17},{17,9},{25,1},{2,26},{10... | collective-permute-start | bytes 417800 | tf_op jit(solution)/shard_map/ppermute | solution.py:415
  58.8 0.5 collective-permute-start.12
  59.3 0.5 collective-permute-start.13
  59.8 0.0 copy-done.1
  59.8 3.9 %backward.3 = (f32[32,2048]{1,0:T(8,128)S(1)}, s16[32,2176]{1,0:T(8,128)(2,1)S(1)}, s16[32,2176]{1,0:T(8,128)(2,1)S(1)}, s16[32,2176]{1,0:T(8,128)(2,1)S(1)}) custom-call(s32[1]{0:T(128)} %bitcast.18.own_ref, bf16[3072,2048]{1,0:T(8,128)(2,1)S(1)} %copy-done.1, bf16[256,3072]{1,0:T(8,128)(2,1)S(1)} %get-tuple-element.35.refs_0_), custom_call_target="tpu_custom_call" | custom-call | flops 3221225472 | bytes 12582912 | tf_op jit(solution)/shard_map/backward/pallas_call | solution.py:397
  63.7 2.5 %collective-permute-start.14 = (s16[32,2176]{1,0:T(8,128)(2,1)S(1)}, s16[32,2176]{1,0:T(8,128)(2,1)S(1)}, u32[]{:S(2)}, u32[]{:S(2)}) collective-permute-start(s16[32,2176]{1,0:T(8,128)(2,1)S(1)} %get-tuple-element.37), channel_id=1, source_target_pairs={{0,24},{8,16},{16,8},{24,0},{1,25},{9,17},{17,9},{25,1},{2,26},{10... | collective-permute-start | bytes 417800 | tf_op jit(solution)/shard_map/ppermute | solution.py:415
  66.2 0.5 collective-permute-start.15
  66.7 0.0 collective-permute-done.11.refs_1_
  66.8 0.5 collective-permute-start.16
  67.3 0.8 %copy.14 = f32[2,32,512]{2,0,1:T(2,128)} copy(f32[2,32,512]{2,1,0:T(8,128)S(1)} %bitcast.39) | data formatting | bytes 262144 | tf_op jit(solution)/shard_map/reshape | solution.py:534
  68.0 0.0 collective-permute-done.12.refs_2_
  68.0 0.0 collective-permute-done.13.refs_3_
  68.0 2.5 %collective-permute-done.14.refs_5_ = s16[32,2176]{1,0:T(8,128)(2,1)S(1)} collective-permute-done((s16[32,2176]{1,0:T(8,128)(2,1)S(1)}, s16[32,2176]{1,0:T(8,128)(2,1)S(1)}, u32[]{:S(2)}, u32[]{:S(2)}) %collective-permute-start.14) | collective-permute-done | bytes 139296 | tf_op jit(solution)/shard_map/ppermute | solution.py:415
  70.5 2.0 %collective-permute-done.15.refs_6_ = s16[32,2176]{1,0:T(8,128)(2,1)S(1)} collective-permute-done((s16[32,2176]{1,0:T(8,128)(2,1)S(1)}, s16[32,2176]{1,0:T(8,128)(2,1)S(1)}, u32[]{:S(2)}, u32[]{:S(2)}) %collective-permute-start.15) | collective-permute-done | bytes 139296 | tf_op jit(solution)/shard_map/ppermute | solution.py:415
  72.5 0.1 collective-permute-done.16.refs_7_
  72.6 1.1 %finish.1 = f32[32,4096]{1,0:T(8,128)} custom-call(f32[32,2048]{1,0:T(8,128)S(1)} %get-tuple-element.30.refs_0_, s16[32,2176]{1,0:T(8,128)(2,1)S(1)} %collective-permute-done.11.refs_1_, s16[32,2176]{1,0:T(8,128)(2,1)S(1)} %collective-permute-done.12.refs_2_, s16[32,2176]{1,0:T(8,128)(2,1)S(1)} %collective-permute-done.13.refs_3_, ...), custom_call_target="tpu_custom_call" | custom-call | tf_op jit(solution)/shard_map/finish/pallas_call | solution.py:438
  (3 shorter events, 0.1 us)
Async XLA Ops:
  0.6 24.8 %copy-start = (f32[256,2,512]{2,1,0:T(2,128)S(1)}, f32[256,2,512]{2,1,0:T(2,128)}, u32[]{:S(2)}) copy-start(f32[256,2,512]{2,1,0:T(2,128)} %param.12) | copy-start | bytes 3145732
  17.6 2.1 %collective-permute-start = (f32[4,32,1024]{2,1,0:T(8,128)S(1)}, f32[4,32,1024]{2,1,0:T(8,128)S(1)}, u32[]{:S(2)}, u32[]{:S(2)}) collective-permute-start(f32[4,32,1024]{2,1,0:T(8,128)S(1)} %get-tuple-element.22), channel_id=1, source_target_pairs={{0,1},{1,0},{2,3},{3,2},{4,5},{5,4},{6,7},{7,6},{8,9},{9,8},{10,11... | collective-permute-start | bytes 1572872 | tf_op jit(solution)/shard_map/ppermute | solution.py:451
  19.8 9.4 %collective-permute-start.3 = (f32[32,1024]{1,0:T(8,128)S(1)}, f32[32,1024]{1,0:T(8,128)S(1)}, u32[]{:S(2)}, u32[]{:S(2)}) collective-permute-start(f32[32,1024]{1,0:T(8,128)S(1)} %get-tuple-element.40), channel_id=1, source_target_pairs={{0,6},{1,7},{2,4},{3,5},{4,2},{5,3},{6,0},{7,1},{8,14},{9,15},{10,... | collective-permute-start | bytes 393224 | tf_op jit(solution)/shard_map/ppermute | solution.py:457
  24.8 7.7 %collective-permute-start.2 = (f32[32,1024]{1,0:T(8,128)S(1)}, f32[32,1024]{1,0:T(8,128)S(1)}, u32[]{:S(2)}, u32[]{:S(2)}) collective-permute-start(f32[32,1024]{1,0:T(8,128)S(1)} %get-tuple-element.41), channel_id=1, source_target_pairs={{0,2},{1,3},{2,0},{3,1},{4,6},{5,7},{6,4},{7,5},{8,10},{9,11},{10,... | collective-permute-start | bytes 393224 | tf_op jit(solution)/shard_map/ppermute | solution.py:457
  24.8 11.4 %collective-permute-start.1 = (f32[32,1024]{1,0:T(8,128)S(1)}, f32[32,1024]{1,0:T(8,128)S(1)}, u32[]{:S(2)}, u32[]{:S(2)}) collective-permute-start(f32[32,1024]{1,0:T(8,128)S(1)} %get-tuple-element.42), channel_id=1, source_target_pairs={{0,4},{1,5},{2,6},{3,7},{4,0},{5,1},{6,2},{7,3},{8,12},{9,13},{10,... | collective-permute-start | bytes 393224 | tf_op jit(solution)/shard_map/ppermute | solution.py:457
  37.6 4.5 %collective-permute-start.6 = (bf16[32,1024]{1,0:T(8,128)(2,1)S(1)}, bf16[32,1024]{1,0:T(8,128)(2,1)S(1)}, u32[]{:S(2)}, u32[]{:S(2)}) collective-permute-start(bf16[32,1024]{1,0:T(8,128)(2,1)S(1)} %get-tuple-element.28.refs_1_), channel_id=1, source_target_pairs={{0,2},{1,3},{2,0},{3,1},{4,6},{5,7},{6,4},{7,5},{8,10},{9,11},{10,... | collective-permute-start | bytes 196616 | tf_op jit(solution)/shard_map/ppermute | solution.py:498
  37.7 7.1 %collective-permute-start.5 = (bf16[32,1024]{1,0:T(8,128)(2,1)S(1)}, bf16[32,1024]{1,0:T(8,128)(2,1)S(1)}, u32[]{:S(2)}, u32[]{:S(2)}) collective-permute-start(bf16[32,1024]{1,0:T(8,128)(2,1)S(1)} %get-tuple-element.28.refs_1_), channel_id=1, source_target_pairs={{0,4},{1,5},{2,6},{3,7},{4,0},{5,1},{6,2},{7,3},{8,12},{9,13},{10,... | collective-permute-start | bytes 196616 | tf_op jit(solution)/shard_map/ppermute | solution.py:498
  40.7 6.1 %collective-permute-start.4 = (bf16[32,1024]{1,0:T(8,128)(2,1)S(1)}, bf16[32,1024]{1,0:T(8,128)(2,1)S(1)}, u32[]{:S(2)}, u32[]{:S(2)}) collective-permute-start(bf16[32,1024]{1,0:T(8,128)(2,1)S(1)} %get-tuple-element.28.refs_1_), channel_id=1, source_target_pairs={{0,6},{1,7},{2,4},{3,5},{4,2},{5,3},{6,0},{7,1},{8,14},{9,15},{10,... | collective-permute-start | bytes 196616 | tf_op jit(solution)/shard_map/ppermute | solution.py:498
  42.0 4.8 %collective-permute-start.7 = (bf16[32,1024]{1,0:T(8,128)(2,1)S(1)}, bf16[32,1024]{1,0:T(8,128)(2,1)S(1)}, u32[]{:S(2)}, u32[]{:S(2)}) collective-permute-start(bf16[32,1024]{1,0:T(8,128)(2,1)S(1)} %get-tuple-element.28.refs_1_), channel_id=1, source_target_pairs={{0,1},{1,0},{2,3},{3,2},{4,5},{5,4},{6,7},{7,6},{8,9},{9,8},{10,11... | collective-permute-start | bytes 196616 | tf_op jit(solution)/shard_map/ppermute | solution.py:501
  42.0 4.8 %collective-permute-start.10 = (bf16[32,1024]{1,0:T(8,128)(2,1)S(1)}, bf16[32,1024]{1,0:T(8,128)(2,1)S(1)}, u32[]{:S(2)}, u32[]{:S(2)}) collective-permute-start(bf16[32,1024]{1,0:T(8,128)(2,1)S(1)} %collective-permute-done.6.refs_4_), channel_id=1, source_target_pairs={{0,1},{1,0},{2,3},{3,2},{4,5},{5,4},{6,7},{7,6},{8,9},{9,8},{10,11... | collective-permute-start | bytes 196616 | tf_op jit(solution)/shard_map/ppermute | solution.py:501
  44.7 2.1 %collective-permute-start.9 = (bf16[32,1024]{1,0:T(8,128)(2,1)S(1)}, bf16[32,1024]{1,0:T(8,128)(2,1)S(1)}, u32[]{:S(2)}, u32[]{:S(2)}) collective-permute-start(bf16[32,1024]{1,0:T(8,128)(2,1)S(1)} %collective-permute-done.5.refs_3_), channel_id=1, source_target_pairs={{0,1},{1,0},{2,3},{3,2},{4,5},{5,4},{6,7},{7,6},{8,9},{9,8},{10,11... | collective-permute-start | bytes 196616 | tf_op jit(solution)/shard_map/ppermute | solution.py:501
  46.8 1.3 %collective-permute-start.8 = (bf16[32,1024]{1,0:T(8,128)(2,1)S(1)}, bf16[32,1024]{1,0:T(8,128)(2,1)S(1)}, u32[]{:S(2)}, u32[]{:S(2)}) collective-permute-start(bf16[32,1024]{1,0:T(8,128)(2,1)S(1)} %collective-permute-done.4.refs_2_), channel_id=1, source_target_pairs={{0,1},{1,0},{2,3},{3,2},{4,5},{5,4},{6,7},{7,6},{8,9},{9,8},{10,11... | collective-permute-start | bytes 196616 | tf_op jit(solution)/shard_map/ppermute | solution.py:501
  46.8 13.0 %copy-start.1 = (bf16[3072,2048]{1,0:T(8,128)(2,1)S(1)}, bf16[3072,2048]{1,0:T(8,128)(2,1)}, u32[]{:S(2)}) copy-start(bf16[3072,2048]{1,0:T(8,128)(2,1)} %get-tuple-element.34.tally_hbm) | copy-start | bytes 37748740
  56.2 10.5 %collective-permute-start.11 = (s16[32,2176]{1,0:T(8,128)(2,1)S(1)}, s16[32,2176]{1,0:T(8,128)(2,1)S(1)}, u32[]{:S(2)}, u32[]{:S(2)}) collective-permute-start(s16[32,2176]{1,0:T(8,128)(2,1)S(1)} %get-tuple-element.31), channel_id=1, source_target_pairs={{0,24},{8,16},{16,8},{24,0},{1,25},{9,17},{17,9},{25,1},{2,26},{10... | collective-permute-start | bytes 417800 | tf_op jit(solution)/shard_map/ppermute | solution.py:415
  58.8 9.3 %collective-permute-start.12 = (s16[32,2176]{1,0:T(8,128)(2,1)S(1)}, s16[32,2176]{1,0:T(8,128)(2,1)S(1)}, u32[]{:S(2)}, u32[]{:S(2)}) collective-permute-start(s16[32,2176]{1,0:T(8,128)(2,1)S(1)} %get-tuple-element.32), channel_id=1, source_target_pairs={{0,16},{8,24},{16,0},{24,8},{1,17},{9,25},{17,1},{25,9},{2,18},{10... | collective-permute-start | bytes 417800 | tf_op jit(solution)/shard_map/ppermute | solution.py:415
  59.3 8.8 %collective-permute-start.13 = (s16[32,2176]{1,0:T(8,128)(2,1)S(1)}, s16[32,2176]{1,0:T(8,128)(2,1)S(1)}, u32[]{:S(2)}, u32[]{:S(2)}) collective-permute-start(s16[32,2176]{1,0:T(8,128)(2,1)S(1)} %get-tuple-element.33), channel_id=1, source_target_pairs={{0,8},{8,0},{16,24},{24,16},{1,9},{9,1},{17,25},{25,17},{2,10},{10... | collective-permute-start | bytes 417800 | tf_op jit(solution)/shard_map/ppermute | solution.py:415
  63.7 6.8 %collective-permute-start.14 = (s16[32,2176]{1,0:T(8,128)(2,1)S(1)}, s16[32,2176]{1,0:T(8,128)(2,1)S(1)}, u32[]{:S(2)}, u32[]{:S(2)}) collective-permute-start(s16[32,2176]{1,0:T(8,128)(2,1)S(1)} %get-tuple-element.37), channel_id=1, source_target_pairs={{0,24},{8,16},{16,8},{24,0},{1,25},{9,17},{17,9},{25,1},{2,26},{10... | collective-permute-start | bytes 417800 | tf_op jit(solution)/shard_map/ppermute | solution.py:415
  66.2 6.3 %collective-permute-start.15 = (s16[32,2176]{1,0:T(8,128)(2,1)S(1)}, s16[32,2176]{1,0:T(8,128)(2,1)S(1)}, u32[]{:S(2)}, u32[]{:S(2)}) collective-permute-start(s16[32,2176]{1,0:T(8,128)(2,1)S(1)} %get-tuple-element.38), channel_id=1, source_target_pairs={{0,16},{8,24},{16,0},{24,8},{1,17},{9,25},{17,1},{25,9},{2,18},{10... | collective-permute-start | bytes 417800 | tf_op jit(solution)/shard_map/ppermute | solution.py:415
  66.8 5.8 %collective-permute-start.16 = (s16[32,2176]{1,0:T(8,128)(2,1)S(1)}, s16[32,2176]{1,0:T(8,128)(2,1)S(1)}, u32[]{:S(2)}, u32[]{:S(2)}) collective-permute-start(s16[32,2176]{1,0:T(8,128)(2,1)S(1)} %get-tuple-element.39), channel_id=1, source_target_pairs={{0,8},{8,0},{16,24},{24,16},{1,9},{9,1},{17,25},{25,17},{2,10},{10... | collective-permute-start | bytes 417800 | tf_op jit(solution)/shard_map/ppermute | solution.py:415

commit v4 on v3

--- a/solution.py
+++ b/solution.py
@@ -183,7 +183,7 @@
     span = units // chunks
     stores = []
     for chunk in range(chunks):
-        lax.fori_loop(chunk * span, (chunk + 1) * span, unit_step, 0, unroll=4)
+        lax.fori_loop(chunk * span, (chunk + 1) * span, unit_step, 0, unroll=8)
         part = pl.ds(chunk * span * rows, span * rows)
         begin = 0
         for spot, tally_hbm in enumerate(tally_hbms):
@@ -269,7 +269,7 @@
             pltpu.VMEM((sensors // UNIT, UNIT * slots), jnp.int32),
             pltpu.VMEM((sensors * combos, pressure.shape[1]), jnp.float32),
             pltpu.SemaphoreType.DMA((len(operands),)),
-            pltpu.SemaphoreType.DMA((8, len(SPANS))),
+            pltpu.SemaphoreType.DMA((4, len(SPANS))),
         ],
         compiler_params=pltpu.CompilerParams(vmem_limit_bytes=48 << 20),
         name="forward",

time: 73.9 us -> 72.6 us (0.982)
  Pallas kernels: 33.6 us -> 32.4 us
    pallas_call x1, Pallas kernels: 17 us -> 15.7 us  [forward(): pl.pallas_call(functools.partial(forward_kernel, kinds, places), in_specs...]
where the time goes in v4:
time: 72.6 us; the launch traced here: 72.5 us
  Pallas kernels  32.4 us (45%)
  waiting for transfers between devices  20.1 us (28%)
  starting transfers between devices  18.3 us (25%)
  local copies, waits for them, and re-layouts  0.94 us (1%)
  between operations  0.76 us (1%)
    pallas_call x1, Pallas kernels, forward(): pl.pallas_call(functools.partial(forward_kernel, kinds, places), in_specs...  15.7 us
    pallas_call x2, Pallas kernels, backward(): pl.pallas_call(functools.partial(backward_kernel, *(combos or (0, 0)), le...  12.1 us
    ppermute x3, waiting for transfers between devices, scatter_slab(): lax.ppermute(block, 'slab', [(j, j ^ 2 * step) for j in range(slabs)])  8.69 us
    ppermute x6, starting transfers between devices, backward(): received.append(lax.ppermute(codes[step - 1], 'sens', pairs))  7.11 us
    ppermute x3, starting transfers between devices, scatter_slab(): lax.ppermute(block, 'slab', [(j, j ^ 2 * step) for j in range(slabs)])  5.67 us
    ppermute x6, waiting for transfers between devices, backward(): received.append(lax.ppermute(codes[step - 1], 'sens', pairs))  4.52 us
    ppermute x3, starting transfers between devices, gather_slab(): lax.ppermute(share, 'slab', [(j, j ^ 2 * step) for j in range(slabs)])  4.44 us
    ppermute x3, waiting for transfers between devices, gather_slab(): lax.ppermute(share, 'slab', [(j, j ^ 2 * step) for j in range(slabs)])  4.2 us
  transfers between devices with their start and end apart: 17, of which 10 were waited for; matrix products, arithmetic and copies ran while one was open for 1% of the time, Pallas kernels for 8%

profile of v4, /device:TPU:0, one launch (start us, length us, event | category | flops | bytes accessed | tf_op | source)
XLA Modules:
  0.0 72.5 jit_solution(17878377878653470110)
XLA Ops:
  0.6 0.0 copy-start
  0.7 15.7 %forward.1 = (bf16[3072,2048]{1,0:T(8,128)(2,1)}, bf16[3072,2048]{1,0:T(8,128)(2,1)}, f32[4,32,1024]{2,1,0:T(8,128)S(1)}, f32[4,32,1024]{2,1,0:T(8,128)S(1)}) custom-call(s32[1]{0:T(128)} %bitcast.core_ref, s32[64,256]{1,0:T(8,128)} %bitcast.44, s32[64,256]{1,0:T(8,128)} %bitcast.45, s32[64,256]{1,0:T(8,128)} %bitcast.46, s32[1,256]{1,0:T(1,128)} %bitcast.48, ...), custom_call_target="tpu_custom_call" | custom-call | tf_op jit(solution)/shard_map/forward/pallas_call | solution.py:257
  16.4 0.5 collective-permute-start
  16.9 1.5 %collective-permute-done = f32[4,32,1024]{2,1,0:T(8,128)S(1)} collective-permute-done((f32[4,32,1024]{2,1,0:T(8,128)S(1)}, f32[4,32,1024]{2,1,0:T(8,128)S(1)}, u32[]{:S(2)}, u32[]{:S(2)}) %collective-permute-start) | collective-permute-done | bytes 524320 | tf_op jit(solution)/shard_map/ppermute | solution.py:451
  18.5 0.1 add.25
  18.6 5.0 %collective-permute-start.3 = (f32[32,1024]{1,0:T(8,128)S(1)}, f32[32,1024]{1,0:T(8,128)S(1)}, u32[]{:S(2)}, u32[]{:S(2)}) collective-permute-start(f32[32,1024]{1,0:T(8,128)S(1)} %get-tuple-element.40), channel_id=1, source_target_pairs={{0,6},{1,7},{2,4},{3,5},{4,2},{5,3},{6,0},{7,1},{8,14},{9,15},{10,... | collective-permute-start | bytes 393224 | tf_op jit(solution)/shard_map/ppermute | solution.py:457
  23.6 0.0 collective-permute-start.2
  23.6 0.6 collective-permute-start.1
  24.3 0.0 copy-done
  24.3 2.0 %filter_matrix.1 = (f32[512,512]{1,0:T(8,128)S(1)}, bf16[256,256]{1,0:T(8,128)(2,1)S(1)}) custom-call(f32[1,512]{1,0:T(1,128)} %bitcast.47, f32[512,512]{1,0:T(8,128)} %constant.56.clone.cosine_hbm, bf16[256,256]{1,0:T(8,128)(2,1)} %bitcast.42), custom_call_target="tpu_custom_call" | custom-call | tf_op jit(solution)/shard_map/filter_matrix/pallas_call | solution.py:60
  26.3 1.6 %collective-permute-done.3.refs_3_ = f32[32,1024]{1,0:T(8,128)S(1)} collective-permute-done((f32[32,1024]{1,0:T(8,128)S(1)}, f32[32,1024]{1,0:T(8,128)S(1)}, u32[]{:S(2)}, u32[]{:S(2)}) %collective-permute-start.3) | collective-permute-done | bytes 131104 | tf_op jit(solution)/shard_map/ppermute | solution.py:457
  27.9 3.4 %collective-permute-done.2.refs_2_ = f32[32,1024]{1,0:T(8,128)S(1)} collective-permute-done((f32[32,1024]{1,0:T(8,128)S(1)}, f32[32,1024]{1,0:T(8,128)S(1)}, u32[]{:S(2)}, u32[]{:S(2)}) %collective-permute-start.2) | collective-permute-done | bytes 131104 | tf_op jit(solution)/shard_map/ppermute | solution.py:457
  31.3 3.7 %collective-permute-done.1.refs_1_ = f32[32,1024]{1,0:T(8,128)S(1)} collective-permute-done((f32[32,1024]{1,0:T(8,128)S(1)}, f32[32,1024]{1,0:T(8,128)S(1)}, u32[]{:S(2)}, u32[]{:S(2)}) %collective-permute-start.1) | collective-permute-done | bytes 131104 | tf_op jit(solution)/shard_map/ppermute | solution.py:457
  35.0 1.4 %refine.1 = (f32[64,512]{1,0:T(8,128)S(1)}, bf16[32,1024]{1,0:T(8,128)(2,1)S(1)}) custom-call(f32[32,1024]{1,0:T(8,128)S(1)} %get-tuple-element.43.refs_0_, f32[32,1024]{1,0:T(8,128)S(1)} %collective-permute-done.1.refs_1_, f32[32,1024]{1,0:T(8,128)S(1)} %collective-permute-done.2.refs_2_, f32[32,1024]{1,0:T(8,128)S(1)} %collective-permute-done.3.refs_3_, ...), custom_call_target="tpu_custom_call" | custom-call | tf_op jit(solution)/shard_map/refine/pallas_call | solution.py:482
  36.4 0.1 collective-permute-start.6
  36.5 3.0 %collective-permute-start.5 = (bf16[32,1024]{1,0:T(8,128)(2,1)S(1)}, bf16[32,1024]{1,0:T(8,128)(2,1)S(1)}, u32[]{:S(2)}, u32[]{:S(2)}) collective-permute-start(bf16[32,1024]{1,0:T(8,128)(2,1)S(1)} %get-tuple-element.28.refs_1_), channel_id=1, source_target_pairs={{0,4},{1,5},{2,6},{3,7},{4,0},{5,1},{6,2},{7,3},{8,12},{9,13},{10,... | collective-permute-start | bytes 196616 | tf_op jit(solution)/shard_map/ppermute | solution.py:498
  39.5 1.3 %collective-permute-start.4 = (bf16[32,1024]{1,0:T(8,128)(2,1)S(1)}, bf16[32,1024]{1,0:T(8,128)(2,1)S(1)}, u32[]{:S(2)}, u32[]{:S(2)}) collective-permute-start(bf16[32,1024]{1,0:T(8,128)(2,1)S(1)} %get-tuple-element.28.refs_1_), channel_id=1, source_target_pairs={{0,6},{1,7},{2,4},{3,5},{4,2},{5,3},{6,0},{7,1},{8,14},{9,15},{10,... | collective-permute-start | bytes 196616 | tf_op jit(solution)/shard_map/ppermute | solution.py:498
  40.8 0.0 collective-permute-start.7
  40.8 0.0 collective-permute-done.6.refs_4_
  40.8 0.5 collective-permute-start.10
  41.3 2.2 %collective-permute-done.5.refs_3_ = bf16[32,1024]{1,0:T(8,128)(2,1)S(1)} collective-permute-done((bf16[32,1024]{1,0:T(8,128)(2,1)S(1)}, bf16[32,1024]{1,0:T(8,128)(2,1)S(1)}, u32[]{:S(2)}, u32[]{:S(2)}) %collective-permute-start.5) | collective-permute-done | bytes 65568 | tf_op jit(solution)/shard_map/ppermute | solution.py:498
  43.5 0.0 collective-permute-start.9
  43.5 2.0 %collective-permute-done.4.refs_2_ = bf16[32,1024]{1,0:T(8,128)(2,1)S(1)} collective-permute-done((bf16[32,1024]{1,0:T(8,128)(2,1)S(1)}, bf16[32,1024]{1,0:T(8,128)(2,1)S(1)}, u32[]{:S(2)}, u32[]{:S(2)}) %collective-permute-start.4) | collective-permute-done | bytes 65568 | tf_op jit(solution)/shard_map/ppermute | solution.py:498
  45.5 0.0 collective-permute-start.8
  45.5 0.1 stack.35.refs_0_
  45.6 0.0 copy-start.1
  45.6 0.0 collective-permute-done.7.refs_5_
  45.6 0.0 collective-permute-done.10.refs_8_
  45.6 0.0 collective-permute-done.9.refs_7_
  45.7 1.1 %collective-permute-done.8.refs_6_ = bf16[32,1024]{1,0:T(8,128)(2,1)S(1)} collective-permute-done((bf16[32,1024]{1,0:T(8,128)(2,1)S(1)}, bf16[32,1024]{1,0:T(8,128)(2,1)S(1)}, u32[]{:S(2)}, u32[]{:S(2)}) %collective-permute-start.8) | collective-permute-done | bytes 65568 | tf_op jit(solution)/shard_map/ppermute | solution.py:501
  46.8 8.2 %backward.2 = (bf16[256,3072]{1,0:T(8,128)(2,1)S(1)}, f32[32,2048]{1,0:T(8,128)S(1)}, s16[32,2176]{1,0:T(8,128)(2,1)S(1)}, s16[32,2176]{1,0:T(8,128)(2,1)S(1)}, s16[32,2176]{1,0:T(8,128)(2,1)S(1)}) custom-call(s32[1]{0:T(128)} %bitcast.18.own_ref, bf16[3072,2048]{1,0:T(8,128)(2,1)} %get-tuple-element.27.tally_hbm, s32[8]{0:T(128)S(1)} %stack.35.refs_0_, ...), custom_call_target="tpu_custom_call" | custom-call | flops 3221225472 | bytes 12582912 | tf_op jit(solution)/shard_map/backward/pallas_call | solution.py:397
  55.0 2.5 %collective-permute-start.11 = (s16[32,2176]{1,0:T(8,128)(2,1)S(1)}, s16[32,2176]{1,0:T(8,128)(2,1)S(1)}, u32[]{:S(2)}, u32[]{:S(2)}) collective-permute-start(s16[32,2176]{1,0:T(8,128)(2,1)S(1)} %get-tuple-element.31), channel_id=1, source_target_pairs={{0,24},{8,16},{16,8},{24,0},{1,25},{9,17},{17,9},{25,1},{2,26},{10... | collective-permute-start | bytes 417800 | tf_op jit(solution)/shard_map/ppermute | solution.py:415
  57.5 0.5 collective-permute-start.12
  58.0 0.5 collective-permute-start.13
  58.6 0.0 copy-done.1
  58.6 3.9 %backward.3 = (f32[32,2048]{1,0:T(8,128)S(1)}, s16[32,2176]{1,0:T(8,128)(2,1)S(1)}, s16[32,2176]{1,0:T(8,128)(2,1)S(1)}, s16[32,2176]{1,0:T(8,128)(2,1)S(1)}) custom-call(s32[1]{0:T(128)} %bitcast.18.own_ref, bf16[3072,2048]{1,0:T(8,128)(2,1)S(1)} %copy-done.1, bf16[256,3072]{1,0:T(8,128)(2,1)S(1)} %get-tuple-element.35.refs_0_), custom_call_target="tpu_custom_call" | custom-call | flops 3221225472 | bytes 12582912 | tf_op jit(solution)/shard_map/backward/pallas_call | solution.py:397
  62.5 2.5 %collective-permute-start.14 = (s16[32,2176]{1,0:T(8,128)(2,1)S(1)}, s16[32,2176]{1,0:T(8,128)(2,1)S(1)}, u32[]{:S(2)}, u32[]{:S(2)}) collective-permute-start(s16[32,2176]{1,0:T(8,128)(2,1)S(1)} %get-tuple-element.37), channel_id=1, source_target_pairs={{0,24},{8,16},{16,8},{24,0},{1,25},{9,17},{17,9},{25,1},{2,26},{10... | collective-permute-start | bytes 417800 | tf_op jit(solution)/shard_map/ppermute | solution.py:415
  65.0 0.5 collective-permute-start.15
  65.5 0.0 collective-permute-done.11.refs_1_
  65.5 0.5 collective-permute-start.16
  66.1 0.8 %copy.14 = f32[2,32,512]{2,0,1:T(2,128)} copy(f32[2,32,512]{2,1,0:T(8,128)S(1)} %bitcast.39) | data formatting | bytes 262144 | tf_op jit(solution)/shard_map/reshape | solution.py:534
  66.8 0.0 collective-permute-done.12.refs_2_
  66.8 0.0 collective-permute-done.13.refs_3_
  66.8 2.5 %collective-permute-done.14.refs_5_ = s16[32,2176]{1,0:T(8,128)(2,1)S(1)} collective-permute-done((s16[32,2176]{1,0:T(8,128)(2,1)S(1)}, s16[32,2176]{1,0:T(8,128)(2,1)S(1)}, u32[]{:S(2)}, u32[]{:S(2)}) %collective-permute-start.14) | collective-permute-done | bytes 139296 | tf_op jit(solution)/shard_map/ppermute | solution.py:415
  69.3 2.0 %collective-permute-done.15.refs_6_ = s16[32,2176]{1,0:T(8,128)(2,1)S(1)} collective-permute-done((s16[32,2176]{1,0:T(8,128)(2,1)S(1)}, s16[32,2176]{1,0:T(8,128)(2,1)S(1)}, u32[]{:S(2)}, u32[]{:S(2)}) %collective-permute-start.15) | collective-permute-done | bytes 139296 | tf_op jit(solution)/shard_map/ppermute | solution.py:415
  71.3 0.1 collective-permute-done.16.refs_7_
  71.3 1.1 %finish.1 = f32[32,4096]{1,0:T(8,128)} custom-call(f32[32,2048]{1,0:T(8,128)S(1)} %get-tuple-element.30.refs_0_, s16[32,2176]{1,0:T(8,128)(2,1)S(1)} %collective-permute-done.11.refs_1_, s16[32,2176]{1,0:T(8,128)(2,1)S(1)} %collective-permute-done.12.refs_2_, s16[32,2176]{1,0:T(8,128)(2,1)S(1)} %collective-permute-done.13.refs_3_, ...), custom_call_target="tpu_custom_call" | custom-call | tf_op jit(solution)/shard_map/finish/pallas_call | solution.py:438
  (3 shorter events, 0.1 us)
Async XLA Ops:
  0.6 23.6 %copy-start = (f32[256,2,512]{2,1,0:T(2,128)S(1)}, f32[256,2,512]{2,1,0:T(2,128)}, u32[]{:S(2)}) copy-start(f32[256,2,512]{2,1,0:T(2,128)} %param.12) | copy-start | bytes 3145732
  16.4 2.1 %collective-permute-start = (f32[4,32,1024]{2,1,0:T(8,128)S(1)}, f32[4,32,1024]{2,1,0:T(8,128)S(1)}, u32[]{:S(2)}, u32[]{:S(2)}) collective-permute-start(f32[4,32,1024]{2,1,0:T(8,128)S(1)} %get-tuple-element.22), channel_id=1, source_target_pairs={{0,1},{1,0},{2,3},{3,2},{4,5},{5,4},{6,7},{7,6},{8,9},{9,8},{10,11... | collective-permute-start | bytes 1572872 | tf_op jit(solution)/shard_map/ppermute | solution.py:451
  18.6 9.4 %collective-permute-start.3 = (f32[32,1024]{1,0:T(8,128)S(1)}, f32[32,1024]{1,0:T(8,128)S(1)}, u32[]{:S(2)}, u32[]{:S(2)}) collective-permute-start(f32[32,1024]{1,0:T(8,128)S(1)} %get-tuple-element.40), channel_id=1, source_target_pairs={{0,6},{1,7},{2,4},{3,5},{4,2},{5,3},{6,0},{7,1},{8,14},{9,15},{10,... | collective-permute-start | bytes 393224 | tf_op jit(solution)/shard_map/ppermute | solution.py:457
  23.6 7.7 %collective-permute-start.2 = (f32[32,1024]{1,0:T(8,128)S(1)}, f32[32,1024]{1,0:T(8,128)S(1)}, u32[]{:S(2)}, u32[]{:S(2)}) collective-permute-start(f32[32,1024]{1,0:T(8,128)S(1)} %get-tuple-element.41), channel_id=1, source_target_pairs={{0,2},{1,3},{2,0},{3,1},{4,6},{5,7},{6,4},{7,5},{8,10},{9,11},{10,... | collective-permute-start | bytes 393224 | tf_op jit(solution)/shard_map/ppermute | solution.py:457
  23.6 11.4 %collective-permute-start.1 = (f32[32,1024]{1,0:T(8,128)S(1)}, f32[32,1024]{1,0:T(8,128)S(1)}, u32[]{:S(2)}, u32[]{:S(2)}) collective-permute-start(f32[32,1024]{1,0:T(8,128)S(1)} %get-tuple-element.42), channel_id=1, source_target_pairs={{0,4},{1,5},{2,6},{3,7},{4,0},{5,1},{6,2},{7,3},{8,12},{9,13},{10,... | collective-permute-start | bytes 393224 | tf_op jit(solution)/shard_map/ppermute | solution.py:457
  36.4 4.5 %collective-permute-start.6 = (bf16[32,1024]{1,0:T(8,128)(2,1)S(1)}, bf16[32,1024]{1,0:T(8,128)(2,1)S(1)}, u32[]{:S(2)}, u32[]{:S(2)}) collective-permute-start(bf16[32,1024]{1,0:T(8,128)(2,1)S(1)} %get-tuple-element.28.refs_1_), channel_id=1, source_target_pairs={{0,2},{1,3},{2,0},{3,1},{4,6},{5,7},{6,4},{7,5},{8,10},{9,11},{10,... | collective-permute-start | bytes 196616 | tf_op jit(solution)/shard_map/ppermute | solution.py:498
  36.5 7.1 %collective-permute-start.5 = (bf16[32,1024]{1,0:T(8,128)(2,1)S(1)}, bf16[32,1024]{1,0:T(8,128)(2,1)S(1)}, u32[]{:S(2)}, u32[]{:S(2)}) collective-permute-start(bf16[32,1024]{1,0:T(8,128)(2,1)S(1)} %get-tuple-element.28.refs_1_), channel_id=1, source_target_pairs={{0,4},{1,5},{2,6},{3,7},{4,0},{5,1},{6,2},{7,3},{8,12},{9,13},{10,... | collective-permute-start | bytes 196616 | tf_op jit(solution)/shard_map/ppermute | solution.py:498
  39.5 6.1 %collective-permute-start.4 = (bf16[32,1024]{1,0:T(8,128)(2,1)S(1)}, bf16[32,1024]{1,0:T(8,128)(2,1)S(1)}, u32[]{:S(2)}, u32[]{:S(2)}) collective-permute-start(bf16[32,1024]{1,0:T(8,128)(2,1)S(1)} %get-tuple-element.28.refs_1_), channel_id=1, source_target_pairs={{0,6},{1,7},{2,4},{3,5},{4,2},{5,3},{6,0},{7,1},{8,14},{9,15},{10,... | collective-permute-start | bytes 196616 | tf_op jit(solution)/shard_map/ppermute | solution.py:498
  40.8 4.8 %collective-permute-start.7 = (bf16[32,1024]{1,0:T(8,128)(2,1)S(1)}, bf16[32,1024]{1,0:T(8,128)(2,1)S(1)}, u32[]{:S(2)}, u32[]{:S(2)}) collective-permute-start(bf16[32,1024]{1,0:T(8,128)(2,1)S(1)} %get-tuple-element.28.refs_1_), channel_id=1, source_target_pairs={{0,1},{1,0},{2,3},{3,2},{4,5},{5,4},{6,7},{7,6},{8,9},{9,8},{10,11... | collective-permute-start | bytes 196616 | tf_op jit(solution)/shard_map/ppermute | solution.py:501
  40.8 4.8 %collective-permute-start.10 = (bf16[32,1024]{1,0:T(8,128)(2,1)S(1)}, bf16[32,1024]{1,0:T(8,128)(2,1)S(1)}, u32[]{:S(2)}, u32[]{:S(2)}) collective-permute-start(bf16[32,1024]{1,0:T(8,128)(2,1)S(1)} %collective-permute-done.6.refs_4_), channel_id=1, source_target_pairs={{0,1},{1,0},{2,3},{3,2},{4,5},{5,4},{6,7},{7,6},{8,9},{9,8},{10,11... | collective-permute-start | bytes 196616 | tf_op jit(solution)/shard_map/ppermute | solution.py:501
  43.5 2.1 %collective-permute-start.9 = (bf16[32,1024]{1,0:T(8,128)(2,1)S(1)}, bf16[32,1024]{1,0:T(8,128)(2,1)S(1)}, u32[]{:S(2)}, u32[]{:S(2)}) collective-permute-start(bf16[32,1024]{1,0:T(8,128)(2,1)S(1)} %collective-permute-done.5.refs_3_), channel_id=1, source_target_pairs={{0,1},{1,0},{2,3},{3,2},{4,5},{5,4},{6,7},{7,6},{8,9},{9,8},{10,11... | collective-permute-start | bytes 196616 | tf_op jit(solution)/shard_map/ppermute | solution.py:501
  45.5 1.3 %collective-permute-start.8 = (bf16[32,1024]{1,0:T(8,128)(2,1)S(1)}, bf16[32,1024]{1,0:T(8,128)(2,1)S(1)}, u32[]{:S(2)}, u32[]{:S(2)}) collective-permute-start(bf16[32,1024]{1,0:T(8,128)(2,1)S(1)} %collective-permute-done.4.refs_2_), channel_id=1, source_target_pairs={{0,1},{1,0},{2,3},{3,2},{4,5},{5,4},{6,7},{7,6},{8,9},{9,8},{10,11... | collective-permute-start | bytes 196616 | tf_op jit(solution)/shard_map/ppermute | solution.py:501
  45.6 12.9 %copy-start.1 = (bf16[3072,2048]{1,0:T(8,128)(2,1)S(1)}, bf16[3072,2048]{1,0:T(8,128)(2,1)}, u32[]{:S(2)}) copy-start(bf16[3072,2048]{1,0:T(8,128)(2,1)} %get-tuple-element.34.tally_hbm) | copy-start | bytes 37748740
  55.0 10.5 %collective-permute-start.11 = (s16[32,2176]{1,0:T(8,128)(2,1)S(1)}, s16[32,2176]{1,0:T(8,128)(2,1)S(1)}, u32[]{:S(2)}, u32[]{:S(2)}) collective-permute-start(s16[32,2176]{1,0:T(8,128)(2,1)S(1)} %get-tuple-element.31), channel_id=1, source_target_pairs={{0,24},{8,16},{16,8},{24,0},{1,25},{9,17},{17,9},{25,1},{2,26},{10... | collective-permute-start | bytes 417800 | tf_op jit(solution)/shard_map/ppermute | solution.py:415
  57.5 9.3 %collective-permute-start.12 = (s16[32,2176]{1,0:T(8,128)(2,1)S(1)}, s16[32,2176]{1,0:T(8,128)(2,1)S(1)}, u32[]{:S(2)}, u32[]{:S(2)}) collective-permute-start(s16[32,2176]{1,0:T(8,128)(2,1)S(1)} %get-tuple-element.32), channel_id=1, source_target_pairs={{0,16},{8,24},{16,0},{24,8},{1,17},{9,25},{17,1},{25,9},{2,18},{10... | collective-permute-start | bytes 417800 | tf_op jit(solution)/shard_map/ppermute | solution.py:415
  58.0 8.8 %collective-permute-start.13 = (s16[32,2176]{1,0:T(8,128)(2,1)S(1)}, s16[32,2176]{1,0:T(8,128)(2,1)S(1)}, u32[]{:S(2)}, u32[]{:S(2)}) collective-permute-start(s16[32,2176]{1,0:T(8,128)(2,1)S(1)} %get-tuple-element.33), channel_id=1, source_target_pairs={{0,8},{8,0},{16,24},{24,16},{1,9},{9,1},{17,25},{25,17},{2,10},{10... | collective-permute-start | bytes 417800 | tf_op jit(solution)/shard_map/ppermute | solution.py:415
  62.5 6.8 %collective-permute-start.14 = (s16[32,2176]{1,0:T(8,128)(2,1)S(1)}, s16[32,2176]{1,0:T(8,128)(2,1)S(1)}, u32[]{:S(2)}, u32[]{:S(2)}) collective-permute-start(s16[32,2176]{1,0:T(8,128)(2,1)S(1)} %get-tuple-element.37), channel_id=1, source_target_pairs={{0,24},{8,16},{16,8},{24,0},{1,25},{9,17},{17,9},{25,1},{2,26},{10... | collective-permute-start | bytes 417800 | tf_op jit(solution)/shard_map/ppermute | solution.py:415
  65.0 6.3 %collective-permute-start.15 = (s16[32,2176]{1,0:T(8,128)(2,1)S(1)}, s16[32,2176]{1,0:T(8,128)(2,1)S(1)}, u32[]{:S(2)}, u32[]{:S(2)}) collective-permute-start(s16[32,2176]{1,0:T(8,128)(2,1)S(1)} %get-tuple-element.38), channel_id=1, source_target_pairs={{0,16},{8,24},{16,0},{24,8},{1,17},{9,25},{17,1},{25,9},{2,18},{10... | collective-permute-start | bytes 417800 | tf_op jit(solution)/shard_map/ppermute | solution.py:415
  65.5 5.8 %collective-permute-start.16 = (s16[32,2176]{1,0:T(8,128)(2,1)S(1)}, s16[32,2176]{1,0:T(8,128)(2,1)S(1)}, u32[]{:S(2)}, u32[]{:S(2)}) collective-permute-start(s16[32,2176]{1,0:T(8,128)(2,1)S(1)} %get-tuple-element.39), channel_id=1, source_target_pairs={{0,8},{8,0},{16,24},{24,16},{1,9},{9,1},{17,25},{25,17},{2,10},{10... | collective-permute-start | bytes 417800 | tf_op jit(solution)/shard_map/ppermute | solution.py:415

commit v5 on v4

--- a/solution.py
+++ b/solution.py
@@ -15,7 +15,7 @@
 CODE = 32766.0
 TINY = 1e-37
 RATE = 256 / math.log(2.0)
-GRAIN = 256
+GRAIN = 512
 SPANS = (4, 4)
 CUT = 512
 
@@ -183,7 +183,7 @@
     span = units // chunks
     stores = []
     for chunk in range(chunks):
-        lax.fori_loop(chunk * span, (chunk + 1) * span, unit_step, 0, unroll=8)
+        lax.fori_loop(chunk * span, (chunk + 1) * span, unit_step, 0, unroll=16)
         part = pl.ds(chunk * span * rows, span * rows)
         begin = 0
         for spot, tally_hbm in enumerate(tally_hbms):
@@ -269,7 +269,7 @@
             pltpu.VMEM((sensors // UNIT, UNIT * slots), jnp.int32),
             pltpu.VMEM((sensors * combos, pressure.shape[1]), jnp.float32),
             pltpu.SemaphoreType.DMA((len(operands),)),
-            pltpu.SemaphoreType.DMA((4, len(SPANS))),
+            pltpu.SemaphoreType.DMA((2, len(SPANS))),
         ],
         compiler_params=pltpu.CompilerParams(vmem_limit_bytes=48 << 20),
         name="forward",

time: 72.6 us -> 72.1 us (level)
  no operation moved by 1% of the time
where the time goes in v5:
time: 72.1 us; the launch traced here: 71.9 us
  Pallas kernels  31.8 us (44%)
  waiting for transfers between devices  20.1 us (28%)
  starting transfers between devices  18.3 us (25%)
  local copies, waits for them, and re-layouts  0.94 us (1%)
  between operations  0.76 us (1%)
    pallas_call x1, Pallas kernels, forward(): pl.pallas_call(functools.partial(forward_kernel, kinds, places), in_specs...  15.4 us
    pallas_call x2, Pallas kernels, backward(): pl.pallas_call(functools.partial(backward_kernel, *(combos or (0, 0)), le...  12 us
    ppermute x3, waiting for transfers between devices, scatter_slab(): lax.ppermute(block, 'slab', [(j, j ^ 2 * step) for j in range(slabs)])  8.69 us
    ppermute x6, starting transfers between devices, backward(): received.append(lax.ppermute(codes[step - 1], 'sens', pairs))  7.11 us
    ppermute x3, starting transfers between devices, scatter_slab(): lax.ppermute(block, 'slab', [(j, j ^ 2 * step) for j in range(slabs)])  5.68 us
    ppermute x6, waiting for transfers between devices, backward(): received.append(lax.ppermute(codes[step - 1], 'sens', pairs))  4.53 us
    ppermute x3, starting transfers between devices, gather_slab(): lax.ppermute(share, 'slab', [(j, j ^ 2 * step) for j in range(slabs)])  4.44 us
    ppermute x3, waiting for transfers between devices, gather_slab(): lax.ppermute(share, 'slab', [(j, j ^ 2 * step) for j in range(slabs)])  4.2 us
  transfers between devices with their start and end apart: 17, of which 10 were waited for; matrix products, arithmetic and copies ran while one was open for 1% of the time, Pallas kernels for 8%

profile of v5, /device:TPU:0, one launch (start us, length us, event | category | flops | bytes accessed | tf_op | source)
XLA Modules:
  0.0 71.9 jit_solution(11194000392446455474)
XLA Ops:
  0.6 0.0 copy-start
  0.7 15.4 %forward.1 = (bf16[3072,2048]{1,0:T(8,128)(2,1)}, bf16[3072,2048]{1,0:T(8,128)(2,1)}, f32[4,32,1024]{2,1,0:T(8,128)S(1)}, f32[4,32,1024]{2,1,0:T(8,128)S(1)}) custom-call(s32[1]{0:T(128)} %bitcast.core_ref, s32[64,256]{1,0:T(8,128)} %bitcast.44, s32[64,256]{1,0:T(8,128)} %bitcast.45, s32[64,256]{1,0:T(8,128)} %bitcast.46, s32[1,256]{1,0:T(1,128)} %bitcast.48, ...), custom_call_target="tpu_custom_call" | custom-call | tf_op jit(solution)/shard_map/forward/pallas_call | solution.py:257
  16.1 0.5 collective-permute-start
  16.6 1.5 %collective-permute-done = f32[4,32,1024]{2,1,0:T(8,128)S(1)} collective-permute-done((f32[4,32,1024]{2,1,0:T(8,128)S(1)}, f32[4,32,1024]{2,1,0:T(8,128)S(1)}, u32[]{:S(2)}, u32[]{:S(2)}) %collective-permute-start) | collective-permute-done | bytes 524320 | tf_op jit(solution)/shard_map/ppermute | solution.py:451
  18.1 0.1 add.25
  18.3 5.0 %collective-permute-start.3 = (f32[32,1024]{1,0:T(8,128)S(1)}, f32[32,1024]{1,0:T(8,128)S(1)}, u32[]{:S(2)}, u32[]{:S(2)}) collective-permute-start(f32[32,1024]{1,0:T(8,128)S(1)} %get-tuple-element.40), channel_id=1, source_target_pairs={{0,6},{1,7},{2,4},{3,5},{4,2},{5,3},{6,0},{7,1},{8,14},{9,15},{10,... | collective-permute-start | bytes 393224 | tf_op jit(solution)/shard_map/ppermute | solution.py:457
  23.3 0.0 collective-permute-start.2
  23.3 0.6 collective-permute-start.1
  24.0 0.0 copy-done
  24.0 2.0 %filter_matrix.1 = (f32[512,512]{1,0:T(8,128)S(1)}, bf16[256,256]{1,0:T(8,128)(2,1)S(1)}) custom-call(f32[1,512]{1,0:T(1,128)} %bitcast.47, f32[512,512]{1,0:T(8,128)} %constant.56.clone.cosine_hbm, bf16[256,256]{1,0:T(8,128)(2,1)} %bitcast.42), custom_call_target="tpu_custom_call" | custom-call | tf_op jit(solution)/shard_map/filter_matrix/pallas_call | solution.py:60
  26.0 1.6 %collective-permute-done.3.refs_3_ = f32[32,1024]{1,0:T(8,128)S(1)} collective-permute-done((f32[32,1024]{1,0:T(8,128)S(1)}, f32[32,1024]{1,0:T(8,128)S(1)}, u32[]{:S(2)}, u32[]{:S(2)}) %collective-permute-start.3) | collective-permute-done | bytes 131104 | tf_op jit(solution)/shard_map/ppermute | solution.py:457
  27.6 3.4 %collective-permute-done.2.refs_2_ = f32[32,1024]{1,0:T(8,128)S(1)} collective-permute-done((f32[32,1024]{1,0:T(8,128)S(1)}, f32[32,1024]{1,0:T(8,128)S(1)}, u32[]{:S(2)}, u32[]{:S(2)}) %collective-permute-start.2) | collective-permute-done | bytes 131104 | tf_op jit(solution)/shard_map/ppermute | solution.py:457
  31.0 3.7 %collective-permute-done.1.refs_1_ = f32[32,1024]{1,0:T(8,128)S(1)} collective-permute-done((f32[32,1024]{1,0:T(8,128)S(1)}, f32[32,1024]{1,0:T(8,128)S(1)}, u32[]{:S(2)}, u32[]{:S(2)}) %collective-permute-start.1) | collective-permute-done | bytes 131104 | tf_op jit(solution)/shard_map/ppermute | solution.py:457
  34.7 1.4 %refine.1 = (f32[64,512]{1,0:T(8,128)S(1)}, bf16[32,1024]{1,0:T(8,128)(2,1)S(1)}) custom-call(f32[32,1024]{1,0:T(8,128)S(1)} %get-tuple-element.43.refs_0_, f32[32,1024]{1,0:T(8,128)S(1)} %collective-permute-done.1.refs_1_, f32[32,1024]{1,0:T(8,128)S(1)} %collective-permute-done.2.refs_2_, f32[32,1024]{1,0:T(8,128)S(1)} %collective-permute-done.3.refs_3_, ...), custom_call_target="tpu_custom_call" | custom-call | tf_op jit(solution)/shard_map/refine/pallas_call | solution.py:482
  36.1 0.1 collective-permute-start.6
  36.1 3.0 %collective-permute-start.5 = (bf16[32,1024]{1,0:T(8,128)(2,1)S(1)}, bf16[32,1024]{1,0:T(8,128)(2,1)S(1)}, u32[]{:S(2)}, u32[]{:S(2)}) collective-permute-start(bf16[32,1024]{1,0:T(8,128)(2,1)S(1)} %get-tuple-element.28.refs_1_), channel_id=1, source_target_pairs={{0,4},{1,5},{2,6},{3,7},{4,0},{5,1},{6,2},{7,3},{8,12},{9,13},{10,... | collective-permute-start | bytes 196616 | tf_op jit(solution)/shard_map/ppermute | solution.py:498
  39.2 1.3 %collective-permute-start.4 = (bf16[32,1024]{1,0:T(8,128)(2,1)S(1)}, bf16[32,1024]{1,0:T(8,128)(2,1)S(1)}, u32[]{:S(2)}, u32[]{:S(2)}) collective-permute-start(bf16[32,1024]{1,0:T(8,128)(2,1)S(1)} %get-tuple-element.28.refs_1_), channel_id=1, source_target_pairs={{0,6},{1,7},{2,4},{3,5},{4,2},{5,3},{6,0},{7,1},{8,14},{9,15},{10,... | collective-permute-start | bytes 196616 | tf_op jit(solution)/shard_map/ppermute | solution.py:498
  40.5 0.0 collective-permute-start.7
  40.5 0.0 collective-permute-done.6.refs_4_
  40.5 0.5 collective-permute-start.10
  41.0 2.2 %collective-permute-done.5.refs_3_ = bf16[32,1024]{1,0:T(8,128)(2,1)S(1)} collective-permute-done((bf16[32,1024]{1,0:T(8,128)(2,1)S(1)}, bf16[32,1024]{1,0:T(8,128)(2,1)S(1)}, u32[]{:S(2)}, u32[]{:S(2)}) %collective-permute-start.5) | collective-permute-done | bytes 65568 | tf_op jit(solution)/shard_map/ppermute | solution.py:498
  43.2 0.0 collective-permute-start.9
  43.2 2.0 %collective-permute-done.4.refs_2_ = bf16[32,1024]{1,0:T(8,128)(2,1)S(1)} collective-permute-done((bf16[32,1024]{1,0:T(8,128)(2,1)S(1)}, bf16[32,1024]{1,0:T(8,128)(2,1)S(1)}, u32[]{:S(2)}, u32[]{:S(2)}) %collective-permute-start.4) | collective-permute-done | bytes 65568 | tf_op jit(solution)/shard_map/ppermute | solution.py:498
  45.2 0.0 collective-permute-start.8
  45.2 0.1 stack.35.refs_0_
  45.3 0.0 copy-start.1
  45.3 0.0 collective-permute-done.7.refs_5_
  45.3 0.0 collective-permute-done.10.refs_8_
  45.3 0.0 collective-permute-done.9.refs_7_
  45.4 1.1 %collective-permute-done.8.refs_6_ = bf16[32,1024]{1,0:T(8,128)(2,1)S(1)} collective-permute-done((bf16[32,1024]{1,0:T(8,128)(2,1)S(1)}, bf16[32,1024]{1,0:T(8,128)(2,1)S(1)}, u32[]{:S(2)}, u32[]{:S(2)}) %collective-permute-start.8) | collective-permute-done | bytes 65568 | tf_op jit(solution)/shard_map/ppermute | solution.py:501
  46.5 8.1 %backward.2 = (bf16[256,3072]{1,0:T(8,128)(2,1)S(1)}, f32[32,2048]{1,0:T(8,128)S(1)}, s16[32,2176]{1,0:T(8,128)(2,1)S(1)}, s16[32,2176]{1,0:T(8,128)(2,1)S(1)}, s16[32,2176]{1,0:T(8,128)(2,1)S(1)}) custom-call(s32[1]{0:T(128)} %bitcast.18.own_ref, bf16[3072,2048]{1,0:T(8,128)(2,1)} %get-tuple-element.27.tally_hbm, s32[8]{0:T(128)S(1)} %stack.35.refs_0_, ...), custom_call_target="tpu_custom_call" | custom-call | flops 3221225472 | bytes 12582912 | tf_op jit(solution)/shard_map/backward/pallas_call | solution.py:397
  54.6 2.5 %collective-permute-start.11 = (s16[32,2176]{1,0:T(8,128)(2,1)S(1)}, s16[32,2176]{1,0:T(8,128)(2,1)S(1)}, u32[]{:S(2)}, u32[]{:S(2)}) collective-permute-start(s16[32,2176]{1,0:T(8,128)(2,1)S(1)} %get-tuple-element.31), channel_id=1, source_target_pairs={{0,24},{8,16},{16,8},{24,0},{1,25},{9,17},{17,9},{25,1},{2,26},{10... | collective-permute-start | bytes 417800 | tf_op jit(solution)/shard_map/ppermute | solution.py:415
  57.1 0.5 collective-permute-start.12
  57.6 0.5 collective-permute-start.13
  58.2 0.0 copy-done.1
  58.2 3.8 %backward.3 = (f32[32,2048]{1,0:T(8,128)S(1)}, s16[32,2176]{1,0:T(8,128)(2,1)S(1)}, s16[32,2176]{1,0:T(8,128)(2,1)S(1)}, s16[32,2176]{1,0:T(8,128)(2,1)S(1)}) custom-call(s32[1]{0:T(128)} %bitcast.18.own_ref, bf16[3072,2048]{1,0:T(8,128)(2,1)S(1)} %copy-done.1, bf16[256,3072]{1,0:T(8,128)(2,1)S(1)} %get-tuple-element.35.refs_0_), custom_call_target="tpu_custom_call" | custom-call | flops 3221225472 | bytes 12582912 | tf_op jit(solution)/shard_map/backward/pallas_call | solution.py:397
  62.0 2.5 %collective-permute-start.14 = (s16[32,2176]{1,0:T(8,128)(2,1)S(1)}, s16[32,2176]{1,0:T(8,128)(2,1)S(1)}, u32[]{:S(2)}, u32[]{:S(2)}) collective-permute-start(s16[32,2176]{1,0:T(8,128)(2,1)S(1)} %get-tuple-element.37), channel_id=1, source_target_pairs={{0,24},{8,16},{16,8},{24,0},{1,25},{9,17},{17,9},{25,1},{2,26},{10... | collective-permute-start | bytes 417800 | tf_op jit(solution)/shard_map/ppermute | solution.py:415
  64.5 0.5 collective-permute-start.15
  65.0 0.0 collective-permute-done.11.refs_1_
  65.0 0.5 collective-permute-start.16
  65.6 0.8 %copy.14 = f32[2,32,512]{2,0,1:T(2,128)} copy(f32[2,32,512]{2,1,0:T(8,128)S(1)} %bitcast.39) | data formatting | bytes 262144 | tf_op jit(solution)/shard_map/reshape | solution.py:534
  66.3 0.0 collective-permute-done.12.refs_2_
  66.3 0.0 collective-permute-done.13.refs_3_
  66.3 2.5 %collective-permute-done.14.refs_5_ = s16[32,2176]{1,0:T(8,128)(2,1)S(1)} collective-permute-done((s16[32,2176]{1,0:T(8,128)(2,1)S(1)}, s16[32,2176]{1,0:T(8,128)(2,1)S(1)}, u32[]{:S(2)}, u32[]{:S(2)}) %collective-permute-start.14) | collective-permute-done | bytes 139296 | tf_op jit(solution)/shard_map/ppermute | solution.py:415
  68.8 2.0 %collective-permute-done.15.refs_6_ = s16[32,2176]{1,0:T(8,128)(2,1)S(1)} collective-permute-done((s16[32,2176]{1,0:T(8,128)(2,1)S(1)}, s16[32,2176]{1,0:T(8,128)(2,1)S(1)}, u32[]{:S(2)}, u32[]{:S(2)}) %collective-permute-start.15) | collective-permute-done | bytes 139296 | tf_op jit(solution)/shard_map/ppermute | solution.py:415
  70.8 0.1 collective-permute-done.16.refs_7_
  70.9 1.1 %finish.1 = f32[32,4096]{1,0:T(8,128)} custom-call(f32[32,2048]{1,0:T(8,128)S(1)} %get-tuple-element.30.refs_0_, s16[32,2176]{1,0:T(8,128)(2,1)S(1)} %collective-permute-done.11.refs_1_, s16[32,2176]{1,0:T(8,128)(2,1)S(1)} %collective-permute-done.12.refs_2_, s16[32,2176]{1,0:T(8,128)(2,1)S(1)} %collective-permute-done.13.refs_3_, ...), custom_call_target="tpu_custom_call" | custom-call | tf_op jit(solution)/shard_map/finish/pallas_call | solution.py:438
  (3 shorter events, 0.1 us)
Async XLA Ops:
  0.6 23.3 %copy-start = (f32[256,2,512]{2,1,0:T(2,128)S(1)}, f32[256,2,512]{2,1,0:T(2,128)}, u32[]{:S(2)}) copy-start(f32[256,2,512]{2,1,0:T(2,128)} %param.12) | copy-start | bytes 3145732
  16.1 2.0 %collective-permute-start = (f32[4,32,1024]{2,1,0:T(8,128)S(1)}, f32[4,32,1024]{2,1,0:T(8,128)S(1)}, u32[]{:S(2)}, u32[]{:S(2)}) collective-permute-start(f32[4,32,1024]{2,1,0:T(8,128)S(1)} %get-tuple-element.22), channel_id=1, source_target_pairs={{0,1},{1,0},{2,3},{3,2},{4,5},{5,4},{6,7},{7,6},{8,9},{9,8},{10,11... | collective-permute-start | bytes 1572872 | tf_op jit(solution)/shard_map/ppermute | solution.py:451
  18.3 9.4 %collective-permute-start.3 = (f32[32,1024]{1,0:T(8,128)S(1)}, f32[32,1024]{1,0:T(8,128)S(1)}, u32[]{:S(2)}, u32[]{:S(2)}) collective-permute-start(f32[32,1024]{1,0:T(8,128)S(1)} %get-tuple-element.40), channel_id=1, source_target_pairs={{0,6},{1,7},{2,4},{3,5},{4,2},{5,3},{6,0},{7,1},{8,14},{9,15},{10,... | collective-permute-start | bytes 393224 | tf_op jit(solution)/shard_map/ppermute | solution.py:457
  23.3 7.7 %collective-permute-start.2 = (f32[32,1024]{1,0:T(8,128)S(1)}, f32[32,1024]{1,0:T(8,128)S(1)}, u32[]{:S(2)}, u32[]{:S(2)}) collective-permute-start(f32[32,1024]{1,0:T(8,128)S(1)} %get-tuple-element.41), channel_id=1, source_target_pairs={{0,2},{1,3},{2,0},{3,1},{4,6},{5,7},{6,4},{7,5},{8,10},{9,11},{10,... | collective-permute-start | bytes 393224 | tf_op jit(solution)/shard_map/ppermute | solution.py:457
  23.3 11.4 %collective-permute-start.1 = (f32[32,1024]{1,0:T(8,128)S(1)}, f32[32,1024]{1,0:T(8,128)S(1)}, u32[]{:S(2)}, u32[]{:S(2)}) collective-permute-start(f32[32,1024]{1,0:T(8,128)S(1)} %get-tuple-element.42), channel_id=1, source_target_pairs={{0,4},{1,5},{2,6},{3,7},{4,0},{5,1},{6,2},{7,3},{8,12},{9,13},{10,... | collective-permute-start | bytes 393224 | tf_op jit(solution)/shard_map/ppermute | solution.py:457
  36.1 4.5 %collective-permute-start.6 = (bf16[32,1024]{1,0:T(8,128)(2,1)S(1)}, bf16[32,1024]{1,0:T(8,128)(2,1)S(1)}, u32[]{:S(2)}, u32[]{:S(2)}) collective-permute-start(bf16[32,1024]{1,0:T(8,128)(2,1)S(1)} %get-tuple-element.28.refs_1_), channel_id=1, source_target_pairs={{0,2},{1,3},{2,0},{3,1},{4,6},{5,7},{6,4},{7,5},{8,10},{9,11},{10,... | collective-permute-start | bytes 196616 | tf_op jit(solution)/shard_map/ppermute | solution.py:498
  36.1 7.1 %collective-permute-start.5 = (bf16[32,1024]{1,0:T(8,128)(2,1)S(1)}, bf16[32,1024]{1,0:T(8,128)(2,1)S(1)}, u32[]{:S(2)}, u32[]{:S(2)}) collective-permute-start(bf16[32,1024]{1,0:T(8,128)(2,1)S(1)} %get-tuple-element.28.refs_1_), channel_id=1, source_target_pairs={{0,4},{1,5},{2,6},{3,7},{4,0},{5,1},{6,2},{7,3},{8,12},{9,13},{10,... | collective-permute-start | bytes 196616 | tf_op jit(solution)/shard_map/ppermute | solution.py:498
  39.2 6.1 %collective-permute-start.4 = (bf16[32,1024]{1,0:T(8,128)(2,1)S(1)}, bf16[32,1024]{1,0:T(8,128)(2,1)S(1)}, u32[]{:S(2)}, u32[]{:S(2)}) collective-permute-start(bf16[32,1024]{1,0:T(8,128)(2,1)S(1)} %get-tuple-element.28.refs_1_), channel_id=1, source_target_pairs={{0,6},{1,7},{2,4},{3,5},{4,2},{5,3},{6,0},{7,1},{8,14},{9,15},{10,... | collective-permute-start | bytes 196616 | tf_op jit(solution)/shard_map/ppermute | solution.py:498
  40.5 4.8 %collective-permute-start.7 = (bf16[32,1024]{1,0:T(8,128)(2,1)S(1)}, bf16[32,1024]{1,0:T(8,128)(2,1)S(1)}, u32[]{:S(2)}, u32[]{:S(2)}) collective-permute-start(bf16[32,1024]{1,0:T(8,128)(2,1)S(1)} %get-tuple-element.28.refs_1_), channel_id=1, source_target_pairs={{0,1},{1,0},{2,3},{3,2},{4,5},{5,4},{6,7},{7,6},{8,9},{9,8},{10,11... | collective-permute-start | bytes 196616 | tf_op jit(solution)/shard_map/ppermute | solution.py:501
  40.5 4.8 %collective-permute-start.10 = (bf16[32,1024]{1,0:T(8,128)(2,1)S(1)}, bf16[32,1024]{1,0:T(8,128)(2,1)S(1)}, u32[]{:S(2)}, u32[]{:S(2)}) collective-permute-start(bf16[32,1024]{1,0:T(8,128)(2,1)S(1)} %collective-permute-done.6.refs_4_), channel_id=1, source_target_pairs={{0,1},{1,0},{2,3},{3,2},{4,5},{5,4},{6,7},{7,6},{8,9},{9,8},{10,11... | collective-permute-start | bytes 196616 | tf_op jit(solution)/shard_map/ppermute | solution.py:501
  43.2 2.1 %collective-permute-start.9 = (bf16[32,1024]{1,0:T(8,128)(2,1)S(1)}, bf16[32,1024]{1,0:T(8,128)(2,1)S(1)}, u32[]{:S(2)}, u32[]{:S(2)}) collective-permute-start(bf16[32,1024]{1,0:T(8,128)(2,1)S(1)} %collective-permute-done.5.refs_3_), channel_id=1, source_target_pairs={{0,1},{1,0},{2,3},{3,2},{4,5},{5,4},{6,7},{7,6},{8,9},{9,8},{10,11... | collective-permute-start | bytes 196616 | tf_op jit(solution)/shard_map/ppermute | solution.py:501
  45.2 1.3 %collective-permute-start.8 = (bf16[32,1024]{1,0:T(8,128)(2,1)S(1)}, bf16[32,1024]{1,0:T(8,128)(2,1)S(1)}, u32[]{:S(2)}, u32[]{:S(2)}) collective-permute-start(bf16[32,1024]{1,0:T(8,128)(2,1)S(1)} %collective-permute-done.4.refs_2_), channel_id=1, source_target_pairs={{0,1},{1,0},{2,3},{3,2},{4,5},{5,4},{6,7},{7,6},{8,9},{9,8},{10,11... | collective-permute-start | bytes 196616 | tf_op jit(solution)/shard_map/ppermute | solution.py:501
  45.3 12.9 %copy-start.1 = (bf16[3072,2048]{1,0:T(8,128)(2,1)S(1)}, bf16[3072,2048]{1,0:T(8,128)(2,1)}, u32[]{:S(2)}) copy-start(bf16[3072,2048]{1,0:T(8,128)(2,1)} %get-tuple-element.34.tally_hbm) | copy-start | bytes 37748740
  54.6 10.4 %collective-permute-start.11 = (s16[32,2176]{1,0:T(8,128)(2,1)S(1)}, s16[32,2176]{1,0:T(8,128)(2,1)S(1)}, u32[]{:S(2)}, u32[]{:S(2)}) collective-permute-start(s16[32,2176]{1,0:T(8,128)(2,1)S(1)} %get-tuple-element.31), channel_id=1, source_target_pairs={{0,24},{8,16},{16,8},{24,0},{1,25},{9,17},{17,9},{25,1},{2,26},{10... | collective-permute-start | bytes 417800 | tf_op jit(solution)/shard_map/ppermute | solution.py:415
  57.1 9.2 %collective-permute-start.12 = (s16[32,2176]{1,0:T(8,128)(2,1)S(1)}, s16[32,2176]{1,0:T(8,128)(2,1)S(1)}, u32[]{:S(2)}, u32[]{:S(2)}) collective-permute-start(s16[32,2176]{1,0:T(8,128)(2,1)S(1)} %get-tuple-element.32), channel_id=1, source_target_pairs={{0,16},{8,24},{16,0},{24,8},{1,17},{9,25},{17,1},{25,9},{2,18},{10... | collective-permute-start | bytes 417800 | tf_op jit(solution)/shard_map/ppermute | solution.py:415
  57.6 8.7 %collective-permute-start.13 = (s16[32,2176]{1,0:T(8,128)(2,1)S(1)}, s16[32,2176]{1,0:T(8,128)(2,1)S(1)}, u32[]{:S(2)}, u32[]{:S(2)}) collective-permute-start(s16[32,2176]{1,0:T(8,128)(2,1)S(1)} %get-tuple-element.33), channel_id=1, source_target_pairs={{0,8},{8,0},{16,24},{24,16},{1,9},{9,1},{17,25},{25,17},{2,10},{10... | collective-permute-start | bytes 417800 | tf_op jit(solution)/shard_map/ppermute | solution.py:415
  62.0 6.8 %collective-permute-start.14 = (s16[32,2176]{1,0:T(8,128)(2,1)S(1)}, s16[32,2176]{1,0:T(8,128)(2,1)S(1)}, u32[]{:S(2)}, u32[]{:S(2)}) collective-permute-start(s16[32,2176]{1,0:T(8,128)(2,1)S(1)} %get-tuple-element.37), channel_id=1, source_target_pairs={{0,24},{8,16},{16,8},{24,0},{1,25},{9,17},{17,9},{25,1},{2,26},{10... | collective-permute-start | bytes 417800 | tf_op jit(solution)/shard_map/ppermute | solution.py:415
  64.5 6.3 %collective-permute-start.15 = (s16[32,2176]{1,0:T(8,128)(2,1)S(1)}, s16[32,2176]{1,0:T(8,128)(2,1)S(1)}, u32[]{:S(2)}, u32[]{:S(2)}) collective-permute-start(s16[32,2176]{1,0:T(8,128)(2,1)S(1)} %get-tuple-element.38), channel_id=1, source_target_pairs={{0,16},{8,24},{16,0},{24,8},{1,17},{9,25},{17,1},{25,9},{2,18},{10... | collective-permute-start | bytes 417800 | tf_op jit(solution)/shard_map/ppermute | solution.py:415
  65.0 5.8 %collective-permute-start.16 = (s16[32,2176]{1,0:T(8,128)(2,1)S(1)}, s16[32,2176]{1,0:T(8,128)(2,1)S(1)}, u32[]{:S(2)}, u32[]{:S(2)}) collective-permute-start(s16[32,2176]{1,0:T(8,128)(2,1)S(1)} %get-tuple-element.39), channel_id=1, source_target_pairs={{0,8},{8,0},{16,24},{24,16},{1,9},{9,1},{17,25},{25,17},{2,10},{10... | collective-permute-start | bytes 417800 | tf_op jit(solution)/shard_map/ppermute | solution.py:415

commit v6 on v5

--- a/solution.py
+++ b/solution.py
@@ -152,6 +152,7 @@
     row_iota = to_bf16(lax.broadcasted_iota(jnp.int32, (rows, width), 0))
     low_iota = to_bf16(lax.broadcasted_iota(jnp.int32, (LANES, width), 0))
     one, zero = jnp.ones((), jnp.bfloat16), jnp.zeros((), jnp.bfloat16)
+    blank = jnp.zeros((step, width // 2), jnp.bfloat16)
     shift = LANES.bit_length() - 1
     depth = block_count.bit_length() - 1
 
@@ -166,7 +167,15 @@
         for top in range(tops):
             here = top_code == jnp.bfloat16(top)
             for cut in range(0, rows, step):
-                row_hot.append(jnp.where(here, picked[cut : cut + step], zero))
+                halves = []
+                for side in range(2):
+                    lanes = slice(side * width // 2, (side + 1) * width // 2)
+                    if cut + step <= side * rows // 2 or cut >= (side + 1) * rows // 2:
+                        halves.append(blank)
+                    else:
+                        block = picked[cut : cut + step, lanes]
+                        halves.append(jnp.where(here[:, lanes], block, zero))
+                row_hot.append(jnp.concatenate(halves, axis=1))
         row_hot = jnp.concatenate(row_hot, axis=0).astype(HOT)
         low_hot = jnp.where(low_iota == low_code, one, zero).astype(HOT)
         tally = lax.dot_general(

time: 72.1 us -> 71.8 us (level)
  no operation moved by 1% of the time
where the time goes in v6:
time: 71.8 us; the launch traced here: 71.6 us
  Pallas kernels  31.5 us (44%)
  waiting for transfers between devices  20.1 us (28%)
  starting transfers between devices  18.3 us (25%)
  local copies, waits for them, and re-layouts  0.94 us (1%)
  between operations  0.76 us (1%)
    pallas_call x1, Pallas kernels, forward(): pl.pallas_call(functools.partial(forward_kernel, kinds, places), in_specs...  15.1 us
    pallas_call x2, Pallas kernels, backward(): pl.pallas_call(functools.partial(backward_kernel, *(combos or (0, 0)), le...  12 us
    ppermute x3, waiting for transfers between devices, scatter_slab(): lax.ppermute(block, 'slab', [(j, j ^ 2 * step) for j in range(slabs)])  8.69 us
    ppermute x6, starting transfers between devices, backward(): received.append(lax.ppermute(codes[step - 1], 'sens', pairs))  7.11 us
    ppermute x3, starting transfers between devices, scatter_slab(): lax.ppermute(block, 'slab', [(j, j ^ 2 * step) for j in range(slabs)])  5.69 us
    ppermute x6, waiting for transfers between devices, backward(): received.append(lax.ppermute(codes[step - 1], 'sens', pairs))  4.52 us
    ppermute x3, starting transfers between devices, gather_slab(): lax.ppermute(share, 'slab', [(j, j ^ 2 * step) for j in range(slabs)])  4.44 us
    ppermute x3, waiting for transfers between devices, gather_slab(): lax.ppermute(share, 'slab', [(j, j ^ 2 * step) for j in range(slabs)])  4.2 us
  transfers between devices with their start and end apart: 17, of which 10 were waited for; matrix products, arithmetic and copies ran while one was open for 1% of the time, Pallas kernels for 8%

profile of v6, /device:TPU:0, one launch (start us, length us, event | category | flops | bytes accessed | tf_op | source)
XLA Modules:
  0.0 71.6 jit_solution(2748154446124027131)
XLA Ops:
  0.6 0.0 copy-start
  0.7 15.1 %forward.1 = (bf16[3072,2048]{1,0:T(8,128)(2,1)}, bf16[3072,2048]{1,0:T(8,128)(2,1)}, f32[4,32,1024]{2,1,0:T(8,128)S(1)}, f32[4,32,1024]{2,1,0:T(8,128)S(1)}) custom-call(s32[1]{0:T(128)} %bitcast.core_ref, s32[64,256]{1,0:T(8,128)} %bitcast.44, s32[64,256]{1,0:T(8,128)} %bitcast.45, s32[64,256]{1,0:T(8,128)} %bitcast.46, s32[1,256]{1,0:T(1,128)} %bitcast.48, ...), custom_call_target="tpu_custom_call" | custom-call | tf_op jit(solution)/shard_map/forward/pallas_call | solution.py:266
  15.8 0.5 collective-permute-start
  16.3 1.5 %collective-permute-done = f32[4,32,1024]{2,1,0:T(8,128)S(1)} collective-permute-done((f32[4,32,1024]{2,1,0:T(8,128)S(1)}, f32[4,32,1024]{2,1,0:T(8,128)S(1)}, u32[]{:S(2)}, u32[]{:S(2)}) %collective-permute-start) | collective-permute-done | bytes 524320 | tf_op jit(solution)/shard_map/ppermute | solution.py:460
  17.9 0.1 add.25
  18.0 5.0 %collective-permute-start.3 = (f32[32,1024]{1,0:T(8,128)S(1)}, f32[32,1024]{1,0:T(8,128)S(1)}, u32[]{:S(2)}, u32[]{:S(2)}) collective-permute-start(f32[32,1024]{1,0:T(8,128)S(1)} %get-tuple-element.40), channel_id=1, source_target_pairs={{0,6},{1,7},{2,4},{3,5},{4,2},{5,3},{6,0},{7,1},{8,14},{9,15},{10,... | collective-permute-start | bytes 393224 | tf_op jit(solution)/shard_map/ppermute | solution.py:466
  23.0 0.0 collective-permute-start.2
  23.0 0.6 collective-permute-start.1
  23.7 0.0 copy-done
  23.7 2.0 %filter_matrix.1 = (f32[512,512]{1,0:T(8,128)S(1)}, bf16[256,256]{1,0:T(8,128)(2,1)S(1)}) custom-call(f32[1,512]{1,0:T(1,128)} %bitcast.47, f32[512,512]{1,0:T(8,128)} %constant.56.clone.cosine_hbm, bf16[256,256]{1,0:T(8,128)(2,1)} %bitcast.42), custom_call_target="tpu_custom_call" | custom-call | tf_op jit(solution)/shard_map/filter_matrix/pallas_call | solution.py:60
  25.7 1.6 %collective-permute-done.3.refs_3_ = f32[32,1024]{1,0:T(8,128)S(1)} collective-permute-done((f32[32,1024]{1,0:T(8,128)S(1)}, f32[32,1024]{1,0:T(8,128)S(1)}, u32[]{:S(2)}, u32[]{:S(2)}) %collective-permute-start.3) | collective-permute-done | bytes 131104 | tf_op jit(solution)/shard_map/ppermute | solution.py:466
  27.3 3.4 %collective-permute-done.2.refs_2_ = f32[32,1024]{1,0:T(8,128)S(1)} collective-permute-done((f32[32,1024]{1,0:T(8,128)S(1)}, f32[32,1024]{1,0:T(8,128)S(1)}, u32[]{:S(2)}, u32[]{:S(2)}) %collective-permute-start.2) | collective-permute-done | bytes 131104 | tf_op jit(solution)/shard_map/ppermute | solution.py:466
  30.7 3.7 %collective-permute-done.1.refs_1_ = f32[32,1024]{1,0:T(8,128)S(1)} collective-permute-done((f32[32,1024]{1,0:T(8,128)S(1)}, f32[32,1024]{1,0:T(8,128)S(1)}, u32[]{:S(2)}, u32[]{:S(2)}) %collective-permute-start.1) | collective-permute-done | bytes 131104 | tf_op jit(solution)/shard_map/ppermute | solution.py:466
  34.4 1.4 %refine.1 = (f32[64,512]{1,0:T(8,128)S(1)}, bf16[32,1024]{1,0:T(8,128)(2,1)S(1)}) custom-call(f32[32,1024]{1,0:T(8,128)S(1)} %get-tuple-element.43.refs_0_, f32[32,1024]{1,0:T(8,128)S(1)} %collective-permute-done.1.refs_1_, f32[32,1024]{1,0:T(8,128)S(1)} %collective-permute-done.2.refs_2_, f32[32,1024]{1,0:T(8,128)S(1)} %collective-permute-done.3.refs_3_, ...), custom_call_target="tpu_custom_call" | custom-call | tf_op jit(solution)/shard_map/refine/pallas_call | solution.py:491
  35.8 0.1 collective-permute-start.6
  35.9 3.0 %collective-permute-start.5 = (bf16[32,1024]{1,0:T(8,128)(2,1)S(1)}, bf16[32,1024]{1,0:T(8,128)(2,1)S(1)}, u32[]{:S(2)}, u32[]{:S(2)}) collective-permute-start(bf16[32,1024]{1,0:T(8,128)(2,1)S(1)} %get-tuple-element.28.refs_1_), channel_id=1, source_target_pairs={{0,4},{1,5},{2,6},{3,7},{4,0},{5,1},{6,2},{7,3},{8,12},{9,13},{10,... | collective-permute-start | bytes 196616 | tf_op jit(solution)/shard_map/ppermute | solution.py:507
  38.9 1.3 %collective-permute-start.4 = (bf16[32,1024]{1,0:T(8,128)(2,1)S(1)}, bf16[32,1024]{1,0:T(8,128)(2,1)S(1)}, u32[]{:S(2)}, u32[]{:S(2)}) collective-permute-start(bf16[32,1024]{1,0:T(8,128)(2,1)S(1)} %get-tuple-element.28.refs_1_), channel_id=1, source_target_pairs={{0,6},{1,7},{2,4},{3,5},{4,2},{5,3},{6,0},{7,1},{8,14},{9,15},{10,... | collective-permute-start | bytes 196616 | tf_op jit(solution)/shard_map/ppermute | solution.py:507
  40.2 0.0 collective-permute-start.7
  40.2 0.0 collective-permute-done.6.refs_4_
  40.2 0.5 collective-permute-start.10
  40.7 2.2 %collective-permute-done.5.refs_3_ = bf16[32,1024]{1,0:T(8,128)(2,1)S(1)} collective-permute-done((bf16[32,1024]{1,0:T(8,128)(2,1)S(1)}, bf16[32,1024]{1,0:T(8,128)(2,1)S(1)}, u32[]{:S(2)}, u32[]{:S(2)}) %collective-permute-start.5) | collective-permute-done | bytes 65568 | tf_op jit(solution)/shard_map/ppermute | solution.py:507
  42.9 0.0 collective-permute-start.9
  42.9 2.0 %collective-permute-done.4.refs_2_ = bf16[32,1024]{1,0:T(8,128)(2,1)S(1)} collective-permute-done((bf16[32,1024]{1,0:T(8,128)(2,1)S(1)}, bf16[32,1024]{1,0:T(8,128)(2,1)S(1)}, u32[]{:S(2)}, u32[]{:S(2)}) %collective-permute-start.4) | collective-permute-done | bytes 65568 | tf_op jit(solution)/shard_map/ppermute | solution.py:507
  44.9 0.0 collective-permute-start.8
  44.9 0.1 stack.35.refs_0_
  45.0 0.0 copy-start.1
  45.0 0.0 collective-permute-done.7.refs_5_
  45.0 0.0 collective-permute-done.10.refs_8_
  45.0 0.0 collective-permute-done.9.refs_7_
  45.1 1.1 %collective-permute-done.8.refs_6_ = bf16[32,1024]{1,0:T(8,128)(2,1)S(1)} collective-permute-done((bf16[32,1024]{1,0:T(8,128)(2,1)S(1)}, bf16[32,1024]{1,0:T(8,128)(2,1)S(1)}, u32[]{:S(2)}, u32[]{:S(2)}) %collective-permute-start.8) | collective-permute-done | bytes 65568 | tf_op jit(solution)/shard_map/ppermute | solution.py:510
  46.2 8.1 %backward.2 = (bf16[256,3072]{1,0:T(8,128)(2,1)S(1)}, f32[32,2048]{1,0:T(8,128)S(1)}, s16[32,2176]{1,0:T(8,128)(2,1)S(1)}, s16[32,2176]{1,0:T(8,128)(2,1)S(1)}, s16[32,2176]{1,0:T(8,128)(2,1)S(1)}) custom-call(s32[1]{0:T(128)} %bitcast.18.own_ref, bf16[3072,2048]{1,0:T(8,128)(2,1)} %get-tuple-element.27.tally_hbm, s32[8]{0:T(128)S(1)} %stack.35.refs_0_, ...), custom_call_target="tpu_custom_call" | custom-call | flops 3221225472 | bytes 12582912 | tf_op jit(solution)/shard_map/backward/pallas_call | solution.py:406
  54.3 2.5 %collective-permute-start.11 = (s16[32,2176]{1,0:T(8,128)(2,1)S(1)}, s16[32,2176]{1,0:T(8,128)(2,1)S(1)}, u32[]{:S(2)}, u32[]{:S(2)}) collective-permute-start(s16[32,2176]{1,0:T(8,128)(2,1)S(1)} %get-tuple-element.31), channel_id=1, source_target_pairs={{0,24},{8,16},{16,8},{24,0},{1,25},{9,17},{17,9},{25,1},{2,26},{10... | collective-permute-start | bytes 417800 | tf_op jit(solution)/shard_map/ppermute | solution.py:424
  56.8 0.5 collective-permute-start.12
  57.3 0.5 collective-permute-start.13
  57.9 0.0 copy-done.1
  57.9 3.8 %backward.3 = (f32[32,2048]{1,0:T(8,128)S(1)}, s16[32,2176]{1,0:T(8,128)(2,1)S(1)}, s16[32,2176]{1,0:T(8,128)(2,1)S(1)}, s16[32,2176]{1,0:T(8,128)(2,1)S(1)}) custom-call(s32[1]{0:T(128)} %bitcast.18.own_ref, bf16[3072,2048]{1,0:T(8,128)(2,1)S(1)} %copy-done.1, bf16[256,3072]{1,0:T(8,128)(2,1)S(1)} %get-tuple-element.35.refs_0_), custom_call_target="tpu_custom_call" | custom-call | flops 3221225472 | bytes 12582912 | tf_op jit(solution)/shard_map/backward/pallas_call | solution.py:406
  61.7 2.5 %collective-permute-start.14 = (s16[32,2176]{1,0:T(8,128)(2,1)S(1)}, s16[32,2176]{1,0:T(8,128)(2,1)S(1)}, u32[]{:S(2)}, u32[]{:S(2)}) collective-permute-start(s16[32,2176]{1,0:T(8,128)(2,1)S(1)} %get-tuple-element.37), channel_id=1, source_target_pairs={{0,24},{8,16},{16,8},{24,0},{1,25},{9,17},{17,9},{25,1},{2,26},{10... | collective-permute-start | bytes 417800 | tf_op jit(solution)/shard_map/ppermute | solution.py:424
  64.2 0.5 collective-permute-start.15
  64.7 0.0 collective-permute-done.11.refs_1_
  64.7 0.5 collective-permute-start.16
  65.3 0.8 %copy.14 = f32[2,32,512]{2,0,1:T(2,128)} copy(f32[2,32,512]{2,1,0:T(8,128)S(1)} %bitcast.39) | data formatting | bytes 262144 | tf_op jit(solution)/shard_map/reshape | solution.py:543
  66.0 0.0 collective-permute-done.12.refs_2_
  66.0 0.0 collective-permute-done.13.refs_3_
  66.1 2.5 %collective-permute-done.14.refs_5_ = s16[32,2176]{1,0:T(8,128)(2,1)S(1)} collective-permute-done((s16[32,2176]{1,0:T(8,128)(2,1)S(1)}, s16[32,2176]{1,0:T(8,128)(2,1)S(1)}, u32[]{:S(2)}, u32[]{:S(2)}) %collective-permute-start.14) | collective-permute-done | bytes 139296 | tf_op jit(solution)/shard_map/ppermute | solution.py:424
  68.6 2.0 %collective-permute-done.15.refs_6_ = s16[32,2176]{1,0:T(8,128)(2,1)S(1)} collective-permute-done((s16[32,2176]{1,0:T(8,128)(2,1)S(1)}, s16[32,2176]{1,0:T(8,128)(2,1)S(1)}, u32[]{:S(2)}, u32[]{:S(2)}) %collective-permute-start.15) | collective-permute-done | bytes 139296 | tf_op jit(solution)/shard_map/ppermute | solution.py:424
  70.5 0.1 collective-permute-done.16.refs_7_
  70.6 1.1 %finish.1 = f32[32,4096]{1,0:T(8,128)} custom-call(f32[32,2048]{1,0:T(8,128)S(1)} %get-tuple-element.30.refs_0_, s16[32,2176]{1,0:T(8,128)(2,1)S(1)} %collective-permute-done.11.refs_1_, s16[32,2176]{1,0:T(8,128)(2,1)S(1)} %collective-permute-done.12.refs_2_, s16[32,2176]{1,0:T(8,128)(2,1)S(1)} %collective-permute-done.13.refs_3_, ...), custom_call_target="tpu_custom_call" | custom-call | tf_op jit(solution)/shard_map/finish/pallas_call | solution.py:447
  (3 shorter events, 0.1 us)
Async XLA Ops:
  0.6 23.0 %copy-start = (f32[256,2,512]{2,1,0:T(2,128)S(1)}, f32[256,2,512]{2,1,0:T(2,128)}, u32[]{:S(2)}) copy-start(f32[256,2,512]{2,1,0:T(2,128)} %param.12) | copy-start | bytes 3145732
  15.8 2.1 %collective-permute-start = (f32[4,32,1024]{2,1,0:T(8,128)S(1)}, f32[4,32,1024]{2,1,0:T(8,128)S(1)}, u32[]{:S(2)}, u32[]{:S(2)}) collective-permute-start(f32[4,32,1024]{2,1,0:T(8,128)S(1)} %get-tuple-element.22), channel_id=1, source_target_pairs={{0,1},{1,0},{2,3},{3,2},{4,5},{5,4},{6,7},{7,6},{8,9},{9,8},{10,11... | collective-permute-start | bytes 1572872 | tf_op jit(solution)/shard_map/ppermute | solution.py:460
  18.0 9.4 %collective-permute-start.3 = (f32[32,1024]{1,0:T(8,128)S(1)}, f32[32,1024]{1,0:T(8,128)S(1)}, u32[]{:S(2)}, u32[]{:S(2)}) collective-permute-start(f32[32,1024]{1,0:T(8,128)S(1)} %get-tuple-element.40), channel_id=1, source_target_pairs={{0,6},{1,7},{2,4},{3,5},{4,2},{5,3},{6,0},{7,1},{8,14},{9,15},{10,... | collective-permute-start | bytes 393224 | tf_op jit(solution)/shard_map/ppermute | solution.py:466
  23.0 7.7 %collective-permute-start.2 = (f32[32,1024]{1,0:T(8,128)S(1)}, f32[32,1024]{1,0:T(8,128)S(1)}, u32[]{:S(2)}, u32[]{:S(2)}) collective-permute-start(f32[32,1024]{1,0:T(8,128)S(1)} %get-tuple-element.41), channel_id=1, source_target_pairs={{0,2},{1,3},{2,0},{3,1},{4,6},{5,7},{6,4},{7,5},{8,10},{9,11},{10,... | collective-permute-start | bytes 393224 | tf_op jit(solution)/shard_map/ppermute | solution.py:466
  23.0 11.4 %collective-permute-start.1 = (f32[32,1024]{1,0:T(8,128)S(1)}, f32[32,1024]{1,0:T(8,128)S(1)}, u32[]{:S(2)}, u32[]{:S(2)}) collective-permute-start(f32[32,1024]{1,0:T(8,128)S(1)} %get-tuple-element.42), channel_id=1, source_target_pairs={{0,4},{1,5},{2,6},{3,7},{4,0},{5,1},{6,2},{7,3},{8,12},{9,13},{10,... | collective-permute-start | bytes 393224 | tf_op jit(solution)/shard_map/ppermute | solution.py:466
  35.8 4.5 %collective-permute-start.6 = (bf16[32,1024]{1,0:T(8,128)(2,1)S(1)}, bf16[32,1024]{1,0:T(8,128)(2,1)S(1)}, u32[]{:S(2)}, u32[]{:S(2)}) collective-permute-start(bf16[32,1024]{1,0:T(8,128)(2,1)S(1)} %get-tuple-element.28.refs_1_), channel_id=1, source_target_pairs={{0,2},{1,3},{2,0},{3,1},{4,6},{5,7},{6,4},{7,5},{8,10},{9,11},{10,... | collective-permute-start | bytes 196616 | tf_op jit(solution)/shard_map/ppermute | solution.py:507
  35.9 7.1 %collective-permute-start.5 = (bf16[32,1024]{1,0:T(8,128)(2,1)S(1)}, bf16[32,1024]{1,0:T(8,128)(2,1)S(1)}, u32[]{:S(2)}, u32[]{:S(2)}) collective-permute-start(bf16[32,1024]{1,0:T(8,128)(2,1)S(1)} %get-tuple-element.28.refs_1_), channel_id=1, source_target_pairs={{0,4},{1,5},{2,6},{3,7},{4,0},{5,1},{6,2},{7,3},{8,12},{9,13},{10,... | collective-permute-start | bytes 196616 | tf_op jit(solution)/shard_map/ppermute | solution.py:507
  38.9 6.1 %collective-permute-start.4 = (bf16[32,1024]{1,0:T(8,128)(2,1)S(1)}, bf16[32,1024]{1,0:T(8,128)(2,1)S(1)}, u32[]{:S(2)}, u32[]{:S(2)}) collective-permute-start(bf16[32,1024]{1,0:T(8,128)(2,1)S(1)} %get-tuple-element.28.refs_1_), channel_id=1, source_target_pairs={{0,6},{1,7},{2,4},{3,5},{4,2},{5,3},{6,0},{7,1},{8,14},{9,15},{10,... | collective-permute-start | bytes 196616 | tf_op jit(solution)/shard_map/ppermute | solution.py:507
  40.2 4.8 %collective-permute-start.7 = (bf16[32,1024]{1,0:T(8,128)(2,1)S(1)}, bf16[32,1024]{1,0:T(8,128)(2,1)S(1)}, u32[]{:S(2)}, u32[]{:S(2)}) collective-permute-start(bf16[32,1024]{1,0:T(8,128)(2,1)S(1)} %get-tuple-element.28.refs_1_), channel_id=1, source_target_pairs={{0,1},{1,0},{2,3},{3,2},{4,5},{5,4},{6,7},{7,6},{8,9},{9,8},{10,11... | collective-permute-start | bytes 196616 | tf_op jit(solution)/shard_map/ppermute | solution.py:510
  40.2 4.8 %collective-permute-start.10 = (bf16[32,1024]{1,0:T(8,128)(2,1)S(1)}, bf16[32,1024]{1,0:T(8,128)(2,1)S(1)}, u32[]{:S(2)}, u32[]{:S(2)}) collective-permute-start(bf16[32,1024]{1,0:T(8,128)(2,1)S(1)} %collective-permute-done.6.refs_4_), channel_id=1, source_target_pairs={{0,1},{1,0},{2,3},{3,2},{4,5},{5,4},{6,7},{7,6},{8,9},{9,8},{10,11... | collective-permute-start | bytes 196616 | tf_op jit(solution)/shard_map/ppermute | solution.py:510
  42.9 2.1 %collective-permute-start.9 = (bf16[32,1024]{1,0:T(8,128)(2,1)S(1)}, bf16[32,1024]{1,0:T(8,128)(2,1)S(1)}, u32[]{:S(2)}, u32[]{:S(2)}) collective-permute-start(bf16[32,1024]{1,0:T(8,128)(2,1)S(1)} %collective-permute-done.5.refs_3_), channel_id=1, source_target_pairs={{0,1},{1,0},{2,3},{3,2},{4,5},{5,4},{6,7},{7,6},{8,9},{9,8},{10,11... | collective-permute-start | bytes 196616 | tf_op jit(solution)/shard_map/ppermute | solution.py:510
  44.9 1.3 %collective-permute-start.8 = (bf16[32,1024]{1,0:T(8,128)(2,1)S(1)}, bf16[32,1024]{1,0:T(8,128)(2,1)S(1)}, u32[]{:S(2)}, u32[]{:S(2)}) collective-permute-start(bf16[32,1024]{1,0:T(8,128)(2,1)S(1)} %collective-permute-done.4.refs_2_), channel_id=1, source_target_pairs={{0,1},{1,0},{2,3},{3,2},{4,5},{5,4},{6,7},{7,6},{8,9},{9,8},{10,11... | collective-permute-start | bytes 196616 | tf_op jit(solution)/shard_map/ppermute | solution.py:510
  45.0 12.9 %copy-start.1 = (bf16[3072,2048]{1,0:T(8,128)(2,1)S(1)}, bf16[3072,2048]{1,0:T(8,128)(2,1)}, u32[]{:S(2)}) copy-start(bf16[3072,2048]{1,0:T(8,128)(2,1)} %get-tuple-element.34.tally_hbm) | copy-start | bytes 37748740
  54.3 10.4 %collective-permute-start.11 = (s16[32,2176]{1,0:T(8,128)(2,1)S(1)}, s16[32,2176]{1,0:T(8,128)(2,1)S(1)}, u32[]{:S(2)}, u32[]{:S(2)}) collective-permute-start(s16[32,2176]{1,0:T(8,128)(2,1)S(1)} %get-tuple-element.31), channel_id=1, source_target_pairs={{0,24},{8,16},{16,8},{24,0},{1,25},{9,17},{17,9},{25,1},{2,26},{10... | collective-permute-start | bytes 417800 | tf_op jit(solution)/shard_map/ppermute | solution.py:424
  56.8 9.2 %collective-permute-start.12 = (s16[32,2176]{1,0:T(8,128)(2,1)S(1)}, s16[32,2176]{1,0:T(8,128)(2,1)S(1)}, u32[]{:S(2)}, u32[]{:S(2)}) collective-permute-start(s16[32,2176]{1,0:T(8,128)(2,1)S(1)} %get-tuple-element.32), channel_id=1, source_target_pairs={{0,16},{8,24},{16,0},{24,8},{1,17},{9,25},{17,1},{25,9},{2,18},{10... | collective-permute-start | bytes 417800 | tf_op jit(solution)/shard_map/ppermute | solution.py:424
  57.3 8.7 %collective-permute-start.13 = (s16[32,2176]{1,0:T(8,128)(2,1)S(1)}, s16[32,2176]{1,0:T(8,128)(2,1)S(1)}, u32[]{:S(2)}, u32[]{:S(2)}) collective-permute-start(s16[32,2176]{1,0:T(8,128)(2,1)S(1)} %get-tuple-element.33), channel_id=1, source_target_pairs={{0,8},{8,0},{16,24},{24,16},{1,9},{9,1},{17,25},{25,17},{2,10},{10... | collective-permute-start | bytes 417800 | tf_op jit(solution)/shard_map/ppermute | solution.py:424
  61.7 6.8 %collective-permute-start.14 = (s16[32,2176]{1,0:T(8,128)(2,1)S(1)}, s16[32,2176]{1,0:T(8,128)(2,1)S(1)}, u32[]{:S(2)}, u32[]{:S(2)}) collective-permute-start(s16[32,2176]{1,0:T(8,128)(2,1)S(1)} %get-tuple-element.37), channel_id=1, source_target_pairs={{0,24},{8,16},{16,8},{24,0},{1,25},{9,17},{17,9},{25,1},{2,26},{10... | collective-permute-start | bytes 417800 | tf_op jit(solution)/shard_map/ppermute | solution.py:424
  64.2 6.3 %collective-permute-start.15 = (s16[32,2176]{1,0:T(8,128)(2,1)S(1)}, s16[32,2176]{1,0:T(8,128)(2,1)S(1)}, u32[]{:S(2)}, u32[]{:S(2)}) collective-permute-start(s16[32,2176]{1,0:T(8,128)(2,1)S(1)} %get-tuple-element.38), channel_id=1, source_target_pairs={{0,16},{8,24},{16,0},{24,8},{1,17},{9,25},{17,1},{25,9},{2,18},{10... | collective-permute-start | bytes 417800 | tf_op jit(solution)/shard_map/ppermute | solution.py:424
  64.7 5.8 %collective-permute-start.16 = (s16[32,2176]{1,0:T(8,128)(2,1)S(1)}, s16[32,2176]{1,0:T(8,128)(2,1)S(1)}, u32[]{:S(2)}, u32[]{:S(2)}) collective-permute-start(s16[32,2176]{1,0:T(8,128)(2,1)S(1)} %get-tuple-element.39), channel_id=1, source_target_pairs={{0,8},{8,0},{16,24},{24,16},{1,9},{9,1},{17,25},{25,17},{2,10},{10... | collective-permute-start | bytes 417800 | tf_op jit(solution)/shard_map/ppermute | solution.py:424
